TPU v7x, 32 devices: a whole 2x2x4 slice. The times are simulated.
32 devices in a mesh: dp: 8 (over z, x), tensor: 4 (over y, core).
Axes of the slice: x: 2, y: 2, z: 4, core: 2. Of those that a mesh axis runs over, the one named last changes fastest.
Arguments:
- tokens: bfloat16 [16384, 1024], P(('dp', 'tensor')), may hold values from -6 to 6
- first_gain: float32 [1024], replicated, may hold values from 0.5 to 1.5
- first_shift: float32 [1024], replicated, may hold values from -2 to 2
- triple_weight: bfloat16 [1024, 3, 1024], P(None, None, 'tensor'), may hold values from -0.1875 to 0.1875
- triple_bias: float32 [3, 1024], P(None, 'tensor'), may hold values from -2 to 2
- merge_weight: bfloat16 [1024, 1024], P('tensor'), may hold values from -6 to 6
- merge_bias: float32 [1024], replicated, may hold values from -2 to 2
- second_gain: float32 [1024], replicated, may hold values from 0.5 to 1.5
- second_shift: float32 [1024], replicated, may hold values from -2 to 2
- up_weight: bfloat16 [1024, 4096], P(None, 'tensor'), may hold values from -0.1875 to 0.1875
- up_bias: float32 [4096], P('tensor'), may hold values from -2 to 2
- down_weight: bfloat16 [4096, 1024], P('tensor'), may hold values from -0.1875 to 0.1875
- down_bias: float32 [1024], replicated, may hold values from -2 to 2
- lengths: int32 [8], P('dp'), may hold values from 1024 to 2048, as said below
- cotangent: bfloat16 [16384, 1024], P(('dp', 'tensor')), may hold values from -8 to 8
Outputs:
- output: bfloat16 [16384, 1024], P(('dp', 'tensor'))
- grad_tokens: float32 [16384, 1024], P(('dp', 'tensor'))
- grad_first_gain: float32 [1024], replicated
- grad_first_shift: float32 [1024], replicated
- grad_triple_weight: float32 [1024, 3, 1024], P(None, None, 'tensor')
- grad_triple_bias: float32 [3, 1024], P(None, 'tensor')
- grad_merge_weight: float32 [1024, 1024], P('tensor')
- grad_merge_bias: float32 [1024], replicated
- grad_second_gain: float32 [1024], replicated
- grad_second_shift: float32 [1024], replicated
- grad_up_weight: float32 [1024, 4096], P(None, 'tensor')
- grad_up_bias: float32 [4096], P('tensor')
- grad_down_weight: float32 [4096, 1024], P('tensor')
- grad_down_bias: float32 [1024], replicated
Inputs may be any that keep to these rules, and one draw needn't show every extreme that they name: lengths[s] is the number of real tokens of sequence slot s; the largest entry equals 2048 in every draw.
All inputs are finite; a program needn't handle non-finite values.
Results may differ from a plain program's by a relative error of at most 0.0095.
The roundings to bfloat16 on the way count: a program that leaves them out, or rounds other values in their place, can miss the bound.
Values may be sent and summed in bfloat16 or wider, within the bound.
A program may use at most 192 MiB of HBM per device.

v0:
```python
from functools import partial

import jax
import jax.numpy as jnp
from jax import lax
from jax.sharding import PartitionSpec as P

HD = 64
LEN = 2048


EPS = 1e-05
MASKED = -1e30


def norm_parts(values, scale_vec, shift_vec):
    centred = values - jnp.mean(values, axis=-1, keepdims=True)
    inverse = lax.rsqrt(jnp.mean(centred * centred, axis=-1, keepdims=True) + EPS)
    unit_part = centred * inverse
    return (unit_part * scale_vec + shift_vec, unit_part, inverse)


def norm_back(grad_out, unit_part, inverse, scale_vec):
    grad_unit = grad_out * scale_vec
    centred_grad = grad_unit - jnp.mean(grad_unit, axis=-1, keepdims=True)
    centred_grad = centred_grad - unit_part * jnp.mean(
        grad_unit * unit_part, axis=-1, keepdims=True
    )
    return (
        centred_grad * inverse,
        jnp.sum(grad_out * unit_part, axis=0),
        jnp.sum(grad_out, axis=0),
    )


def live_rows(lengths, first_row, row_count):
    row_index = first_row + jnp.arange(row_count)
    position = row_index % LEN
    owner_slot = row_index // LEN
    slot_ids = jnp.arange(lengths.shape[0])
    limit_len = jnp.sum(
        jnp.where(owner_slot[:, None] == slot_ids[None, :], lengths[None, :], 0), axis=1
    )
    return position < limit_len


def block_scores(query_block, key_block, start_row, length):
    scores = jnp.einsum(
        "qhd,khd->hqk", query_block, key_block, preferred_element_type=jnp.float32
    ) * HD ** (-0.5)
    query_index = start_row + jnp.arange(query_block.shape[0])
    key_index = jnp.arange(LEN)
    key_mask = (key_index[None, :] <= query_index[:, None]) & (key_index[None, :] < length)
    query_live = jnp.where(query_index < length, 1.0, 0.0).astype(jnp.float32)
    magnitude = jnp.where(key_mask[None], jnp.abs(scores), MASKED)
    return (scores, magnitude, key_mask, query_live)


def attend_forward(queries, key_heads, value_heads, lengths):

    def one_slot(slot_pack):
        query_slot, key_slot, value_slot, length = slot_pack
        start_rows = jnp.arange(query_slot.shape[0]) * query_slot.shape[1]

        def one_block(block_item):
            query_block, start_row = block_item
            scores, magnitude, key_mask, query_live = block_scores(
                query_block, key_slot, start_row, length
            )
            row_max = jnp.max(magnitude, axis=-1, keepdims=True)
            exponent = jnp.exp(magnitude - row_max)
            row_total = jnp.sum(exponent, axis=-1, keepdims=True)
            weights = (
                jnp.sign(scores) * (exponent / row_total) * query_live[None, :, None]
            ).astype(jnp.bfloat16)
            result = jnp.einsum(
                "hqk,khd->qhd", weights, value_slot, preferred_element_type=jnp.float32
            )
            return (result.astype(jnp.bfloat16), (row_max + jnp.log(row_total))[..., 0])

        return lax.map(one_block, (query_slot, start_rows))

    return lax.map(one_slot, (queries, key_heads, value_heads, lengths))


def attend_backward(queries, key_heads, value_heads, grad_heads, log_total, lengths):
    scale_factor = HD ** (-0.5)

    def one_slot(slot_pack):
        query_slot, key_slot, value_slot, grad_slot, total_slot, length = slot_pack
        start_rows = jnp.arange(query_slot.shape[0]) * query_slot.shape[1]

        def one_block(running, block_item):
            grad_keys, grad_values = running
            query_block, grad_block, block_total, start_row = block_item
            scores, magnitude, key_mask, query_live = block_scores(
                query_block, key_slot, start_row, length
            )
            probability = jnp.where(
                key_mask[None], jnp.exp(magnitude - block_total[..., None]), 0.0
            )
            score_sign = jnp.sign(scores)
            signed = score_sign * probability
            weights = (signed * query_live[None, :, None]).astype(jnp.bfloat16)
            grad_weights = (
                jnp.einsum(
                    "qhd,khd->hqk", grad_block, value_slot, preferred_element_type=jnp.float32
                )
                * query_live[None, :, None]
            )
            row_term = jnp.sum(signed * grad_weights, axis=-1, keepdims=True)
            grad_scores = (signed * (score_sign * grad_weights - row_term)).astype(jnp.bfloat16)
            grad_queries = (
                jnp.einsum(
                    "hqk,khd->qhd", grad_scores, key_slot, preferred_element_type=jnp.float32
                )
                * scale_factor
            )
            grad_keys = (
                grad_keys
                + jnp.einsum(
                    "hqk,qhd->khd", grad_scores, query_block, preferred_element_type=jnp.float32
                )
                * scale_factor
            )
            grad_values = grad_values + jnp.einsum(
                "hqk,qhd->khd", weights, grad_block, preferred_element_type=jnp.float32
            )
            return ((grad_keys, grad_values), grad_queries)

        zero_init = jnp.zeros(key_slot.shape, jnp.float32)
        (grad_keys, grad_values), grad_queries = lax.scan(
            one_block, (zero_init, zero_init), (query_slot, grad_slot, total_slot, start_rows)
        )
        return (grad_queries, grad_keys, grad_values)

    return lax.map(one_slot, (queries, key_heads, value_heads, grad_heads, log_total, lengths))


def contract_rows(left, right):
    return lax.dot_general(
        left, right, (((0,), (0,)), ((), ())), preferred_element_type=jnp.float32
    )


def contract_cols(left, right):
    return lax.dot_general(
        left, right, (((1,), (1,)), ((), ())), preferred_element_type=jnp.float32
    )


def on_device(
    tokens,
    first_gain,
    first_shift,
    triple_weight,
    triple_bias,
    merge_weight,
    merge_bias,
    second_gain,
    second_shift,
    up_weight,
    up_bias,
    down_weight,
    down_bias,
    lengths,
    cotangent,
):
    row_count = tokens.shape[0]
    local_width = triple_weight.shape[2]
    head_count = local_width // HD
    group_rows = row_count * lax.axis_size("tensor")
    first_row = lax.axis_index("tensor") * row_count
    slot_count = lengths.shape[0]
    block_rows = min(512, LEN)
    block_count = LEN // block_rows
    gelu_tanh = partial(jax.nn.gelu, approximate=True)
    live_mask = live_rows(lengths, first_row, row_count)
    residual = tokens.astype(jnp.float32)
    first_norm, first_unit, first_inverse = norm_parts(residual, first_gain, first_shift)
    every_first = lax.all_gather(first_norm.astype(jnp.bfloat16), "tensor", axis=0, tiled=True)
    mixed = (
        jnp.einsum("td,dce->tce", every_first, triple_weight, preferred_element_type=jnp.float32)
        + triple_bias
    )
    mixed = mixed.astype(jnp.bfloat16)
    queries = mixed[:, 0].reshape(slot_count, block_count, block_rows, head_count, HD)
    key_heads = mixed[:, 1].reshape(slot_count, LEN, head_count, HD)
    value_heads = mixed[:, 2].reshape(slot_count, LEN, head_count, HD)
    attended, log_total = attend_forward(queries, key_heads, value_heads, lengths)
    attended = attended.reshape(group_rows, local_width)
    block_part = attended
    residual_two = (
        residual
        + lax.psum_scatter(
            jnp.dot(block_part, merge_weight, preferred_element_type=jnp.float32),
            "tensor",
            scatter_dimension=0,
            tiled=True,
        )
        + merge_bias
    )
    second_norm, second_unit, second_inverse = norm_parts(residual_two, second_gain, second_shift)
    second_input = second_norm.astype(jnp.bfloat16)
    grad_top = cotangent.astype(jnp.float32) * live_mask[:, None]
    grad_low = grad_top.astype(jnp.bfloat16)
    every_second = lax.all_gather(second_input, "tensor", axis=0, tiled=True)
    before = jnp.dot(every_second, up_weight, preferred_element_type=jnp.float32) + up_bias
    hidden = gelu_tanh(before).astype(jnp.bfloat16)
    block_part = lax.slice_in_dim(hidden, 0, lax.axis_size("tensor") * row_count, axis=0)
    branch = lax.psum_scatter(
        jnp.dot(block_part, down_weight, preferred_element_type=jnp.float32),
        "tensor",
        scatter_dimension=0,
        tiled=True,
    )
    every_grad = lax.all_gather(grad_low, "tensor", axis=0, tiled=True)
    grad_down_weight = contract_rows(hidden, every_grad)
    grad_hidden = contract_cols(every_grad, down_weight)
    grad_before = jax.vjp(gelu_tanh, before)[1](grad_hidden)[0].astype(jnp.bfloat16)
    grad_up_weight = contract_rows(every_second, grad_before)
    grad_up_bias = jnp.sum(grad_before.astype(jnp.float32), axis=0)
    block_part = grad_before
    grad_second = lax.psum_scatter(
        contract_cols(block_part, up_weight), "tensor", scatter_dimension=0, tiled=True
    )
    output = (residual_two + branch + down_bias).astype(jnp.bfloat16)
    grad_norm_two, grad_second_gain, grad_second_shift = norm_back(
        grad_second, second_unit, second_inverse, second_gain
    )
    grad_residual = grad_top + grad_norm_two
    every_residual = lax.all_gather(
        grad_residual.astype(jnp.bfloat16), "tensor", axis=0, tiled=True
    )
    grad_merge_weight = contract_rows(attended, every_residual)
    grad_attended = contract_cols(every_residual, merge_weight).astype(jnp.bfloat16)
    grad_attended = grad_attended.reshape(slot_count, block_count, block_rows, head_count, HD)
    grad_queries, grad_keys, grad_values = attend_backward(
        queries, key_heads, value_heads, grad_attended, log_total, lengths
    )
    grad_mixed = jnp.stack(
        [
            grad_queries.reshape(group_rows, local_width),
            grad_keys.reshape(group_rows, local_width),
            grad_values.reshape(group_rows, local_width),
        ],
        axis=1,
    ).astype(jnp.bfloat16)
    grad_triple_weight = jnp.einsum(
        "td,tce->dce", every_first, grad_mixed, preferred_element_type=jnp.float32
    )
    grad_triple_bias = jnp.sum(grad_mixed.astype(jnp.float32), axis=0)
    block_part = grad_mixed
    grad_first = lax.psum_scatter(
        jnp.einsum("tce,dce->td", block_part, triple_weight, preferred_element_type=jnp.float32),
        "tensor",
        scatter_dimension=0,
        tiled=True,
    )
    grad_norm_one, grad_first_gain, grad_first_shift = norm_back(
        grad_first, first_unit, first_inverse, first_gain
    )
    grad_tokens = grad_residual + grad_norm_one
    matrix_sums = lax.psum(
        (
            grad_triple_weight,
            grad_triple_bias,
            grad_merge_weight,
            grad_up_weight,
            grad_up_bias,
            grad_down_weight,
        ),
        "dp",
    )
    small_sums = lax.psum(
        (
            grad_first_gain,
            grad_first_shift,
            jnp.sum(grad_residual, axis=0),
            grad_second_gain,
            grad_second_shift,
            jnp.sum(grad_top, axis=0),
        ),
        ("dp", "tensor"),
    )
    return (
        output,
        grad_tokens,
        small_sums[0],
        small_sums[1],
        matrix_sums[0],
        matrix_sums[1],
        matrix_sums[2],
        small_sums[2],
        small_sums[3],
        small_sums[4],
        matrix_sums[3],
        matrix_sums[4],
        matrix_sums[5],
        small_sums[5],
    )


def solution(mesh):
    in_specs = (
        P(("dp", "tensor"), None),
        P(),
        P(),
        P(None, None, "tensor"),
        P(None, "tensor"),
        P("tensor", None),
        P(),
        P(),
        P(),
        P(None, "tensor"),
        P("tensor"),
        P("tensor", None),
        P(),
        P("dp"),
        P(("dp", "tensor"), None),
    )
    out_specs = (
        P(("dp", "tensor"), None),
        P(("dp", "tensor"), None),
        P(),
        P(),
        P(None, None, "tensor"),
        P(None, "tensor"),
        P("tensor", None),
        P(),
        P(),
        P(),
        P(None, "tensor"),
        P("tensor"),
        P("tensor", None),
        P(),
    )
    return jax.shard_map(
        on_device, mesh=mesh, in_specs=in_specs, out_specs=out_specs, check_vma=False
    )
```

profile of v0, /device:TPU:24, one launch (start us, length us, event | category | flops | bytes accessed | tf_op | source)
XLA Modules:
  0.0 1335.8 jit_solution(11701981832680439994)
XLA Ops:
  13.3 35.5 %all-gather.5.cloned.1.call-done = bf16[2048,1024]{1,0:T(8,128)(2,1)} async-done(((bf16[512,1024]{1,0:T(8,128)(2,1)}), bf16[2048,1024]{1,0:T(8,128)(2,1)}) %all-gather.5.cloned.1.call-update) | async-done | bytes 4194320 | tf_op jit(solution)/shard_map/all_gather | solution.py:181
  48.8 6.1 add_convert_fusion
  61.7 104.2 %while.47 = (s32[]{:T(128)}, bf16[4,512,4,64]{1,3,2,0:T(8,128)(2,1)}, f32[4,4,512]{2,1,0:T(4,128)S(1)}, bf16[4,512,4,64]{1,3,2,0:T(8,128)(2,1)}, bf16[2048,4,64]...) while((s32[]{:T(128)}, ...), condition=%wide.region_5.6_spmd, body=%wide.region_2.5_spmd.sunk | while | flops 1151469568 | bytes 61419688 | solution.py:81
  65.7 5.2 fusion.134
  70.8 4.9 fusion.135
  75.8 12.0 fusion.136
  91.7 5.2 fusion.134
  101.8 12.0 fusion.136
  117.8 5.2 fusion.134
  127.9 12.0 fusion.136
  143.8 5.2 fusion.134
  149.0 4.9 fusion.135
  153.9 12.0 fusion.136
  173.9 71.8 %reduce-scatter.5.cloned.1.call-done = f32[512,1024]{1,0:T(8,128)} async-done(((f32[2048,1024]{1,0:T(8,128)}), f32[512,1024]{1,0:T(8,128)}) %reduce-scatter.5.cloned.1.call-update) | async-done | bytes 2097168 | tf_op jit(solution)/shard_map/reduce_scatter | solution.py:195
  254.1 31.2 %all-gather.7.cloned.1.call-done = bf16[2048,1024]{1,0:T(8,128)(2,1)} async-done(((bf16[512,1024]{1,0:T(8,128)(2,1)}), bf16[2048,1024]{1,0:T(8,128)(2,1)}) %all-gather.7.cloned.1.call-update) | async-done | bytes 4194320 | tf_op jit(solution)/shard_map/all_gather | solution.py:207
  285.3 11.2 fusion.79
  296.5 25.4 %all-gather.9.cloned.1.call-done = bf16[2048,1024]{1,0:T(8,128)(2,1)} async-done(((bf16[512,1024]{1,0:T(8,128)(2,1)}), bf16[2048,1024]{1,0:T(8,128)(2,1)}) %all-gather.9.cloned.1.call-update) | async-done | bytes 4194320 | tf_op jit(solution)/shard_map/all_gather | solution.py:217
  321.9 14.8 %convert_reduce_fusion = (f32[1024]{0:T(1024)}, bf16[2048,1024]{1,0:T(8,128)(2,1)S(1)}, bf16[2048,1024]{1,0:T(8,128)(2,1)}) fusion(f32[2048,1024]{1,0:T(8,128)} %fusion.79, f32[1024]{0:T(1024)S(1)} %copy-done.47, bf16[2048,1024]{1,0:T(8,128)(2,1)} %all-gather.9.cloned.1.call-done, bf16[1024,1024]{1,0:T(8,128)(2,1)S(1)} %copy-done), kind=kOutput, calls=%fused_computation.66 | convolution fusion | flops 4347395072 | bytes 23076864 | tf_op jit(solution)/shard_map/dot_general | solution.py:147
  338.7 7.1 fusion.81
  345.9 9.4 fusion.80
  355.8 61.9 %reduce-scatter.9.cloned.1.call-done = f32[512,1024]{1,0:T(8,128)} async-done(((f32[2048,1024]{1,0:T(8,128)}), f32[512,1024]{1,0:T(8,128)}) %reduce-scatter.9.cloned.1.call-update) | async-done | bytes 2097168 | tf_op jit(solution)/shard_map/reduce_scatter | solution.py:224
  420.7 71.1 %reduce-scatter.7.cloned.1.call-done = f32[512,1024]{1,0:T(8,128)} async-done(((f32[2048,1024]{1,0:T(8,128)}), f32[512,1024]{1,0:T(8,128)}) %reduce-scatter.7.cloned.1.call-update) | async-done | bytes 2097168 | tf_op jit(solution)/shard_map/reduce_scatter | solution.py:211
  498.9 34.6 %all-gather.11.cloned.1.call-done = bf16[2048,1024]{1,0:T(8,128)(2,1)} async-done(((bf16[512,1024]{1,0:T(8,128)(2,1)}), bf16[2048,1024]{1,0:T(8,128)(2,1)}) %all-gather.11.cloned.1.call-update) | async-done | bytes 4194320 | tf_op jit(solution)/shard_map/all_gather | solution.py:232
  543.6 276.1 %while.48 = (s32[]{:T(128)}, f32[2048,4,64]{0,2,1:T(8,128)}, f32[2048,4,64]{0,2,1:T(8,128)}, bf16[4,512,4,64]{1,3,2,0:T(8,128)(2,1)}, bf16[4,512,4,64]{1,3,2,0:T...) while((s32[]{:T(128)}, f32[2048,4,64]{0,2,1:T(8,128)}, ...), condition=%wide.region_15.16_spmd.clone, body=%wide.region_13.15_spmd.clone.sunk | while | flops 2819229696 | bytes 260645296 | solution.py:132
  551.2 5.7 copy-done.2
  557.0 10.8 fusion.148
  567.8 20.4 %multiply_reduce_fusion.7 = (f32[4,512]{1,0:T(4,128)S(1)}, f32[4,512,2048]{2,1,0:T(8,128)}) fusion(f32[4,512,2048]{2,1,0:T(8,128)} %copy-done.2, f32[512]{0:T(512)S(1)} %compare_select_fusion.5, f32[4,512]{1,0:T(4,128)S(1)} %dynamic-slice_bitcast_fusion.2, pred[512,2048]{1,0:T(8,128)(4,1)S(1)} %fusion.146, bf16[2048,4,64]{0,2,1:T(8,128)(2,1)S(1)} %copy-done.25, ...), kind=kOutput, calls=%fused_computation.23.clone.1 | convolution fusion | flops 578811904 | bytes 35932164 | tf_op jit(solution)/shard_map/while/body/eval_jaxpr/while/body/eval_jaxpr/qhd,khd->hqk/dot_general | solution.py:106
  588.2 15.8 %multiply_convert_fusion.21 = bf16[4,512,2048]{2,1,0:T(8,128)(2,1)S(1)} fusion(f32[4,512,2048]{2,1,0:T(8,128)} %get-tuple-element.444, f32[4,512,2048]{2,1,0:T(8,128)} %copy-done.2, f32[4,512]{1,0:T(4,128)S(1)} %get-tuple-element.445, f32[512]{0:T(512)S(1)} %compare_select_fusion.5, f32[4,512]{1,0:T(4,128)S(1)} %dynamic-slice_bitcast_fusion.2, ...), kind=kLoop, calls=%fused_computation.22.clone.1 | loop fusion | flops 50331648 | bytes 43010048 | tf_op jit(solution)/shard_map/while/body/eval_jaxpr/while/body/eval_jaxpr/convert_element_type | solution.py:112
  618.5 5.7 copy-done.2
  624.2 10.8 fusion.148
  635.0 20.4 %multiply_reduce_fusion.7 = (f32[4,512]{1,0:T(4,128)S(1)}, f32[4,512,2048]{2,1,0:T(8,128)}) fusion(f32[4,512,2048]{2,1,0:T(8,128)} %copy-done.2, f32[512]{0:T(512)S(1)} %compare_select_fusion.5, f32[4,512]{1,0:T(4,128)S(1)} %dynamic-slice_bitcast_fusion.2, pred[512,2048]{1,0:T(8,128)(4,1)S(1)} %fusion.146, bf16[2048,4,64]{0,2,1:T(8,128)(2,1)S(1)} %copy-done.25, ...), kind=kOutput, calls=%fused_computation.23.clone.1 | convolution fusion | flops 578811904 | bytes 35932164 | tf_op jit(solution)/shard_map/while/body/eval_jaxpr/while/body/eval_jaxpr/qhd,khd->hqk/dot_general | solution.py:106
  655.5 15.8 %multiply_convert_fusion.21 = bf16[4,512,2048]{2,1,0:T(8,128)(2,1)S(1)} fusion(f32[4,512,2048]{2,1,0:T(8,128)} %get-tuple-element.444, f32[4,512,2048]{2,1,0:T(8,128)} %copy-done.2, f32[4,512]{1,0:T(4,128)S(1)} %get-tuple-element.445, f32[512]{0:T(512)S(1)} %compare_select_fusion.5, f32[4,512]{1,0:T(4,128)S(1)} %dynamic-slice_bitcast_fusion.2, ...), kind=kLoop, calls=%fused_computation.22.clone.1 | loop fusion | flops 50331648 | bytes 43010048 | tf_op jit(solution)/shard_map/while/body/eval_jaxpr/while/body/eval_jaxpr/convert_element_type | solution.py:112
  685.7 5.7 copy-done.2
  691.5 10.8 fusion.148
  702.3 20.4 %multiply_reduce_fusion.7 = (f32[4,512]{1,0:T(4,128)S(1)}, f32[4,512,2048]{2,1,0:T(8,128)}) fusion(f32[4,512,2048]{2,1,0:T(8,128)} %copy-done.2, f32[512]{0:T(512)S(1)} %compare_select_fusion.5, f32[4,512]{1,0:T(4,128)S(1)} %dynamic-slice_bitcast_fusion.2, pred[512,2048]{1,0:T(8,128)(4,1)S(1)} %fusion.146, bf16[2048,4,64]{0,2,1:T(8,128)(2,1)S(1)} %copy-done.25, ...), kind=kOutput, calls=%fused_computation.23.clone.1 | convolution fusion | flops 578811904 | bytes 35932164 | tf_op jit(solution)/shard_map/while/body/eval_jaxpr/while/body/eval_jaxpr/qhd,khd->hqk/dot_general | solution.py:106
  722.7 15.8 %multiply_convert_fusion.21 = bf16[4,512,2048]{2,1,0:T(8,128)(2,1)S(1)} fusion(f32[4,512,2048]{2,1,0:T(8,128)} %get-tuple-element.444, f32[4,512,2048]{2,1,0:T(8,128)} %copy-done.2, f32[4,512]{1,0:T(4,128)S(1)} %get-tuple-element.445, f32[512]{0:T(512)S(1)} %compare_select_fusion.5, f32[4,512]{1,0:T(4,128)S(1)} %dynamic-slice_bitcast_fusion.2, ...), kind=kLoop, calls=%fused_computation.22.clone.1 | loop fusion | flops 50331648 | bytes 43010048 | tf_op jit(solution)/shard_map/while/body/eval_jaxpr/while/body/eval_jaxpr/convert_element_type | solution.py:112
  753.0 5.7 copy-done.2
  758.7 10.8 fusion.148
  769.5 20.4 %multiply_reduce_fusion.7 = (f32[4,512]{1,0:T(4,128)S(1)}, f32[4,512,2048]{2,1,0:T(8,128)}) fusion(f32[4,512,2048]{2,1,0:T(8,128)} %copy-done.2, f32[512]{0:T(512)S(1)} %compare_select_fusion.5, f32[4,512]{1,0:T(4,128)S(1)} %dynamic-slice_bitcast_fusion.2, pred[512,2048]{1,0:T(8,128)(4,1)S(1)} %fusion.146, bf16[2048,4,64]{0,2,1:T(8,128)(2,1)S(1)} %copy-done.25, ...), kind=kOutput, calls=%fused_computation.23.clone.1 | convolution fusion | flops 578811904 | bytes 35932164 | tf_op jit(solution)/shard_map/while/body/eval_jaxpr/while/body/eval_jaxpr/qhd,khd->hqk/dot_general | solution.py:106
  790.0 15.8 %multiply_convert_fusion.21 = bf16[4,512,2048]{2,1,0:T(8,128)(2,1)S(1)} fusion(f32[4,512,2048]{2,1,0:T(8,128)} %get-tuple-element.444, f32[4,512,2048]{2,1,0:T(8,128)} %copy-done.2, f32[4,512]{1,0:T(4,128)S(1)} %get-tuple-element.445, f32[512]{0:T(512)S(1)} %compare_select_fusion.5, f32[4,512]{1,0:T(4,128)S(1)} %dynamic-slice_bitcast_fusion.2, ...), kind=kLoop, calls=%fused_computation.22.clone.1 | loop fusion | flops 50331648 | bytes 43010048 | tf_op jit(solution)/shard_map/while/body/eval_jaxpr/while/body/eval_jaxpr/convert_element_type | solution.py:112
  833.6 8.4 convolution_bitcast_fusion
  842.1 10.5 fusion.83
  852.6 6.3 fusion.84
  861.8 5.3 fusion.45
  869.7 17.6 %all-reduce.1 = (f32[3,256]{1,0:T(4,128)}, f32[1024]{0:T(1024)}) all-reduce(f32[3,256]{1,0:T(4,128)S(1)} %convert_reduce_fusion.1, f32[1024]{0:T(1024)S(1)} %copy-done.40), channel_id=1, replica_groups=mesh['dp'=8,'tensor'=4] {'dp'}, use_global_device_ids=true, to_apply=%region_25.26 | all-reduce | flops 1792 | bytes 14336 | tf_op jit(solution)/shard_map/psum | solution.py:264
  887.3 26.5 %reduce-scatter.11.cloned.1.call-done = f32[512,1024]{1,0:T(8,128)} async-done(((f32[2048,1024]{1,0:T(8,128)}), f32[512,1024]{1,0:T(8,128)}) %reduce-scatter.11.cloned.1.call-update) | async-done | bytes 2097168 | tf_op jit(solution)/shard_map/reduce_scatter | solution.py:254
  916.5 43.4 %all-reduce = (f32[1024]{0:T(1024)}, f32[1024]{0:T(1024)}, f32[1024]{0:T(1024)}, f32[1024]{0:T(1024)}, f32[1024]{0:T(1024)}, /*index=5*/f32[1024]{0:T(1024)}) all-reduce(f32[1024]{0:T(1024)S(1)} %get-tuple-element.248, f32[1024]{0:T(1024)S(1)} %get-tuple-element.253, ...), channel_id=1, replica_groups=mesh['dp'=8,'tensor'=4] {'dp','tensor'}, use_global_device_ids=true, to_apply=%region_20.21 | all-reduce | flops 6144 | bytes 49152 | tf_op jit(solution)/shard_map/psum | solution.py:275
  963.5 355.0 %all-reduce.5.cloned.1.call-done = (f32[1024,3,256]{2,0,1:T(8,128)}, f32[256,1024]{1,0:T(8,128)}, f32[1024,1024]{1,0:T(8,128)}, f32[1024,1024]{1,0:T(8,128)}) async-done(((f32[1024,3,256]{2,0,1:T(8,128)}, f32[256,1024]{1,0:T(8,128)}, f32[1024,1024]{1,0:T(8,128)}, f32[1024,1024]{1,0:T(8,128)}), (f32[1024,3,256]{2,0,1:T(8,128)}, f32[256,1024]{1,0:T(8,128)}, f32[1024,1024]{1,0:T(8,128)}, ...) | async-done | bytes 12582928 | tf_op jit(solution)/shard_map/psum | solution.py:264
  (283 shorter events, 170.2 us)
Async XLA Ops:
  7.2 314.7 %copy-start = (bf16[1024,1024]{1,0:T(8,128)(2,1)S(1)}, bf16[1024,1024]{1,0:T(8,128)(2,1)}, u32[]{:S(2)}) copy-start(bf16[1024,1024]{1,0:T(8,128)(2,1)} %param.30) | copy-start | bytes 6291460
  7.2 41.6 %copy-start.46 = (f32[3,256]{1,0:T(4,128)S(1)}, f32[3,256]{1,0:T(4,128)}, u32[]{:S(2)}) copy-start(f32[3,256]{1,0:T(4,128)} %param.23) | copy-start | bytes 9220
  7.2 41.6 %all-gather.5.cloned.1.call-start = ((), (), s32[]{:S(2)}) async-start(), calls=%async_computation.4 | async-start | bytes 5242880 | tf_op jit(solution)/shard_map/all_gather | solution.py:181
  8.8 40.0 %copy-start.28 = (f32[512]{0:T(512)}, f32[512]{0:T(512)S(1)}, u32[]{:S(2)}) copy-start(f32[512]{0:T(512)S(1)} %broadcast_multiply_fusion.5) | copy-start | bytes 6148
  10.5 38.3 %copy-start.32 = (f32[512]{0:T(512)}, f32[512]{0:T(512)S(1)}, u32[]{:S(2)}) copy-start(f32[512]{0:T(512)S(1)} %add_rsqrt_fusion.1) | copy-start | bytes 6148
  13.2 232.5 %reduce-scatter.5.cloned.1.call-start = ((), (), s32[]{:S(2)}) async-start(), calls=%async_computation.5 | async-start | bytes 10485760 | tf_op jit(solution)/shard_map/reduce_scatter | solution.py:195
  173.8 71.9 %copy-start.41 = (f32[1024]{0:T(1024)S(1)}, f32[1024]{0:T(1024)}, u32[]{:S(2)}) copy-start(f32[1024]{0:T(1024)} %param.25) | copy-start | bytes 12292
  173.8 75.4 %copy-start.30 = (f32[1024]{0:T(1024)S(1)}, f32[1024]{0:T(1024)}, u32[]{:S(2)}) copy-start(f32[1024]{0:T(1024)} %param.26) | copy-start | bytes 12292
  173.8 75.4 %copy-start.39 = (f32[1024]{0:T(1024)S(1)}, f32[1024]{0:T(1024)}, u32[]{:S(2)}) copy-start(f32[1024]{0:T(1024)} %param.27) | copy-start | bytes 12292
  173.8 111.4 %all-gather.7.cloned.1.call-start = ((), (), s32[]{:S(2)}) async-start(), calls=%async_computation.6 | async-start | bytes 5242880 | tf_op jit(solution)/shard_map/all_gather | solution.py:207
  250.6 71.2 %all-gather.9.cloned.1.call-start = ((), (), s32[]{:S(2)}) async-start(), calls=%async_computation.8 | async-start | bytes 5242880 | tf_op jit(solution)/shard_map/all_gather | solution.py:217
  253.8 68.0 %copy-start.47 = (f32[1024]{0:T(1024)S(1)}, f32[1024]{0:T(1024)}, u32[]{:S(2)}) copy-start(f32[1024]{0:T(1024)} %param.29) | copy-start | bytes 12292
  253.8 163.9 %reduce-scatter.9.cloned.1.call-start = ((), (), s32[]{:S(2)}) async-start(), calls=%async_computation.9 | async-start | bytes 10485760 | tf_op jit(solution)/shard_map/reduce_scatter | solution.py:224
  321.9 16.9 %copy-start.45 = (bf16[1024,1024]{1,0:T(8,128)(2,1)S(1)}, bf16[1024,1024]{1,0:T(8,128)(2,1)}, u32[]{:S(2)}) copy-start(bf16[1024,1024]{1,0:T(8,128)(2,1)} %param.28) | copy-start | bytes 6291460
  345.8 146.1 %reduce-scatter.7.cloned.1.call-start = ((), (), s32[]{:S(2)}) async-start(), calls=%async_computation.7 | async-start | bytes 10485760 | tf_op jit(solution)/shard_map/reduce_scatter | solution.py:211
  355.2 62.4 %copy-start.7 = (f32[512,1024]{1,0:T(8,128)S(1)}, f32[512,1024]{1,0:T(8,128)}, u32[]{:S(2)}) copy-start(f32[512,1024]{1,0:T(8,128)} %copy-done.6) | copy-start | bytes 6291460
  355.3 136.6 %copy-start.38 = (f32[1024]{0:T(1024)S(1)}, f32[1024]{0:T(1024)}, u32[]{:S(2)}) copy-start(f32[1024]{0:T(1024)} %param.31) | copy-start | bytes 12292
  355.3 178.2 %all-gather.11.cloned.1.call-start = ((), (), s32[]{:S(2)}) async-start(), calls=%async_computation.10 | async-start | bytes 5242880 | tf_op jit(solution)/shard_map/all_gather | solution.py:232
  496.3 37.1 %copy-start.27 = (bf16[256,1024]{1,0:T(8,128)(2,1)S(1)}, bf16[256,1024]{1,0:T(8,128)(2,1)}, u32[]{:S(2)}) copy-start(bf16[256,1024]{1,0:T(8,128)(2,1)} %param.24) | copy-start | bytes 1572868
  498.8 415.1 %reduce-scatter.11.cloned.1.call-start = ((), (), s32[]{:S(2)}) async-start(), calls=%async_computation.11 | async-start | bytes 10485760 | tf_op jit(solution)/shard_map/reduce_scatter | solution.py:254
  547.7 9.2 copy-start.18
  557.0 10.8 copy-start.25
  567.8 20.4 %copy-start.19 = (f32[2048,4,64]{0,2,1:T(8,128)}, f32[2048,4,64]{0,2,1:T(8,128)S(1)}, u32[]{:S(2)}) copy-start(f32[2048,4,64]{0,2,1:T(8,128)S(1)} %fusion.148) | copy-start | bytes 6291460 | tf_op jit(solution)/shard_map/while/body/eval_jaxpr/while
  588.2 15.8 %copy-start.21 = (bf16[4,512,4,64]{1,3,2,0:T(8,128)(2,1)S(1)}, bf16[4,512,4,64]{1,3,2,0:T(8,128)(2,1)}, u32[]{:S(2)}) copy-start(bf16[4,512,4,64]{1,3,2,0:T(8,128)(2,1)} %get-tuple-element.489) | copy-start | bytes 3145732 | tf_op jit(solution)/shard_map/while/body/eval_jaxpr/while
  624.2 10.8 copy-start.25
  635.0 20.4 %copy-start.19 = (f32[2048,4,64]{0,2,1:T(8,128)}, f32[2048,4,64]{0,2,1:T(8,128)S(1)}, u32[]{:S(2)}) copy-start(f32[2048,4,64]{0,2,1:T(8,128)S(1)} %fusion.148) | copy-start | bytes 6291460 | tf_op jit(solution)/shard_map/while/body/eval_jaxpr/while
  655.5 15.8 %copy-start.21 = (bf16[4,512,4,64]{1,3,2,0:T(8,128)(2,1)S(1)}, bf16[4,512,4,64]{1,3,2,0:T(8,128)(2,1)}, u32[]{:S(2)}) copy-start(bf16[4,512,4,64]{1,3,2,0:T(8,128)(2,1)} %get-tuple-element.489) | copy-start | bytes 3145732 | tf_op jit(solution)/shard_map/while/body/eval_jaxpr/while
  682.2 9.2 copy-start.18
  691.5 10.8 copy-start.25
  702.3 20.4 %copy-start.19 = (f32[2048,4,64]{0,2,1:T(8,128)}, f32[2048,4,64]{0,2,1:T(8,128)S(1)}, u32[]{:S(2)}) copy-start(f32[2048,4,64]{0,2,1:T(8,128)S(1)} %fusion.148) | copy-start | bytes 6291460 | tf_op jit(solution)/shard_map/while/body/eval_jaxpr/while
  722.7 15.8 %copy-start.21 = (bf16[4,512,4,64]{1,3,2,0:T(8,128)(2,1)S(1)}, bf16[4,512,4,64]{1,3,2,0:T(8,128)(2,1)}, u32[]{:S(2)}) copy-start(bf16[4,512,4,64]{1,3,2,0:T(8,128)(2,1)} %get-tuple-element.489) | copy-start | bytes 3145732 | tf_op jit(solution)/shard_map/while/body/eval_jaxpr/while
  758.7 10.8 copy-start.25
  769.5 20.4 %copy-start.19 = (f32[2048,4,64]{0,2,1:T(8,128)}, f32[2048,4,64]{0,2,1:T(8,128)S(1)}, u32[]{:S(2)}) copy-start(f32[2048,4,64]{0,2,1:T(8,128)S(1)} %fusion.148) | copy-start | bytes 6291460 | tf_op jit(solution)/shard_map/while/body/eval_jaxpr/while
  790.0 15.8 %copy-start.21 = (bf16[4,512,4,64]{1,3,2,0:T(8,128)(2,1)S(1)}, bf16[4,512,4,64]{1,3,2,0:T(8,128)(2,1)}, u32[]{:S(2)}) copy-start(bf16[4,512,4,64]{1,3,2,0:T(8,128)(2,1)} %get-tuple-element.489) | copy-start | bytes 3145732 | tf_op jit(solution)/shard_map/while/body/eval_jaxpr/while
  827.4 33.8 %copy-start.13 = (bf16[2048,1,256]{2,0,1:T(8,128)(2,1)}, bf16[2048,1,256]{2,0,1:T(8,128)(2,1)S(1)}, u32[]{:S(2)}) copy-start(bf16[2048,1,256]{2,0,1:T(8,128)(2,1)S(1)} %reshape.261) | copy-start | bytes 3145732
  830.1 31.1 %copy-start.16 = (bf16[2048,1,256]{2,0,1:T(8,128)(2,1)}, bf16[2048,1,256]{2,0,1:T(8,128)(2,1)S(1)}, u32[]{:S(2)}) copy-start(bf16[2048,1,256]{2,0,1:T(8,128)(2,1)S(1)} %copy.45) | copy-start | bytes 3145732
  842.0 476.5 %all-reduce.5.cloned.1.call-start = ((), (), s32[]{:S(2)}) async-start(), calls=%async_computation.12 | async-start | bytes 25165824 | tf_op jit(solution)/shard_map/psum | solution.py:264
  842.1 10.5 copy-start.43
  842.1 10.5 copy-start.48
  867.1 46.8 %copy-start.8 = (bf16[512,1024]{1,0:T(8,128)(2,1)S(1)}, bf16[512,1024]{1,0:T(8,128)(2,1)}, u32[]{:S(2)}) copy-start(bf16[512,1024]{1,0:T(8,128)(2,1)} %param.19) | copy-start | bytes 3145732
  867.1 46.8 %copy-start.29 = (f32[512]{0:T(512)S(1)}, f32[512]{0:T(512)}, u32[]{:S(2)}) copy-start(f32[512]{0:T(512)} %copy-done.28) | copy-start | bytes 6148
  867.1 46.8 %copy-start.31 = (f32[1024]{0:T(1024)S(1)}, f32[1024]{0:T(1024)}, u32[]{:S(2)}) copy-start(f32[1024]{0:T(1024)} %param.20) | copy-start | bytes 12292
  867.1 46.8 %copy-start.33 = (f32[512]{0:T(512)S(1)}, f32[512]{0:T(512)}, u32[]{:S(2)}) copy-start(f32[512]{0:T(512)} %copy-done.32) | copy-start | bytes 6148
  867.1 49.3 %copy-start.34 = (f32[1024]{0:T(1024)S(1)}, f32[1024]{0:T(1024)}, u32[]{:S(2)}) copy-start(f32[1024]{0:T(1024)} %get-tuple-element.306) | copy-start | bytes 12292
  867.2 49.3 %copy-start.35 = (f32[1024]{0:T(1024)S(1)}, f32[1024]{0:T(1024)}, u32[]{:S(2)}) copy-start(f32[1024]{0:T(1024)} %get-tuple-element.319) | copy-start | bytes 12292
  867.2 49.3 %copy-start.36 = (f32[1024]{0:T(1024)S(1)}, f32[1024]{0:T(1024)}, u32[]{:S(2)}) copy-start(f32[1024]{0:T(1024)} %get-tuple-element.246) | copy-start | bytes 12292
  867.2 49.3 %copy-start.37 = (f32[1024]{0:T(1024)S(1)}, f32[1024]{0:T(1024)}, u32[]{:S(2)}) copy-start(f32[1024]{0:T(1024)} %get-tuple-element.252) | copy-start | bytes 12292
  867.2 92.7 %copy-start.10 = (f32[512,1024]{1,0:T(8,128)S(1)}, f32[512,1024]{1,0:T(8,128)}, u32[]{:S(2)}) copy-start(f32[512,1024]{1,0:T(8,128)} %copy-done.9) | copy-start | bytes 6291460
  (41 other events, 181.4 us)
Sparse Core Ops, SparseCore 0:
  13.3 35.4 all-gather.4
  173.9 71.7 reduce-scatter.4
  250.7 34.4 all-gather.6
  287.3 34.4 all-gather.8
  345.9 71.6 reduce-scatter.8
  420.1 71.7 reduce-scatter.6
  498.9 34.4 all-gather.10
  842.1 71.6 reduce-scatter.10
  919.8 398.6 all-reduce.4
where the time goes:
time: 1350 us; the launch traced here: 1340 us
  waiting for transfers between devices  713 us (53%)
  matrix products  320 us (24%)
  other arithmetic  142 us (11%)
  local copies, waits for them, and re-layouts  75 us (6%)
  blocking collectives  61.1 us (5%)
  between operations  15.1 us (1%)
    psum x1, waiting for transfers between devices, on_device(): lax.psum((grad_triple_weight, grad_triple_bias, grad_merge_weight, grad_u...  355 us
    dot_general x4, matrix products, one_block(): jnp.einsum('qhd,khd->hqk', grad_block, value_slot, preferred_element_type...  81.7 us
    reduce_scatter x1, waiting for transfers between devices, on_device(): lax.psum_scatter(jnp.dot(block_part, merge_weight, preferred_element_type...  71.8 us
    reduce_scatter x1, waiting for transfers between devices, on_device(): lax.psum_scatter(jnp.dot(block_part, down_weight, preferred_element_type=...  71.1 us
    convert_element_type x4, other arithmetic, one_block(): (signed * (score_sign * grad_weights - row_term)).astype(jnp.bfloat16)  63.1 us
    reduce_scatter x1, waiting for transfers between devices, on_device(): lax.psum_scatter(contract_cols(block_part, up_weight), 'tensor', scatter_...  61.9 us
    dot_general x4, matrix products, one_block(): jnp.einsum('hqk,khd->qhd', weights, value_slot, preferred_element_type=jn...  47.9 us
    psum x1, blocking collectives, on_device(): lax.psum((grad_first_gain, grad_first_shift, jnp.sum(grad_residual, axis=...  43.4 us
  transfers between devices with their start and end apart: 9, of which 9 were waited for; matrix products, arithmetic and copies ran while one was open for 4% of the time, Pallas kernels for 0%

commit v1 on v0

v1 whole, which is shorter than its diff:
```python
import functools

import jax
import jax.numpy as jnp
from jax import lax
from jax.experimental import pallas as pl
from jax.experimental.pallas import tpu as pltpu
from jax.sharding import PartitionSpec as P

EPS = 1e-05
HD = 64
LOG2E = 1.4426950408889634
SC = HD ** (-0.5) * LOG2E
BIG = 1e30
NT = (((1,), (1,)), ((), ()))
TN = (((0,), (0,)), ((), ()))
NN = (((1,), (0,)), ((), ()))


def mm(a, b, dims):
    return lax.dot_general(a, b, dims, preferred_element_type=jnp.float32)


def sgn_of(s):
    return jnp.minimum(jnp.maximum(s * BIG, -1.0), 1.0)


def fwd_kernel(bq, bk, len_ref, q_ref, k_ref, v_ref, o_ref, lse_ref, s_sc, v0_sc, v1_sc):
    n = q_ref.shape[0]
    lane = lax.broadcasted_iota(jnp.int32, (1, 128), 1)
    hm = [lane < HD, lane >= HD]
    v_sc = [v0_sc, v1_sc]
    for h in range(2):
        v_sc[h][...] = jnp.where(hm[h], v_ref[...], jnp.zeros_like(v_ref))
    length = len_ref[0]
    row = lax.broadcasted_iota(jnp.int32, (bq, bk), 0)
    col = lax.broadcasted_iota(jnp.int32, (bq, bk), 1)

    def fold(x, op):
        r = x[:, :128]
        for c in range(1, bk // 128):
            r = op(r, x[:, c * 128:(c + 1) * 128])
        return r

    def qblock(i, _):
        q0 = pl.multiple_of(i * bq, bq)
        qb = q_ref[pl.ds(q0, bq), :]
        qh = [jnp.where(hm[h], qb, jnp.zeros_like(qb)) for h in range(2)]
        nfull = q0 // bk

        def p1(j, mx):
            kb = k_ref[pl.ds(pl.multiple_of(j * bk, bk), bk), :]
            out = []
            for h in range(2):
                s = mm(qh[h], kb, NT)
                s_sc[h, j] = s
                out.append(jnp.maximum(mx[h], fold(jnp.abs(s), jnp.maximum)))
            return tuple(out)

        zero = jnp.zeros((bq, 128), jnp.float32)
        mx = lax.fori_loop(0, nfull, p1, (zero, zero))
        kb = k_ref[pl.ds(pl.multiple_of(nfull * bk, bk), bk), :]
        mask = (col + nfull * bk) <= (row + q0)
        mrow = []
        for h in range(2):
            s = mm(qh[h], kb, NT)
            s_sc[h, nfull] = jnp.where(mask, s, 0.0)
            m = jnp.maximum(mx[h], fold(jnp.where(mask, jnp.abs(s), 0.0), jnp.maximum))
            mrow.append(jnp.max(m, axis=1, keepdims=True) * SC)

        def p2(j, carry):
            new = []
            for h in range(2):
                acc, ls = carry[h]
                s = s_sc[h, j]
                p = jnp.exp2(jnp.abs(s) * SC - mrow[h])
                ls = ls + fold(p, jnp.add)
                w = (sgn_of(s) * p).astype(jnp.bfloat16)
                acc = acc + mm(w, v_sc[h][pl.ds(pl.multiple_of(j * bk, bk), bk), :], NN)
                new.append((acc, ls))
            return tuple(new)

        carry = lax.fori_loop(0, nfull, p2, ((zero, zero), (zero, zero)))
        outs = []
        for h in range(2):
            acc, ls = carry[h]
            s = s_sc[h, nfull]
            p = jnp.where(mask, jnp.exp2(jnp.abs(s) * SC - mrow[h]), 0.0)
            ls = ls + fold(p, jnp.add)
            w = (sgn_of(s) * p).astype(jnp.bfloat16)
            acc = acc + mm(w, v_sc[h][pl.ds(pl.multiple_of(nfull * bk, bk), bk), :], NN)
            tot = jnp.sum(ls, axis=1, keepdims=True)
            outs.append(acc / tot)
            lse = jnp.broadcast_to(mrow[h] + jnp.log(tot) * LOG2E, (bq, 128))
            lse_ref[0, h:h + 1, pl.ds(q0, bq)] = jnp.transpose(lse)[0:1, :]
        live = (lax.broadcasted_iota(jnp.int32, (bq, 1), 0) + q0) < length
        o_ref[pl.ds(q0, bq), :] = jnp.where(live, outs[0] + outs[1], 0.0).astype(jnp.bfloat16)
        return 0

    lax.fori_loop(0, n // bq, qblock, 0)


def attend_fwd(mixed, lengths, bq=512, bk=512):
    n = mixed.shape[0]
    width = mixed.shape[1] // 3
    pairs = width // 128
    spec = lambda off: pl.BlockSpec((n, 128), lambda p, off=off: (0, off + p))
    return pl.pallas_call(
        functools.partial(fwd_kernel, bq, bk),
        grid=(pairs,),
        out_shape=(jax.ShapeDtypeStruct((n, width), jnp.bfloat16), jax.ShapeDtypeStruct((pairs, 8, n), jnp.float32)),
        in_specs=[pl.BlockSpec(memory_space=pltpu.SMEM), spec(0), spec(pairs), spec(2 * pairs)],
        out_specs=(pl.BlockSpec((n, 128), lambda p: (0, p)), pl.BlockSpec((1, 8, n), lambda p: (p, 0, 0))),
        scratch_shapes=[pltpu.VMEM((2, n // bk, bq, bk), jnp.float32)] + [pltpu.VMEM((n, 128), jnp.bfloat16)] * 2,
        compiler_params=pltpu.CompilerParams(vmem_limit_bytes=48 << 20),
        cost_estimate=pl.CostEstimate(flops=4 * n * n * width, bytes_accessed=8 * n * width, transcendentals=n * n * width // 128),
        name="attend_fwd",
    )(lengths, mixed, mixed, mixed)


def bwd_kernel(bq, bk, q_ref, k_ref, v_ref, do_ref, o_ref, lse_ref, dq_ref, dk_ref, dv_ref,
               qm, km, dom, dsc, dq_acc):
    n = q_ref.shape[0]
    lane = lax.broadcasted_iota(jnp.int32, (1, 128), 1)
    hm = [lane < HD, lane >= HD]
    for h in range(2):
        for r in range(0, n, 512):
            sl = pl.ds(r, 512)
            z = jnp.zeros((512, 128), jnp.bfloat16)
            qm[h, sl, :] = jnp.where(hm[h], q_ref[sl, :], z)
            km[h, sl, :] = jnp.where(hm[h], k_ref[sl, :], z)
            d = jnp.where(hm[h], do_ref[sl, :], z)
            dom[h, sl, :] = d
            prod = d.astype(jnp.float32) * o_ref[sl, :].astype(jnp.float32)
            dd = jnp.broadcast_to(jnp.sum(prod, axis=1, keepdims=True), (512, 128))
            dsc[h:h + 1, sl] = jnp.transpose(dd)[0:1, :]
    dq_acc[...] = jnp.zeros_like(dq_acc)
    row = lax.broadcasted_iota(jnp.int32, (bk, bq), 0)
    col = lax.broadcasted_iota(jnp.int32, (bk, bq), 1)

    def tile(j, i, dk, dv, diag):
        k0 = pl.multiple_of(j * bk, bk)
        q0 = pl.multiple_of(i * bq, bq)
        ks, qs = pl.ds(k0, bk), pl.ds(q0, bq)
        kb, vb = k_ref[ks, :], v_ref[ks, :]
        dq = None
        for h in range(2):
            qh = qm[h, qs, :]
            doh = dom[h, qs, :]
            s = mm(kb, qh, NT)
            dp = mm(vb, doh, NT)
            p = jnp.exp2(jnp.abs(s) * SC - lse_ref[0, h:h + 1, qs])
            if diag:
                p = jnp.where((row + k0) <= (col + q0), p, 0.0)
            sg = sgn_of(s)
            w = sg * p
            ds = (w * (sg * dp - dsc[h:h + 1, qs])).astype(jnp.bfloat16)
            dv = dv + mm(w.astype(jnp.bfloat16), doh, NN)
            dk = dk + mm(ds, qh, NN)
            t = mm(ds, km[h, ks, :], TN)
            dq = t if dq is None else dq + t
        dq_acc[qs, :] += dq
        return dk, dv

    r = bk // bq
    def kvblock(j, _):
        z = jnp.zeros((bk, 128), jnp.float32)
        dk, dv = z, z
        for a in range(r):
            dk, dv = tile(j, j * r + a, dk, dv, True)
        dk, dv = lax.fori_loop((j + 1) * r, n // bq, lambda i, c: tile(j, i, c[0], c[1], False), (dk, dv))
        ks = pl.ds(pl.multiple_of(j * bk, bk), bk)
        dk_ref[ks, :] = (dk * HD ** (-0.5)).astype(jnp.bfloat16)
        dv_ref[ks, :] = dv.astype(jnp.bfloat16)
        return 0

    lax.fori_loop(0, n // bk, kvblock, 0)
    dq_ref[...] = (dq_acc[...] * HD ** (-0.5)).astype(jnp.bfloat16)


def attend_bwd(mixed, attended, lse, grad, bq=512, bk=512):
    n = mixed.shape[0]
    width = mixed.shape[1] // 3
    pairs = width // 128
    spec = lambda off: pl.BlockSpec((n, 128), lambda p, off=off: (0, off + p))
    o = jax.ShapeDtypeStruct((n, width), jnp.bfloat16)
    return pl.pallas_call(
        functools.partial(bwd_kernel, bq, bk),
        grid=(pairs,),
        out_shape=(o, o, o),
        in_specs=[spec(0), spec(pairs), spec(2 * pairs), spec(0), spec(0), pl.BlockSpec((1, 8, n), lambda p: (p, 0, 0))],
        out_specs=(spec(0),) * 3,
        scratch_shapes=[pltpu.VMEM((2, n, 128), jnp.bfloat16)] * 3 + [pltpu.VMEM((8, n), jnp.float32), pltpu.VMEM((n, 128), jnp.float32)],
        compiler_params=pltpu.CompilerParams(vmem_limit_bytes=48 << 20),
        cost_estimate=pl.CostEstimate(flops=10 * n * n * width, bytes_accessed=16 * n * width, transcendentals=n * n * width // 128),
        name="attend_bwd",
    )(mixed, mixed, mixed, grad, attended, lse)


BF = jnp.bfloat16
F32 = jnp.float32
CHUNKS = 4
VMEM_SPEC = pl.BlockSpec(memory_space=pltpu.VMEM)
SMEM_SPEC = pl.BlockSpec(memory_space=pltpu.SMEM)


def remote(src, dst, send_sem, recv_sem, axis, index):
    return pltpu.make_async_remote_copy(
        src_ref=src,
        dst_ref=dst,
        send_sem=send_sem,
        recv_sem=recv_sem,
        device_id={axis: index},
        device_id_type=pl.DeviceIdType.MESH,
    )


class Group:
    def __init__(self, size):
        self.size = size
        self.chips = size // 2
        self.me = lax.axis_index("tensor")
        self.chip = self.me // 2
        self.core = self.me % 2
        self.sibling = self.chip * 2 + 1 - self.core

    def same(self, off):
        return (self.chip + off) % self.chips * 2 + self.core

    def other(self, off):
        return (self.chip + off) % self.chips * 2 + 1 - self.core

    def greet(self, barrier):
        peers = [self.sibling] + [self.same(off) for off in range(1, self.chips)]
        for peer in peers:
            pl.semaphore_signal(
                barrier, inc=1, device_id={"tensor": peer}, device_id_type=pl.DeviceIdType.MESH
            )
        return len(peers)


def loop(count, body):
    def step(k, carry):
        body(k)
        return carry

    lax.fori_loop(0, count, step, 0)


def loop_range(low, high, body):
    def step(k, carry):
        body(k)
        return carry

    lax.fori_loop(low, high, step, 0)


class Gather:
    def __init__(self, group, buf, sem):
        self.g, self.buf, self.sem = group, buf, sem

    def own(self, off, k):
        g, sem = self.g, self.sem
        here = self.buf.at[g.me, k]
        if off == 0:
            return remote(here, here, sem.at[0, 0, k], sem.at[3, 0, k], "tensor", g.sibling)
        return remote(
            here, here, sem.at[0, off, k], sem.at[2, g.chips - off, k], "tensor", g.same(off)
        )

    def passed(self, off, k):
        here = self.buf.at[self.g.same(off), k]
        sem = self.sem
        return remote(here, here, sem.at[1, off, k], sem.at[3, off, k], "tensor", self.g.sibling)

    def send(self, k):
        for off in list(range(1, self.g.chips)) + [0]:
            self.own(off, k).start()

    def forward(self, k):
        g, sem = self.g, self.sem
        for off in range(1, g.chips):
            here = self.buf.at[g.same(off), k]
            remote(
                here, here, sem.at[0, off, k], sem.at[2, off, k], "tensor", g.same(off)
            ).wait_recv()
            self.passed(off, k).start()

    def wait(self, k):
        g, sem = self.g, self.sem
        for off in range(g.chips):
            here = self.buf.at[g.other(off), k]
            remote(
                here, here, sem.at[0, 0, k], sem.at[3, off, k], "tensor", g.sibling
            ).wait_recv()

    def drain(self, k):
        for off in range(self.g.chips):
            self.own(off, k).wait_send()
            if off:
                self.passed(off, k).wait_send()


class Scatter:
    def __init__(self, group, part, in_near, out_far, in_far, sem):
        self.g, self.part, self.sem = group, part, sem
        self.in_near, self.out_far, self.in_far = in_near, out_far, in_far

    def near(self, off, k):
        sem = self.sem
        return remote(
            self.part.at[self.g.other(off), k], self.in_near.at[off, k], sem.at[0, off, k],
            sem.at[1, off, k], "tensor", self.g.sibling,
        )

    def far(self, off, k):
        g, sem = self.g, self.sem
        back = g.chips - off
        return remote(
            self.out_far.at[off - 1, k], self.in_far.at[back - 1, k], sem.at[2, off, k],
            sem.at[3, back, k], "tensor", g.same(off),
        )

    def send(self, k):
        for off in list(range(1, self.g.chips)) + [0]:
            self.near(off, k).start()

    def combine(self, k):
        g = self.g
        for off in range(1, g.chips):
            self.near(off, k).wait_recv()
            total = self.part[g.same(off), k].astype(F32) + self.in_near[off, k].astype(F32)
            self.out_far[off - 1, k] = total.astype(BF)
            self.far(off, k).start()

    def final(self, k):
        g, sem = self.g, self.sem
        self.near(0, k).wait_recv()
        total = self.part[g.me, k].astype(F32) + self.in_near[0, k].astype(F32)
        for off in range(1, g.chips):
            remote(
                self.out_far.at[off - 1, k], self.in_far.at[off - 1, k], sem.at[2, off, k],
                sem.at[3, off, k], "tensor", g.same(off),
            ).wait_recv()
            total = total + self.in_far[off - 1, k].astype(F32)
        return total

    def drain(self, k):
        for off in range(self.g.chips):
            self.near(off, k).wait_send()
            if off:
                self.far(off, k).wait_send()


def scatter_scratch(size, rows, d):
    chips = size // 2
    block = lambda c: pltpu.VMEM((c, CHUNKS, rows, d), BF)
    return [pltpu.VMEM((size, CHUNKS, rows, d), BF), block(chips), block(chips - 1), block(chips - 1)]


def sems(group):
    return pltpu.SemaphoreType.DMA((4, group // 2, CHUNKS))


class Place:
    def __init__(self, count):
        self.count = count
        self.line = count // 2
        self.me = lax.axis_index("dp")
        self.row = self.me // 2
        self.side = self.me % 2
        self.partner = self.row * 2 + 1 - self.side

    def step(self, off):
        return (self.row + off) % self.line

    def peer(self, off):
        return self.step(off) * 2 + self.side

    def greet(self, barrier):
        peers = [self.partner] + [self.peer(off) for off in range(1, self.line)]
        for peer in peers:
            pl.semaphore_signal(
                barrier, inc=1, device_id={"dp": peer}, device_id_type=pl.DeviceIdType.MESH
            )
        return len(peers)


class Total:
    def __init__(self, place, src, near, half, far, out, sem):
        self.p, self.src, self.near = place, src, near
        self.half, self.far, self.out, self.sem = half, far, out, sem

    def pair(self):
        p, sem = self.p, self.sem
        return remote(
            self.src.at[1 - p.side], self.near, sem.at[0, 0], sem.at[1, 0], "dp", p.partner
        )

    def piece(self, off):
        p, sem = self.p, self.sem
        back = p.line - off
        return remote(
            self.half.at[p.step(off)], self.far.at[back - 1], sem.at[0, off], sem.at[1, back],
            "dp", p.peer(off),
        )

    def start(self):
        self.pair().start()

    def halve(self):
        self.pair().wait_recv()
        for j in range(self.p.line):
            total = self.src[self.p.side, j].astype(F32) + self.near[j].astype(F32)
            self.half[j] = total.astype(BF)
        for off in range(1, self.p.line):
            self.piece(off).start()

    def settle(self):
        p, sem = self.p, self.sem
        total = self.src[p.side, p.row].astype(F32) + self.near[p.row].astype(F32)
        for off in range(1, p.line):
            remote(
                self.half.at[p.row], self.far.at[off - 1], sem.at[0, off], sem.at[1, off],
                "dp", p.peer(off),
            ).wait_recv()
            total = total + self.far[off - 1].astype(F32)
        return total.astype(BF)

    def drain(self):
        self.pair().wait_send()
        for off in range(1, self.p.line):
            self.piece(off).wait_send()


class Share:
    def __init__(self, place, out, sem):
        self.p, self.out, self.sem = place, out, sem

    def piece(self, off):
        p, sem = self.p, self.sem
        here = self.out.at[p.side, p.row]
        return remote(here, here, sem.at[0, off], sem.at[1, p.line - off], "dp", p.peer(off))

    def half(self):
        p, sem = self.p, self.sem
        here = self.out.at[p.side]
        return remote(here, here, sem.at[0, 0], sem.at[1, 0], "dp", p.partner)

    def start(self, piece):
        self.out[self.p.side, self.p.row] = piece
        for off in range(1, self.p.line):
            self.piece(off).start()

    def spread(self):
        p, sem = self.p, self.sem
        for off in range(1, p.line):
            here = self.out.at[p.side, p.step(off)]
            remote(here, here, sem.at[0, off], sem.at[1, off], "dp", p.peer(off)).wait_recv()
        self.half().start()

    def finish(self):
        p, sem = self.p, self.sem
        there = self.out.at[1 - p.side]
        remote(there, there, sem.at[0, 0], sem.at[1, 0], "dp", p.partner).wait_recv()
        for off in range(1, p.line):
            self.piece(off).wait_send()
        self.half().wait_send()


def total_scratch(line, block):
    return [pltpu.VMEM((line,) + block, BF)] * 2 + [
        pltpu.VMEM((line - 1,) + block, BF),
        pltpu.SemaphoreType.DMA((2, line)),
    ]


def norm_stats(x):
    centred = x - jnp.mean(x, axis=-1, keepdims=True)
    inverse = lax.rsqrt(jnp.mean(centred * centred, axis=-1, keepdims=True) + EPS)
    return centred * inverse, inverse


def norm_pull(grad, unit, inverse, gain):
    g = grad * gain
    g = g - jnp.mean(g, axis=-1, keepdims=True) - unit * jnp.mean(g * unit, axis=-1, keepdims=True)
    return g * inverse


def rows_of(ref, k, cols=slice(None)):
    x = ref[:, k, :, cols]
    return x.reshape(x.shape[0] * x.shape[1], x.shape[2])


def col_sum(x):
    return jnp.sum(x, axis=0, keepdims=True)


def enter_kernel(group):
    barrier = pltpu.get_barrier_semaphore()
    pl.semaphore_wait(barrier, group.greet(barrier))


def project_kernel(size, length, tok, cot, gain, shift, w, b, full, mixed, top, sem):
    g = Group(size)
    rows = tok.shape[0] // CHUNKS
    width = w.shape[2]
    enter_kernel(g)
    gather = Gather(g, full, sem)

    def norm(k):
        unit, _ = norm_stats(tok[pl.ds(pl.multiple_of(k * rows, rows), rows), :].astype(F32))
        full[g.me, k] = (unit * gain[...] + shift[...]).astype(BF)
        gather.send(k)

    loop(CHUNKS, norm)

    def mask(k):
        span = pl.ds(pl.multiple_of(k * rows, rows), rows)
        row = lax.broadcasted_iota(jnp.int32, (rows, 1), 0) + (g.me * CHUNKS + k) * rows
        top[span, :] = jnp.where(row < length[0], cot[span, :].astype(F32), 0.0).astype(BF)

    loop(CHUNKS, mask)

    def multiply(k):
        gather.wait(k)
        x = rows_of(full, k)
        for c in range(3):
            cols = slice(c * width, (c + 1) * width)
            y = (mm(x, w[c], NN) + b[:, cols]).astype(BF)
            for s in range(size):
                mixed[s, k, :, cols] = y[s * rows:(s + 1) * rows]

    def body(k):
        gather.forward(k)

        @pl.when(k > 0)
        def _():
            multiply(k - 1)

    loop(CHUNKS, body)
    multiply(CHUNKS - 1)
    loop(CHUNKS, gather.drain)


def project(size, lengths, tokens, cotangent, gain, shift, w, b):
    rows, d = tokens.shape
    r = rows // CHUNKS
    return pl.pallas_call(
        functools.partial(project_kernel, size),
        out_shape=(
            jax.ShapeDtypeStruct((size, CHUNKS, r, d), BF),
            jax.ShapeDtypeStruct((size, CHUNKS, r, 3 * w.shape[2]), BF),
            jax.ShapeDtypeStruct((rows, d), BF),
        ),
        in_specs=[SMEM_SPEC] + [VMEM_SPEC] * 6,
        out_specs=(VMEM_SPEC,) * 3,
        scratch_shapes=[sems(size)],
        compiler_params=pltpu.CompilerParams(
            collective_id=0, has_side_effects=True, vmem_limit_bytes=40 << 20
        ),
        name="project",
    )(lengths, tokens, cotangent, gain, shift, w, b)


def middle_kernel(
    size, count, length, att, tok, cot, mw, mb, gain, shift, up, ub, down,
    gatt, gres, resid, pout, g_up, g_down, g_merge, small, bias, *rest,
):
    pieces, rest = (rest[:2], rest[2:]) if count else ((), rest)
    part, in_near, out_far, in_far, full, gfull, hid, gb, sem1, sem2, sem3, sem4 = rest[:12]
    rest = rest[12:]
    g = Group(size)
    rows, d = tok.shape[0] // CHUNKS, tok.shape[1]
    units = up.shape[1]
    step = min(256, units)
    p = Place(count) if count else None
    barrier = pltpu.get_barrier_semaphore()
    pl.semaphore_wait(barrier, g.greet(barrier) + (p.greet(barrier) if count else 0))
    first = Scatter(g, part, in_near, out_far, in_far, sem1)
    spread = Gather(g, full, sem2)
    second = Scatter(g, part, in_near, out_far, in_far, sem3)
    back = Gather(g, gfull, sem4)
    span = lambda k: pl.ds(pl.multiple_of(k * rows, rows), rows)
    sums = []
    for ref in (g_down, g_up) if count else ():
        for h in range(2):
            near, half, far, sem = rest[:4]
            rest = rest[4:]
            sums.append(Total(p, ref.at[h], near, half, far, None, sem))

    def merge(k):
        y = mm(rows_of(att, k), mw[...], NN).astype(BF)
        for s in range(size):
            part[s, k] = y[s * rows:(s + 1) * rows]
        first.send(k)

    loop(CHUNKS, merge)
    loop(CHUNKS, first.combine)

    def norm(k):
        x = tok[span(k), :].astype(F32) + first.final(k) + mb[...]
        resid[span(k), :] = x
        unit, _ = norm_stats(x)
        full[g.me, k] = (unit * gain[...] + shift[...]).astype(BF)
        spread.send(k)

    loop(CHUNKS, norm)
    loop(CHUNKS, first.drain)
    bias[...] = jnp.zeros_like(bias)

    def enter(k):
        spread.forward(k)
        spread.wait(k)
        x = rows_of(full, k)
        top = rows_of(cot, k)

        def inner(j):
            cols = pl.ds(pl.multiple_of(j * step, step), step)
            v = mm(x, up[:, cols], NN) + ub[:, cols]
            gh = mm(top, down[cols, :], NT)
            c0, c1 = 0.7978845608, 0.044715
            v2 = v * v
            th = jnp.tanh(c0 * (v + c1 * v2 * v))
            half = 0.5 * (1.0 + th)
            h = (v * half).astype(BF)
            slope = half + 0.5 * v * (1.0 - th * th) * (c0 * (1.0 + 3.0 * c1 * v2))
            gv = (gh * slope).astype(BF)
            bias[0:1, cols] += col_sum(gv.astype(F32))
            for s in range(size):
                hid[s, k, :, cols] = h[s * rows:(s + 1) * rows]
                gb[s, k, :, cols] = gv[s * rows:(s + 1) * rows]

        loop(units // step, inner)

    loop(CHUNKS, enter)

    def flat(ref, cols):
        x = ref[:, :, :, cols]
        return x.reshape(size * CHUNKS * rows, x.shape[3])

    def products(ref, left, right, extent):
        tall = min(256, extent)

        def block(i):
            cols = pl.ds(pl.multiple_of(i * tall, tall), tall)
            y = mm(flat(left, cols), flat(right, slice(None)), TN).astype(BF)
            if not count:
                ref[cols, :] = y
            else:
                deep = ref.shape[3]
                for e in range(tall // deep):
                    f = i * (tall // deep) + e
                    ref[f // (2 * p.line), f // p.line % 2, f % p.line] = y[e * deep:(e + 1) * deep]

        return block, extent // tall

    block, blocks = products(g_down, hid, cot, units)
    if count:
        for h in range(2):
            loop_range(h * blocks // 2, (h + 1) * blocks // 2, block)
            sums[h].start()
    else:
        loop(blocks, block)

    def leave(k):
        h, gv = rows_of(hid, k), rows_of(gb, k)

        def outer(j):
            cols = pl.ds(pl.multiple_of(j * 256, 256), 256)
            y = mm(h, down[:, cols], NN).astype(BF)
            z = mm(gv, up[cols, :], NT).astype(BF)
            for s in range(size):
                pout[s, k, :, cols] = y[s * rows:(s + 1) * rows]
                part[s, k, :, cols] = z[s * rows:(s + 1) * rows]

        loop(d // 256, outer)
        second.send(k)

        @pl.when(k > 0)
        def _():
            second.combine(k - 1)

    if count:
        loop_range(0, 3, leave)
        sums[0].halve()
        loop_range(3, CHUNKS, leave)
    else:
        loop(CHUNKS, leave)
    second.combine(CHUNKS - 1)
    block, blocks = products(g_up, full, gb, d)
    if count:
        for h in range(2):
            loop_range(h * blocks // 2, (h + 1) * blocks // 2, block)
            sums[2 + h].start()
        sums[1].halve()
    else:
        loop(blocks, block)
    loop(CHUNKS, spread.drain)
    small[...] = jnp.zeros_like(small)

    def pull(k):
        gs = second.final(k)
        unit, inverse = norm_stats(resid[span(k), :])
        top = cot[g.me, k].astype(F32)
        gr = top + norm_pull(gs, unit, inverse, gain[...])
        gres[span(k), :] = gr
        gfull[g.me, k] = gr.astype(BF)
        back.send(k)
        small[2:3, :] += col_sum(gr)
        small[3:4, :] += col_sum(gs * unit)
        small[4:5, :] += col_sum(gs)
        small[5:6, :] += col_sum(top)

    loop(CHUNKS, pull)
    loop(CHUNKS, second.drain)
    if count:
        sums[2].halve()

    def last(k):
        back.forward(k)
        back.wait(k)
        y = mm(rows_of(gfull, k), mw[...], NT)
        for s in range(size):
            row = lax.broadcasted_iota(jnp.int32, (rows, 1), 0) + (s * CHUNKS + k) * rows
            gatt[s, k] = jnp.where(row < length[0], y[s * rows:(s + 1) * rows], 0.0).astype(BF)

    loop(CHUNKS // 2, last)
    if count:
        sums[3].halve()
    loop_range(CHUNKS // 2, CHUNKS, last)
    block, blocks = products(g_merge, att, gfull, mw.shape[0])
    if count:
        deep = g_merge.shape[2]
        y = mm(flat(att, slice(None)), flat(gfull, slice(None)), TN).astype(BF)
        for f in range(2 * p.line):
            g_merge[f // p.line, f % p.line] = y[f * deep:(f + 1) * deep]
        for h in range(4):
            pieces[h // 2][h % 2] = sums[h].settle()
        for h in range(4):
            sums[h].drain()
    else:
        loop(blocks, block)
    loop(CHUNKS, back.drain)


def middle(size, count, lengths, att, tokens, cot, mw, mb, gain, shift, up, ub, down):
    rows, d = tokens.shape
    r = rows // CHUNKS
    width, units = mw.shape[0], up.shape[1]
    shape = jax.ShapeDtypeStruct
    wide = lambda c: pltpu.VMEM((size, CHUNKS, r, c), BF)
    line = count // 2
    if count:
        grads = (
            shape((2, 2, line, d // (4 * line), units), BF),
            shape((2, 2, line, units // (4 * line), d), BF),
            shape((2, line, width // (2 * line), d), BF),
        )
        extra = (
            shape((2, units // (4 * line), d), BF),
            shape((2, d // (4 * line), units), BF),
        )
        scratch = total_scratch(line, (units // (4 * line), d)) * 2
        scratch += total_scratch(line, (d // (4 * line), units)) * 2
    else:
        grads = (shape((d, units), BF), shape((units, d), BF), shape((width, d), BF))
        extra, scratch = (), []
    outs = (
        shape((size, CHUNKS, r, width), BF),
        shape((rows, d), F32),
        shape((rows, d), F32),
        shape((size, CHUNKS, r, d), BF),
        *grads,
        shape((8, d), F32),
        shape((8, units), F32),
        *extra,
    )
    return pl.pallas_call(
        functools.partial(middle_kernel, size, count),
        out_shape=outs,
        in_specs=[SMEM_SPEC] + [VMEM_SPEC] * 10,
        out_specs=(VMEM_SPEC,) * len(outs),
        scratch_shapes=scatter_scratch(size, r, d)
        + [wide(d), wide(d), wide(units), wide(units)]
        + [sems(size)] * 4
        + scratch,
        compiler_params=pltpu.CompilerParams(
            collective_id=1, has_side_effects=True, vmem_limit_bytes=63 << 20
        ),
        name="middle",
    )(lengths, att, tokens, cot, mw, mb, gain, shift, up, ub, down)


def tail_kernel(
    size, dq, dk, dv, full, w, tok, gres, gain,
    gtok, g_triple, small, bias,
    part, in_near, out_far, in_far, sem,
):
    g = Group(size)
    rows, d = tok.shape[0] // CHUNKS, tok.shape[1]
    width = dq.shape[3]
    enter_kernel(g)
    scatter = Scatter(g, part, in_near, out_far, in_far, sem)
    span = lambda k: pl.ds(pl.multiple_of(k * rows, rows), rows)
    grads = (dq, dk, dv)

    def back(k):
        def tile(j):
            cols = pl.ds(pl.multiple_of(j * 256, 256), 256)
            z = sum(
                mm(rows_of(x, k), w[c, cols, :], NT)
                for c, x in enumerate(grads)
            )
            for s in range(size):
                part[s, k, :, cols] = z[s * rows:(s + 1) * rows].astype(BF)

        loop(d // 256, tile)
        scatter.send(k)

    loop(CHUNKS, back)
    loop(CHUNKS, scatter.combine)

    def flat(ref, cols):
        x = ref[:, :, :, cols]
        return x.reshape(size * CHUNKS * rows, x.shape[3])

    bias[...] = jnp.zeros_like(bias)
    for c, x in enumerate(grads):
        y = flat(x, slice(None))
        bias[0:1, c * width:(c + 1) * width] = col_sum(y.astype(F32))

        def tile(i):
            more = pl.ds(pl.multiple_of(i * 256, 256), 256)
            g_triple[c, more, :] = mm(flat(full, more), y, TN).astype(BF)

        loop(d // 256, tile)
    small[...] = jnp.zeros_like(small)

    def pull(k):
        gf = scatter.final(k)
        unit, inverse = norm_stats(tok[span(k), :].astype(F32))
        gtok[span(k), :] = gres[span(k), :] + norm_pull(gf, unit, inverse, gain[...])
        small[0:1, :] += col_sum(gf * unit)
        small[1:2, :] += col_sum(gf)

    loop(CHUNKS, pull)
    loop(CHUNKS, scatter.drain)


def tail(size, dq, dk, dv, full, w, tokens, gres, gain):
    rows, d = tokens.shape
    r = rows // CHUNKS
    width = dq.shape[-1]
    shape = jax.ShapeDtypeStruct
    return pl.pallas_call(
        functools.partial(tail_kernel, size),
        out_shape=(
            shape((rows, d), F32),
            shape((3, d, width), BF),
            shape((8, d), F32),
            shape((8, 3 * width), F32),
        ),
        in_specs=[VMEM_SPEC] * 8,
        out_specs=(VMEM_SPEC,) * 4,
        scratch_shapes=scatter_scratch(size, r, d) + [sems(size)],
        compiler_params=pltpu.CompilerParams(
            collective_id=2, has_side_effects=True, vmem_limit_bytes=56 << 20
        ),
        name="tail",
    )(dq, dk, dv, full, w, tokens, gres, gain)


class Everyone:
    def __init__(self, axis, count, buf, sem):
        self.axis, self.count, self.buf, self.sem = axis, count, buf, sem
        self.me = lax.axis_index(axis)

    def copy(self, owner, off, back):
        here = self.buf.at[owner]
        return remote(
            here, here, self.sem.at[0, off], self.sem.at[1, back], self.axis,
            (self.me + off) % self.count,
        )

    def start(self, value):
        self.buf[self.me] = value
        for off in range(1, self.count):
            self.copy(self.me, off, self.count - off).start()

    def finish(self):
        for off in range(1, self.count):
            self.copy((self.me + off) % self.count, off, off).wait_recv()
        total = self.buf[0]
        for j in range(1, self.count):
            total = total + self.buf[j]
        for off in range(1, self.count):
            self.copy(self.me, off, self.count - off).wait_send()
        return total


def late_kernel(
    size, count, bk, mixed, att, gatt, lse, full, w, tok, gres, gain, p_down, p_up, g_merge,
    small_in, bias_in,
    gtok, o_down, o_up, o_merge, o_triple, small,
    qm, km, dom, dsc, dq_acc, gm, g_triple, part, in_near, out_far, in_far, sem,
    m_near, m_half, m_far, m_sem, t_near, t_half, t_far, t_sem, s_sem, t_buf, t_sems, d_buf, d_sems,
):
    g, p = Group(size), Place(count)
    n = mixed.shape[0]
    rows, d = tok.shape[0] // CHUNKS, tok.shape[1]
    width = att.shape[1]
    pairs = width // 128
    barrier = pltpu.get_barrier_semaphore()
    for axis, extent in (("tensor", size), ("dp", count)):
        for off in range(1, extent):
            pl.semaphore_signal(
                barrier,
                inc=1,
                device_id={axis: (lax.axis_index(axis) + off) % extent},
                device_id_type=pl.DeviceIdType.MESH,
            )
    pl.semaphore_wait(barrier, size + count - 2)

    shares = [Share(p, ref.at[h], s_sem.at[2 * a + h]) for a, ref in enumerate((o_down, o_up)) for h in range(2)]
    merge_total = Total(p, g_merge, m_near, m_half, m_far, None, m_sem)
    merge_share = Share(p, o_merge, s_sem.at[4])
    totals = [
        Total(p, g_triple.at[x], t_near.at[x], t_half.at[x], t_far.at[x], None, t_sem.at[x])
        for x in range(pairs)
    ]
    triples = [Share(p, o_triple.at[x], s_sem.at[5 + x]) for x in range(pairs)]
    for h in range(4):
        shares[h].start((p_down, p_up)[h // 2][h % 2])
    merge_total.start()

    lane = lax.broadcasted_iota(jnp.int32, (1, 128), 1)
    heads = [lane < HD, lane >= HD]
    row = lax.broadcasted_iota(jnp.int32, (bk, bk), 0)
    col = lax.broadcasted_iota(jnp.int32, (bk, bk), 1)

    def attention(x, events):
        def lanes(c):
            return slice(c * width + x * 128, c * width + (x + 1) * 128)

        def prepare(i):
            sl = pl.ds(pl.multiple_of(i * bk, bk), bk)
            z = jnp.zeros((bk, 128), BF)
            for h in range(2):
                qm[h, sl, :] = jnp.where(heads[h], mixed[sl, lanes(0)], z)
                km[h, sl, :] = jnp.where(heads[h], mixed[sl, lanes(1)], z)
                do = jnp.where(heads[h], gatt[sl, lanes(0)], z)
                dom[h, sl, :] = do
                prod = do.astype(F32) * att[sl, lanes(0)].astype(F32)
                dd = jnp.broadcast_to(jnp.sum(prod, axis=1, keepdims=True), (bk, 128))
                dsc[h:h + 1, sl] = jnp.transpose(dd)[0:1, :]
            dq_acc[sl, :] = jnp.zeros((bk, 128), F32)

        loop(n // bk, prepare)

        def tile(j, i, dk, dv, diag):
            ks, qs = pl.ds(pl.multiple_of(j * bk, bk), bk), pl.ds(pl.multiple_of(i * bk, bk), bk)
            kb, vb = mixed[ks, lanes(1)], mixed[ks, lanes(2)]
            dq = None
            for h in range(2):
                qh, doh = qm[h, qs, :], dom[h, qs, :]
                s = mm(kb, qh, NT)
                dp = mm(vb, doh, NT)
                e = jnp.exp2(jnp.abs(s) * SC - lse[x, h:h + 1, qs])
                if diag:
                    e = jnp.where(row <= col, e, 0.0)
                sg = sgn_of(s)
                a = sg * e
                ds = (a * (sg * dp - dsc[h:h + 1, qs])).astype(BF)
                dv = dv + mm(a.astype(BF), doh, NN)
                dk = dk + mm(ds, qh, NN)
                t = mm(ds, km[h, ks, :], TN)
                dq = t if dq is None else dq + t
            dq_acc[qs, :] += dq
            return dk, dv

        def block(j):
            for at, event in events:
                @pl.when(j == at)
                def _():
                    event()

            z = jnp.zeros((bk, 128), F32)
            dk, dv = tile(j, j, z, z, True)
            dk, dv = lax.fori_loop(
                j + 1, n // bk, lambda i, c: tile(j, i, c[0], c[1], False), (dk, dv)
            )
            ks = pl.ds(pl.multiple_of(j * bk, bk), bk)
            gm[1, ks, x * 128:(x + 1) * 128] = (dk * HD ** (-0.5)).astype(BF)
            gm[2, ks, x * 128:(x + 1) * 128] = dv.astype(BF)

        loop(n // bk, block)
        gm[0, :, x * 128:(x + 1) * 128] = (dq_acc[...] * HD ** (-0.5)).astype(BF)

    def flat(ref, cols):
        y = ref[:, :, :, cols]
        return y.reshape(n, y.shape[3])

    def weights(x):
        y = jnp.concatenate([gm[c, :, x * 128:(x + 1) * 128] for c in range(3)], axis=1)
        deep = g_triple.shape[4]

        def tile(i):
            z = mm(flat(full, pl.ds(pl.multiple_of(i * 256, 256), 256)), y, TN).astype(BF)
            for e in range(256 // deep):
                f = i * (256 // deep) + e
                for c in range(3):
                    g_triple[x, f // p.line, f % p.line, c] = z[
                        e * deep:(e + 1) * deep, c * 128:(c + 1) * 128
                    ]

        loop(d // 256, tile)
        totals[x].start()

    schedule = [[] for _ in range(pairs)]
    schedule[0] = [(2, shares[0].spread), (3, shares[1].spread)]
    schedule[-1] = schedule[-1] + [
        (1, shares[2].spread),
        (2, merge_total.halve),
        (3, shares[3].spread),
    ]
    for x in range(pairs):
        attention(x, schedule[x])
        weights(x)
        if x == 0 and pairs > 1:
            continue
    totals[0].halve()

    scatter = Scatter(g, part, in_near, out_far, in_far, sem)

    def back(k):
        def tile(j):
            cols = pl.ds(pl.multiple_of(j * 256, 256), 256)
            z = 0.0
            for c in range(3):
                y = jnp.concatenate(
                    [
                        gm[c, pl.ds(pl.multiple_of((s * CHUNKS + k) * rows, rows), rows), :]
                        for s in range(size)
                    ],
                    axis=0,
                )
                z = z + mm(y, w[c, cols, :], NT)
            for s in range(size):
                part[s, k, :, cols] = z[s * rows:(s + 1) * rows].astype(BF)

        loop(d // 256, tile)
        scatter.send(k)

    loop(CHUNKS, back)
    loop(CHUNKS, scatter.combine)
    for x in range(1, pairs):
        totals[x].halve()
    merge_share.start(merge_total.settle())
    triples[0].start(totals[0].settle())
    small[...] = small_in[...]
    units = bias_in.shape[1]
    small[6:7, :units] = bias_in[0:1, :]
    for c in range(3):
        small[7:8, c * width:(c + 1) * width] = col_sum(gm[c].astype(F32))
    span = lambda k: pl.ds(pl.multiple_of(k * rows, rows), rows)

    def pull(k):
        gf = scatter.final(k)
        unit, inverse = norm_stats(tok[span(k), :].astype(F32))
        gtok[span(k), :] = gres[span(k), :] + norm_pull(gf, unit, inverse, gain[...])
        small[0:1, :] += col_sum(gf * unit)
        small[1:2, :] += col_sum(gf)

    loop(CHUNKS, pull)
    group_sum = Everyone("tensor", size, t_buf, t_sems)
    group_sum.start(small[...])
    merge_share.spread()
    for x in range(1, pairs):
        triples[x].start(totals[x].settle())
    total = group_sum.finish()
    keep = lax.broadcasted_iota(jnp.int32, (8, 1), 0) < 6
    all_sum = Everyone("dp", count, d_buf, d_sems)
    all_sum.start(jnp.where(keep, total, small[...]))
    triples[0].spread()
    for x in range(1, pairs):
        triples[x].spread()
    small[...] = all_sum.finish()
    for share in shares + [merge_share] + triples:
        share.finish()
    merge_total.drain()
    for t in totals:
        t.drain()
    loop(CHUNKS, scatter.drain)


def late(size, count, mixed, att, gatt, lse, full, w, tokens, gres, gain, p_down, p_up, g_merge,
         small_in, bias_in):
    rows, d = tokens.shape
    n, width = att.shape
    r = rows // CHUNKS
    line = count // 2
    pairs = width // 128
    bk = min(512, n)
    shape = jax.ShapeDtypeStruct
    piece = d // count
    vm = pltpu.VMEM
    dma = pltpu.SemaphoreType.DMA
    deep = g_merge.shape[2]
    units = bias_in.shape[1]
    return pl.pallas_call(
        functools.partial(late_kernel, size, count, bk),
        out_shape=(
            shape((rows, d), F32),
            shape((2, 2, line) + p_down.shape[1:], BF),
            shape((2, 2, line) + p_up.shape[1:], BF),
            shape(g_merge.shape, BF),
            shape((pairs, 2, line, 3, piece, 128), BF),
            shape((8, d), F32),
        ),
        in_specs=[VMEM_SPEC] * 14,
        out_specs=(VMEM_SPEC,) * 6,
        scratch_shapes=[vm((2, n, 128), BF)] * 3
        + [vm((8, n), F32), vm((n, 128), F32), vm((3, n, width), BF)]
        + [vm((pairs, 2, line, 3, piece, 128), BF)]
        + scatter_scratch(size, r, d)
        + [sems(size)]
        + total_scratch(line, (deep, d))
        + [vm((pairs, line, 3, piece, 128), BF)] * 2
        + [vm((pairs, line - 1, 3, piece, 128), BF), dma((pairs, 2, line)), dma((5 + pairs, 2, line))]
        + [vm((size, 8, d), F32), dma((2, size)), vm((count, 8, d), F32), dma((2, count))],
        compiler_params=pltpu.CompilerParams(
            collective_id=3, has_side_effects=True, vmem_limit_bytes=63 << 20
        ),
        name="late",
    )(mixed, att, gatt, lse, full, w, tokens, gres, gain, p_down, p_up, g_merge, small_in, bias_in)


def on_device(
    tokens,
    first_gain,
    first_shift,
    triple_weight,
    triple_bias,
    merge_weight,
    merge_bias,
    second_gain,
    second_shift,
    up_weight,
    up_bias,
    down_weight,
    down_bias,
    lengths,
    cotangent,
):
    size = lax.axis_size("tensor")
    count = lax.axis_size("dp")
    row_count, d = tokens.shape
    rows = row_count // CHUNKS
    width = triple_weight.shape[2]
    units = up_weight.shape[1]
    n = row_count * size
    fused = units % (64 * count) == 0 and width % (8 * count) == 0 and 3 * width <= d and units <= d
    count = count if fused else 0
    line = lambda v: v.reshape(1, -1)
    w = jnp.transpose(triple_weight, (1, 0, 2))
    full, mixed, top = project(
        size, lengths, tokens, cotangent, line(first_gain), line(first_shift), w, line(triple_bias)
    )
    mixed = mixed.reshape(n, 3 * width)
    every_top = lax.all_gather(top, "tensor", axis=0, tiled=True).reshape(size, CHUNKS, rows, d)
    attended, log_total = attend_fwd(mixed, lengths)
    blocks = lambda x: x.reshape(size, CHUNKS, rows, x.shape[-1])
    gatt, gres, resid, pout, g_up, g_down, g_merge, small_b, bias_b, *pieces = middle(
        size, count, lengths, blocks(attended), tokens, every_top, merge_weight, line(merge_bias),
        line(second_gain), line(second_shift), up_weight, line(up_bias), down_weight,
    )
    branch = lax.psum_scatter(pout.reshape(n, d), "tensor", scatter_dimension=0, tiled=True)
    gatt = gatt.reshape(n, width)
    if fused:
        gtok, down, up, merge, triple, small = late(
            size, count, mixed, attended, gatt, log_total, full, w, tokens, gres, line(first_gain),
            pieces[0], pieces[1], g_merge, small_b, bias_b,
        )
        down = down.reshape(units, d).astype(F32)
        up = up.reshape(d, units).astype(F32)
        merge = merge.reshape(width, d).astype(F32)
        triple = jnp.transpose(triple, (1, 2, 4, 3, 0, 5)).reshape(d, 3, width).astype(F32)
        triple_b, up_b = small[7, :3 * width].reshape(3, width), small[6, :units]
    else:
        dq, dk, dv = attend_bwd(mixed, attended, log_total, gatt)
        gtok, g_triple, small_c, bias_c = tail(
            size, blocks(dq), blocks(dk), blocks(dv), full, w, tokens, gres, line(first_gain)
        )
        merge, up, down, triple = lax.psum((g_merge, g_up, g_down, g_triple), "dp")
        triple_b, up_b = lax.psum((bias_c[0], bias_b[0]), "dp")
        small = lax.psum(small_b + small_c, ("dp", "tensor"))
        triple = jnp.transpose(triple, (1, 0, 2)).astype(F32)
        triple_b = triple_b.reshape(3, width)
        merge, up, down = merge.astype(F32), up.astype(F32), down.astype(F32)
    output = (resid + branch.astype(F32) + down_bias).astype(BF)
    return (
        output,
        gtok,
        small[0],
        small[1],
        triple,
        triple_b,
        merge,
        small[2],
        small[3],
        small[4],
        up,
        up_b,
        down,
        small[5],
    )


def solution(mesh):
    in_specs = (
        P(("dp", "tensor"), None),
        P(),
        P(),
        P(None, None, "tensor"),
        P(None, "tensor"),
        P("tensor", None),
        P(),
        P(),
        P(),
        P(None, "tensor"),
        P("tensor"),
        P("tensor", None),
        P(),
        P("dp"),
        P(("dp", "tensor"), None),
    )
    out_specs = (
        P(("dp", "tensor"), None),
        P(("dp", "tensor"), None),
        P(),
        P(),
        P(None, None, "tensor"),
        P(None, "tensor"),
        P("tensor", None),
        P(),
        P(),
        P(),
        P(None, "tensor"),
        P("tensor"),
        P("tensor", None),
        P(),
    )
    return jax.shard_map(
        on_device, mesh=mesh, in_specs=in_specs, out_specs=out_specs, check_vma=False
    )
```

time: 1350 us -> 385 us (0.29); the launches traced: 1340 us -> 385 us
  waiting for transfers between devices: 713 us -> 0.04 us
  Pallas kernels: 0 us -> 337 us
  matrix products: 320 us -> 0 us
  other arithmetic: 142 us -> 13.4 us
  blocking collectives: 61.1 us -> 0 us
  local copies, waits for them, and re-layouts: 75 us -> 19.2 us
    psum x1 -> x0, waiting for transfers between devices: 355 us -> none  [on_device(): lax.psum((grad_triple_weight, grad_triple_bias, grad_merge_weight, grad_u...]
    pallas_call x0 -> x4, Pallas kernels: none -> 337 us  [the longest x1 144 us: late(): pl.pallas_call(functools.partial(late_kernel, size, count, bk), out_shape...]
    dot_general x40 -> x0, matrix products: 320 us -> none  [the longest x4 81.7 us: one_block(): jnp.einsum('qhd,khd->hqk', grad_block, value_slot, preferred_element_type...]
    reduce_scatter x4 -> x1, waiting for transfers between devices: 231 us -> 0.01 us  [on_device(): lax.psum_scatter(pout.reshape(n, d), 'tensor', scatter_dimension=0, tiled...]
    all_gather x4 -> x1, waiting for transfers between devices: 127 us -> 0.01 us  [on_device(): lax.all_gather(top, 'tensor', axis=0, tiled=True)]
    psum x2 -> x0, blocking collectives: 61.1 us -> none  [the longest x1 43.4 us: on_device(): lax.psum((grad_first_gain, grad_first_shift, jnp.sum(grad_residual, axis=...]
    convert_element_type x9 -> x4, other arithmetic: 70.7 us -> 13.4 us  [the longest x1 6.81 us: on_device(): down = down.reshape(units, d).astype(F32)]
    reduce_sum x12 -> x0, other arithmetic: 37.9 us -> none  [the longest x4 19.6 us: one_block(): row_total = jnp.sum(exponent, axis=-1, keepdims=True)]
  transfers between devices with their start and end apart: 9 -> 2, of which waited for: 9 -> 0; matrix products, arithmetic and copies ran while one was open for 4% -> 5% of each run, Pallas kernels for 0% -> 46%
where the time goes in v1:
time: 385 us
  Pallas kernels  337 us (88%)
  local copies, waits for them, and re-layouts  19.2 us (5%)
  between operations  14.8 us (4%)
  other arithmetic  13.4 us (3%)
    pallas_call x1, Pallas kernels, late(): pl.pallas_call(functools.partial(late_kernel, size, count, bk), out_shape...  144 us
    pallas_call x1, Pallas kernels, middle(): pl.pallas_call(functools.partial(middle_kernel, size, count), out_shape=o...  131 us
    pallas_call x1, Pallas kernels, attend_fwd(): pl.pallas_call(functools.partial(fwd_kernel, bq, bk), grid=(pairs,), out_...  34.3 us
    pallas_call x1, Pallas kernels, project(): pl.pallas_call(functools.partial(project_kernel, size), out_shape=(jax.Sh...  27.9 us
    unnamed x30, local copies, waits for them, and re-layouts  11.9 us
  transfers between devices with their start and end apart: 2, of which 0 were waited for; matrix products, arithmetic and copies ran while one was open for 5% of the time, Pallas kernels for 46%

profile of v1, /device:TPU:24, one launch (start us, length us, event | category | flops | bytes accessed | tf_op | source)
XLA Modules:
  0.0 384.9 jit_solution(329303650308257192)
XLA Ops:
  7.2 0.0 all-gather.2.cloned.1.call-start
  7.9 0.7 copy.30
  8.6 0.0 copy-start
  8.6 1.2 copy-done
  9.8 0.0 copy-start.1
  9.8 1.4 copy-done.1
  11.2 0.0 copy-start.6
  11.2 1.2 copy-done.6
  12.4 0.0 copy-start.8
  12.4 0.7 copy-done.8
  13.1 0.0 copy-start.9
  13.1 0.7 copy-done.9
  13.8 27.9 %project.1 = (bf16[4,4,128,1024]{3,2,1,0:T(8,128)(2,1)S(1)}, bf16[4,4,128,768]{3,2,1,0:T(8,128)(2,1)S(1)}, bf16[512,1024]{1,0:T(8,128)(2,1)S(1)}) custom-call(s32[1]{0:T(128)S(6)} %copy.32.length.len_ref, bf16[512,1024]{1,0:T(8,128)(2,1)S(1)} %copy-done, bf16[512,1024]{1,0:T(8,128)(2,1)S(1)} %copy-done.6, f32[1,1024]{1,0:T(1,128)S(1)} %bitcast.43, ...), custom_call_target="tpu_custom_call" | custom-call | tf_op jit(solution)/shard_map/project/pallas_call | solution.py:549
  41.7 0.0 copy-start.2
  41.7 2.0 copy-done.2
  43.7 0.0 copy-start.5
  43.7 1.0 copy-done.5
  44.7 0.0 copy-start.4
  44.7 0.0 all-gather.2.cloned.1.call-update
  44.7 0.0 reduce-scatter.2.cloned.1.call-start
  44.8 34.3 %attend_fwd.1 = (bf16[2048,256]{1,0:T(8,128)(2,1)S(1)}, f32[2,8,2048]{2,1,0:T(8,128)S(1)}) custom-call(s32[1]{0:T(128)S(6)} %copy.32.length.len_ref, bf16[2048,768]{1,0:T(8,128)(2,1)S(1)} %bitcast.38, bf16[2048,768]{1,0:T(8,128)(2,1)S(1)} %bitcast.39, bf16[2048,768]{1,0:T(8,128)(2,1)S(1)} %bitcast.40), custom_call_target="tpu_custom_call" | custom-call | flops 4294967296 | bytes 4194304 | tf_op jit(solution)/shard_map/attend_fwd/pallas_call | solution.py:108
  79.1 0.0 copy-done.4
  79.1 0.0 copy-start.3
  79.1 1.0 copy-done.3
  80.1 0.0 copy-start.7
  80.1 0.7 copy-done.7
  80.7 0.0 all-gather.2.cloned.1.call-done
  80.7 130.9 %middle.1 = (bf16[4,4,128,256]{3,2,1,0:T(8,128)(2,1)}, f32[512,1024]{1,0:T(8,128)}, f32[512,1024]{1,0:T(8,128)}, bf16[4,4,128,1024]{3,2,1,0:T(8,128)(2,1)}, bf16...) custom-call(s32[1]{0:T(128)S(6)} %copy.32.length.len_ref, ...), custom_call_target="tpu_custom_call" | custom-call | tf_op jit(solution)/shard_map/middle/pallas_call | solution.py:779
  211.6 0.0 reduce-scatter.2.cloned.1.call-update
  211.6 144.2 %late.1 = (f32[512,1024]{1,0:T(8,128)}, bf16[2,2,4,64,1024]{4,3,2,1,0:T(8,128)(2,1)}, bf16[2,2,4,64,1024]{4,3,2,1,0:T(8,128)(2,1)}, bf16[2,4,32,1024]{3,2,1,0:T(...) custom-call(bf16[2048,768]{1,0:T(8,128)(2,1)} %bitcast.41, bf16[2048,256]{1,0:T(8,128)(2,1)} %copy-done.3, ...), custom_call_target="tpu_custom_call" | custom-call | tf_op jit(solution)/shard_map/late/pallas_call | solution.py:1111
  355.9 1.8 convert_bitcast_fusion
  357.7 2.5 copy.29
  360.1 0.0 copy-start.12
  360.1 3.6 reshape.90
  363.8 0.0 copy-done.12
  363.8 0.6 reshape_squeeze.3
  364.4 0.6 fusion
  365.0 2.1 bitcast_convert_fusion.2
  367.2 0.0 copy-start.10
  367.2 0.0 copy-start.13
  367.2 6.8 %bitcast_convert_fusion = (f32[1024,1024]{1,0:T(8,128)}, f32[1024,1024]{1,0:T(8,128)}) fusion(bf16[2,2,4,64,1024]{4,3,2,1,0:T(8,128)(2,1)} %get-tuple-element.53, bf16[2,2,4,64,1024]{4,3,2,1,0:T(8,128)(2,1)} %get-tuple-element.52), kind=kLoop, calls=%fused_computation.1 | loop fusion | flops 2097152 | bytes 12582912 | tf_op jit(solution)/shard_map/convert_element_type | solution.py:1185
  374.0 0.0 reduce-scatter.2.cloned.1.call-done
  374.0 0.0 copy-done.10
  374.0 0.0 copy-done.13
  374.0 0.0 copy-start.11
  374.0 2.7 add_convert_fusion
  376.7 0.0 copy-done.11
  376.7 1.3 copy.33
  (1 shorter events, 0.0 us)
Async XLA Ops:
  7.2 73.5 %all-gather.2.cloned.1.call-start = ((), (), s32[]{:S(2)}) async-start(), calls=%async_computation.1 | async-start | bytes 5242880 | tf_op jit(solution)/shard_map/all_gather | solution.py:1171
  8.6 1.2 copy-start
  9.8 1.4 copy-start.1
  11.2 1.2 copy-start.6
  12.4 0.7 copy-start.8
  13.1 0.7 copy-start.9
  41.7 2.0 copy-start.2
  43.7 1.0 copy-start.5
  44.7 34.4 %copy-start.4 = (bf16[4,4,128,768]{3,2,1,0:T(8,128)(2,1)}, bf16[4,4,128,768]{3,2,1,0:T(8,128)(2,1)S(1)}, u32[]{:S(2)}) copy-start(bf16[4,4,128,768]{3,2,1,0:T(8,128)(2,1)S(1)} %get-tuple-element.34) | copy-start | bytes 9437188
  44.7 329.3 %reduce-scatter.2.cloned.1.call-start = ((), (), s32[]{:S(2)}) async-start(), calls=%async_computation.2 | async-start | bytes 5242880 | tf_op jit(solution)/shard_map/reduce_scatter | solution.py:1178
  79.1 1.0 copy-start.3
  80.1 0.7 copy-start.7
  360.1 3.6 copy-start.12
  367.2 6.8 %copy-start.10 = (f32[512,1024]{1,0:T(8,128)S(1)}, f32[512,1024]{1,0:T(8,128)}, u32[]{:S(2)}) copy-start(f32[512,1024]{1,0:T(8,128)} %get-tuple-element.37) | copy-start | bytes 6291460
  367.2 6.8 %copy-start.13 = (f32[1024]{0:T(1024)S(1)}, f32[1024]{0:T(1024)}, u32[]{:S(2)}) copy-start(f32[1024]{0:T(1024)} %param.27) | copy-start | bytes 12292
  374.0 2.7 copy-start.11
Sparse Core Ops, SparseCore 0:
  44.8 35.1 all-gather.1
  211.8 44.3 reduce-scatter.1

commit v2 on v1

--- a/solution.py
+++ b/solution.py
@@ -23,99 +23,6 @@
 
 def sgn_of(s):
     return jnp.minimum(jnp.maximum(s * BIG, -1.0), 1.0)
-
-
-def fwd_kernel(bq, bk, len_ref, q_ref, k_ref, v_ref, o_ref, lse_ref, s_sc, v0_sc, v1_sc):
-    n = q_ref.shape[0]
-    lane = lax.broadcasted_iota(jnp.int32, (1, 128), 1)
-    hm = [lane < HD, lane >= HD]
-    v_sc = [v0_sc, v1_sc]
-    for h in range(2):
-        v_sc[h][...] = jnp.where(hm[h], v_ref[...], jnp.zeros_like(v_ref))
-    length = len_ref[0]
-    row = lax.broadcasted_iota(jnp.int32, (bq, bk), 0)
-    col = lax.broadcasted_iota(jnp.int32, (bq, bk), 1)
-
-    def fold(x, op):
-        r = x[:, :128]
-        for c in range(1, bk // 128):
-            r = op(r, x[:, c * 128:(c + 1) * 128])
-        return r
-
-    def qblock(i, _):
-        q0 = pl.multiple_of(i * bq, bq)
-        qb = q_ref[pl.ds(q0, bq), :]
-        qh = [jnp.where(hm[h], qb, jnp.zeros_like(qb)) for h in range(2)]
-        nfull = q0 // bk
-
-        def p1(j, mx):
-            kb = k_ref[pl.ds(pl.multiple_of(j * bk, bk), bk), :]
-            out = []
-            for h in range(2):
-                s = mm(qh[h], kb, NT)
-                s_sc[h, j] = s
-                out.append(jnp.maximum(mx[h], fold(jnp.abs(s), jnp.maximum)))
-            return tuple(out)
-
-        zero = jnp.zeros((bq, 128), jnp.float32)
-        mx = lax.fori_loop(0, nfull, p1, (zero, zero))
-        kb = k_ref[pl.ds(pl.multiple_of(nfull * bk, bk), bk), :]
-        mask = (col + nfull * bk) <= (row + q0)
-        mrow = []
-        for h in range(2):
-            s = mm(qh[h], kb, NT)
-            s_sc[h, nfull] = jnp.where(mask, s, 0.0)
-            m = jnp.maximum(mx[h], fold(jnp.where(mask, jnp.abs(s), 0.0), jnp.maximum))
-            mrow.append(jnp.max(m, axis=1, keepdims=True) * SC)
-
-        def p2(j, carry):
-            new = []
-            for h in range(2):
-                acc, ls = carry[h]
-                s = s_sc[h, j]
-                p = jnp.exp2(jnp.abs(s) * SC - mrow[h])
-                ls = ls + fold(p, jnp.add)
-                w = (sgn_of(s) * p).astype(jnp.bfloat16)
-                acc = acc + mm(w, v_sc[h][pl.ds(pl.multiple_of(j * bk, bk), bk), :], NN)
-                new.append((acc, ls))
-            return tuple(new)
-
-        carry = lax.fori_loop(0, nfull, p2, ((zero, zero), (zero, zero)))
-        outs = []
-        for h in range(2):
-            acc, ls = carry[h]
-            s = s_sc[h, nfull]
-            p = jnp.where(mask, jnp.exp2(jnp.abs(s) * SC - mrow[h]), 0.0)
-            ls = ls + fold(p, jnp.add)
-            w = (sgn_of(s) * p).astype(jnp.bfloat16)
-            acc = acc + mm(w, v_sc[h][pl.ds(pl.multiple_of(nfull * bk, bk), bk), :], NN)
-            tot = jnp.sum(ls, axis=1, keepdims=True)
-            outs.append(acc / tot)
-            lse = jnp.broadcast_to(mrow[h] + jnp.log(tot) * LOG2E, (bq, 128))
-            lse_ref[0, h:h + 1, pl.ds(q0, bq)] = jnp.transpose(lse)[0:1, :]
-        live = (lax.broadcasted_iota(jnp.int32, (bq, 1), 0) + q0) < length
-        o_ref[pl.ds(q0, bq), :] = jnp.where(live, outs[0] + outs[1], 0.0).astype(jnp.bfloat16)
-        return 0
-
-    lax.fori_loop(0, n // bq, qblock, 0)
-
-
-def attend_fwd(mixed, lengths, bq=512, bk=512):
-    n = mixed.shape[0]
-    width = mixed.shape[1] // 3
-    pairs = width // 128
-    spec = lambda off: pl.BlockSpec((n, 128), lambda p, off=off: (0, off + p))
-    return pl.pallas_call(
-        functools.partial(fwd_kernel, bq, bk),
-        grid=(pairs,),
-        out_shape=(jax.ShapeDtypeStruct((n, width), jnp.bfloat16), jax.ShapeDtypeStruct((pairs, 8, n), jnp.float32)),
-        in_specs=[pl.BlockSpec(memory_space=pltpu.SMEM), spec(0), spec(pairs), spec(2 * pairs)],
-        out_specs=(pl.BlockSpec((n, 128), lambda p: (0, p)), pl.BlockSpec((1, 8, n), lambda p: (p, 0, 0))),
-        scratch_shapes=[pltpu.VMEM((2, n // bk, bq, bk), jnp.float32)] + [pltpu.VMEM((n, 128), jnp.bfloat16)] * 2,
-        compiler_params=pltpu.CompilerParams(vmem_limit_bytes=48 << 20),
-        cost_estimate=pl.CostEstimate(flops=4 * n * n * width, bytes_accessed=8 * n * width, transcendentals=n * n * width // 128),
-        name="attend_fwd",
-    )(lengths, mixed, mixed, mixed)
 
 
 def bwd_kernel(bq, bk, q_ref, k_ref, v_ref, do_ref, o_ref, lse_ref, dq_ref, dk_ref, dv_ref,
@@ -387,9 +294,8 @@
 
 
 class Total:
-    def __init__(self, place, src, near, half, far, out, sem):
-        self.p, self.src, self.near = place, src, near
-        self.half, self.far, self.out, self.sem = half, far, out, sem
+    def __init__(self, place, src, near, far, sem):
+        self.p, self.src, self.near, self.far, self.sem = place, src, near, far, sem
 
     def pair(self):
         p, sem = self.p, self.sem
@@ -401,67 +307,74 @@
         p, sem = self.p, self.sem
         back = p.line - off
         return remote(
-            self.half.at[p.step(off)], self.far.at[back - 1], sem.at[0, off], sem.at[1, back],
+            self.near.at[p.step(off)], self.far.at[back - 1], sem.at[0, off], sem.at[1, back],
             "dp", p.peer(off),
         )
 
     def start(self):
         self.pair().start()
 
-    def halve(self):
+    def add(self):
         self.pair().wait_recv()
         for j in range(self.p.line):
             total = self.src[self.p.side, j].astype(F32) + self.near[j].astype(F32)
-            self.half[j] = total.astype(BF)
+            self.near[j] = total.astype(BF)
+
+    def scatter(self):
         for off in range(1, self.p.line):
             self.piece(off).start()
 
+    def halve(self):
+        self.add()
+        self.scatter()
+
     def settle(self):
         p, sem = self.p, self.sem
-        total = self.src[p.side, p.row].astype(F32) + self.near[p.row].astype(F32)
+        total = self.near[p.row].astype(F32)
         for off in range(1, p.line):
             remote(
-                self.half.at[p.row], self.far.at[off - 1], sem.at[0, off], sem.at[1, off],
+                self.near.at[p.row], self.far.at[off - 1], sem.at[0, off], sem.at[1, off],
                 "dp", p.peer(off),
             ).wait_recv()
             total = total + self.far[off - 1].astype(F32)
         return total.astype(BF)
 
-    def drain(self):
-        self.pair().wait_send()
-        for off in range(1, self.p.line):
+    def drain(self, pair=True, pieces=True):
+        if pair:
+            self.pair().wait_send()
+        for off in range(1, self.p.line) if pieces else ():
             self.piece(off).wait_send()
 
 
 class Share:
-    def __init__(self, place, out, sem):
-        self.p, self.out, self.sem = place, out, sem
+    def __init__(self, place, piece, half, sem):
+        self.p, self.piece_at, self.half_at, self.sem = place, piece, half, sem
 
     def piece(self, off):
         p, sem = self.p, self.sem
-        here = self.out.at[p.side, p.row]
+        here = self.piece_at(p.side, p.row)
         return remote(here, here, sem.at[0, off], sem.at[1, p.line - off], "dp", p.peer(off))
 
     def half(self):
         p, sem = self.p, self.sem
-        here = self.out.at[p.side]
+        here = self.half_at(p.side)
         return remote(here, here, sem.at[0, 0], sem.at[1, 0], "dp", p.partner)
 
     def start(self, piece):
-        self.out[self.p.side, self.p.row] = piece
+        self.piece_at(self.p.side, self.p.row)[...] = piece
         for off in range(1, self.p.line):
             self.piece(off).start()
 
     def spread(self):
         p, sem = self.p, self.sem
         for off in range(1, p.line):
-            here = self.out.at[p.side, p.step(off)]
+            here = self.piece_at(p.side, p.step(off))
             remote(here, here, sem.at[0, off], sem.at[1, off], "dp", p.peer(off)).wait_recv()
         self.half().start()
 
     def finish(self):
         p, sem = self.p, self.sem
-        there = self.out.at[1 - p.side]
+        there = self.half_at(1 - p.side)
         remote(there, there, sem.at[0, 0], sem.at[1, 0], "dp", p.partner).wait_recv()
         for off in range(1, p.line):
             self.piece(off).wait_send()
@@ -469,10 +382,26 @@
 
 
 def total_scratch(line, block):
-    return [pltpu.VMEM((line,) + block, BF)] * 2 + [
+    return [
+        pltpu.VMEM((line,) + block, BF),
         pltpu.VMEM((line - 1,) + block, BF),
         pltpu.SemaphoreType.DMA((2, line)),
     ]
+
+
+ANY_SPEC = pl.BlockSpec(memory_space=pl.ANY)
+
+
+class Move:
+    def __init__(self, src, dst, sem):
+        self.copy = pltpu.make_async_copy(src, dst, sem)
+
+    def start(self):
+        self.copy.start()
+        return self
+
+    def wait(self):
+        self.copy.wait()
 
 
 def norm_stats(x):
@@ -501,10 +430,11 @@
     pl.semaphore_wait(barrier, group.greet(barrier))
 
 
-def project_kernel(size, length, tok, cot, gain, shift, w, b, full, mixed, top, sem):
+def project_kernel(size, tok, gain, shift, w_hbm, b, full_hbm, mixed_hbm, full, mixed, w, sem, w_sem, out_sem):
     g = Group(size)
     rows = tok.shape[0] // CHUNKS
     width = w.shape[2]
+    load = Move(w_hbm, w, w_sem).start()
     enter_kernel(g)
     gather = Gather(g, full, sem)
 
@@ -514,22 +444,24 @@
         gather.send(k)
 
     loop(CHUNKS, norm)
-
-    def mask(k):
-        span = pl.ds(pl.multiple_of(k * rows, rows), rows)
-        row = lax.broadcasted_iota(jnp.int32, (rows, 1), 0) + (g.me * CHUNKS + k) * rows
-        top[span, :] = jnp.where(row < length[0], cot[span, :].astype(F32), 0.0).astype(BF)
-
-    loop(CHUNKS, mask)
+    load.wait()
+
+    def stores(k):
+        return (
+            Move(full.at[:, k], full_hbm.at[:, k], out_sem.at[0, k]),
+            Move(mixed.at[:, k], mixed_hbm.at[:, k], out_sem.at[1, k]),
+        )
 
     def multiply(k):
         gather.wait(k)
         x = rows_of(full, k)
         for c in range(3):
             cols = slice(c * width, (c + 1) * width)
-            y = (mm(x, w[c], NN) + b[:, cols]).astype(BF)
+            y = (mm(x, w[c], NN) + b[c:c + 1, :]).astype(BF)
             for s in range(size):
                 mixed[s, k, :, cols] = y[s * rows:(s + 1) * rows]
+        for store in stores(k):
+            store.start()
 
     def body(k):
         gather.forward(k)
@@ -540,82 +472,206 @@
 
     loop(CHUNKS, body)
     multiply(CHUNKS - 1)
-    loop(CHUNKS, gather.drain)
-
-
-def project(size, lengths, tokens, cotangent, gain, shift, w, b):
+
+    def drain(k):
+        gather.drain(k)
+        for store in stores(k):
+            store.wait()
+
+    loop(CHUNKS, drain)
+
+
+def project(size, tokens, gain, shift, w, b):
     rows, d = tokens.shape
     r = rows // CHUNKS
+    shapes = ((size, CHUNKS, r, d), (size, CHUNKS, r, 3 * w.shape[2]))
+    dma = pltpu.SemaphoreType.DMA
     return pl.pallas_call(
         functools.partial(project_kernel, size),
-        out_shape=(
-            jax.ShapeDtypeStruct((size, CHUNKS, r, d), BF),
-            jax.ShapeDtypeStruct((size, CHUNKS, r, 3 * w.shape[2]), BF),
-            jax.ShapeDtypeStruct((rows, d), BF),
-        ),
-        in_specs=[SMEM_SPEC] + [VMEM_SPEC] * 6,
-        out_specs=(VMEM_SPEC,) * 3,
-        scratch_shapes=[sems(size)],
+        out_shape=tuple(jax.ShapeDtypeStruct(x, BF) for x in shapes),
+        in_specs=[VMEM_SPEC] * 3 + [ANY_SPEC, VMEM_SPEC],
+        out_specs=(ANY_SPEC,) * 2,
+        scratch_shapes=[pltpu.VMEM(x, BF) for x in shapes]
+        + [pltpu.VMEM(w.shape, BF), sems(size), dma, dma((2, CHUNKS))],
         compiler_params=pltpu.CompilerParams(
-            collective_id=0, has_side_effects=True, vmem_limit_bytes=40 << 20
+            collective_id=0, has_side_effects=True, vmem_limit_bytes=63 << 20
         ),
         name="project",
-    )(lengths, tokens, cotangent, gain, shift, w, b)
-
-
-def middle_kernel(
-    size, count, length, att, tok, cot, mw, mb, gain, shift, up, ub, down,
-    gatt, gres, resid, pout, g_up, g_down, g_merge, small, bias, *rest,
+    )(tokens, gain, shift, w, b)
+
+
+def fold(x, op):
+    r = x[:, :128]
+    for c in range(1, x.shape[1] // 128):
+        r = op(r, x[:, c * 128:(c + 1) * 128])
+    return r
+
+
+class Attend:
+    def __init__(self, size, units, length, mixed, out, lse, scores, values):
+        self.size, self.units, self.length = size, units, length
+        self.mixed, self.out, self.lse, self.scores, self.values = mixed, out, lse, scores, values
+        self.width = out.shape[-1]
+        self.pairs = self.width // 128
+        self.block = mixed.shape[0] // size
+        self.rows = self.block // units
+        lane = lax.broadcasted_iota(jnp.int32, (1, 128), 1)
+        self.heads = [lane < HD, lane >= HD]
+
+    def prepare(self):
+        for x in range(self.pairs):
+            for h in range(2):
+                v = self.mixed[:, 2 * self.width + x * 128:2 * self.width + (x + 1) * 128]
+                self.values[2 * x + h] = jnp.where(self.heads[h], v, jnp.zeros_like(v))
+
+    def run(self, u, low, high):
+        def body(i):
+            self.unit(u, i // self.pairs, i % self.pairs)
+
+        loop_range(low * self.pairs, high * self.pairs, body)
+
+    def unit(self, u, s, x):
+        bq, bk = self.rows, self.block
+        lanes = pl.ds(pl.multiple_of(x * 128, 128), 128)
+        k_lanes = pl.ds(pl.multiple_of(self.width + x * 128, 128), 128)
+        k0 = pl.multiple_of(s * bk, bk)
+        q0 = pl.multiple_of(s * bk + u * bq, bq)
+        qb = self.mixed[pl.ds(q0, bq), lanes]
+        qh = [jnp.where(self.heads[h], qb, jnp.zeros_like(qb)) for h in range(2)]
+        edge = (u + 1) * bq
+        row = lax.broadcasted_iota(jnp.int32, (bq, edge), 0) + u * bq
+        mask = lax.broadcasted_iota(jnp.int32, (bq, edge), 1) <= row
+        zero = jnp.zeros((bq, 128), F32)
+
+        def first(j, most):
+            kb = self.mixed[pl.ds(pl.multiple_of(j * bk, bk), bk), k_lanes]
+            new = []
+            for h in range(2):
+                sc = mm(qh[h], kb, NT)
+                self.scores[h, j] = sc
+                new.append(jnp.maximum(most[h], fold(jnp.abs(sc), jnp.maximum)))
+            return tuple(new)
+
+        most = lax.fori_loop(0, s, first, (zero, zero))
+        kb = self.mixed[pl.ds(k0, edge), k_lanes]
+        top, state = [], []
+        for h in range(2):
+            sc = jnp.where(mask, mm(qh[h], kb, NT), 0.0)
+            m = jnp.maximum(most[h], fold(jnp.abs(sc), jnp.maximum))
+            top.append(jnp.max(m, axis=1, keepdims=True) * SC)
+            e = jnp.where(mask, jnp.exp2(jnp.abs(sc) * SC - top[h]), 0.0)
+            w = (sgn_of(sc) * e).astype(BF)
+            state.append((mm(w, self.values[2 * x + h, pl.ds(k0, edge), :], NN), fold(e, jnp.add)))
+
+        def second(j, carry):
+            new = []
+            for h in range(2):
+                acc, total = carry[h]
+                sc = self.scores[h, j]
+                e = jnp.exp2(jnp.abs(sc) * SC - top[h])
+                w = (sgn_of(sc) * e).astype(BF)
+                rows = pl.ds(pl.multiple_of(j * bk, bk), bk)
+                acc = acc + mm(w, self.values[2 * x + h, rows, :], NN)
+                new.append((acc, total + fold(e, jnp.add)))
+            return tuple(new)
+
+        state = lax.fori_loop(0, s, second, tuple(state))
+        result = 0.0
+        for h in range(2):
+            total = jnp.sum(state[h][1], axis=1, keepdims=True)
+            result = result + state[h][0] / total
+            log_total = jnp.broadcast_to(top[h] + jnp.log(total) * LOG2E, (bq, 128))
+            self.lse[x, h:h + 1, pl.ds(q0, bq)] = jnp.transpose(log_total)[0:1, :]
+        live = (lax.broadcasted_iota(jnp.int32, (bq, 1), 0) + q0) < self.length[0]
+        self.out[pl.ds(q0, bq), lanes] = jnp.where(live, result, 0.0).astype(BF)
+
+
+def core_kernel(
+    size, count, length, mb, gain, shift, ub, mixed_hbm, tok_hbm, cot_hbm, mw_hbm, up_hbm, down_hbm,
+    att, lse, gatt, gres_hbm, resid_hbm, pout_hbm, g_merge, small, bias, *rest,
 ):
-    pieces, rest = (rest[:2], rest[2:]) if count else ((), rest)
-    part, in_near, out_far, in_far, full, gfull, hid, gb, sem1, sem2, sem3, sem4 = rest[:12]
-    rest = rest[12:]
+    if count:
+        (pieces, held, rest) = (rest[:3], rest[3], rest[4:])
+    else:
+        (g_up, g_down, rest) = (rest[0], rest[1], rest[2:])
+    (
+        mixed, tok, cot, mw, up, down, scores, values, resid, gres, pout, part, in_near, out_far, in_far,
+        full, hid, gb, sem1, sem2, sem3, sem4, sem5, load_sem, cot_sem, out_sem, free,
+    ) = rest[:27]
+    rest = rest[27:]
     g = Group(size)
     rows, d = tok.shape[0] // CHUNKS, tok.shape[1]
-    units = up.shape[1]
-    step = min(256, units)
+    width, units = mw.shape[0], up.shape[1]
+    step = min(512, units)
     p = Place(count) if count else None
+    span = lambda k: pl.ds(pl.multiple_of(k * rows, rows), rows)
+    loads = [
+        Move(src, dst, load_sem.at[i]).start()
+        for i, (src, dst) in enumerate(
+            ((mixed_hbm, mixed), (tok_hbm, tok), (mw_hbm, mw), (up_hbm, up), (down_hbm, down))
+        )
+    ]
+    own = lambda k: Move(cot_hbm.at[k], cot.at[g.me, k], cot_sem.at[k])
+    loop(CHUNKS, lambda k: own(k).start())
     barrier = pltpu.get_barrier_semaphore()
     pl.semaphore_wait(barrier, g.greet(barrier) + (p.greet(barrier) if count else 0))
+    tops = Gather(g, cot, sem5)
     first = Scatter(g, part, in_near, out_far, in_far, sem1)
     spread = Gather(g, full, sem2)
     second = Scatter(g, part, in_near, out_far, in_far, sem3)
+    if units == d:
+        gfull = hid
+    else:
+        gfull, rest = rest[0], rest[1:]
     back = Gather(g, gfull, sem4)
-    span = lambda k: pl.ds(pl.multiple_of(k * rows, rows), rows)
     sums = []
-    for ref in (g_down, g_up) if count else ():
-        for h in range(2):
-            near, half, far, sem = rest[:4]
-            rest = rest[4:]
-            sums.append(Total(p, ref.at[h], near, half, far, None, sem))
+    if count:
+        g_up, g_down, rest = rest[0], rest[1], rest[2:]
+        for ref in (g_down, g_up):
+            for h in range(2):
+                near, far, sem = rest[:3]
+                rest = rest[3:]
+                sums.append(Total(p, ref.at[h], near, far, sem))
+
+    def mask(k):
+        own(k).wait()
+        row = lax.broadcasted_iota(jnp.int32, (rows, 1), 0) + (g.me * CHUNKS + k) * rows
+        cot[g.me, k] = jnp.where(row < length[0], cot[g.me, k].astype(F32), 0.0).astype(BF)
+        tops.send(k)
+
+    loop(CHUNKS, mask)
+    attend = Attend(size, 2, length, mixed, att, lse, scores, values)
+    loads[0].wait()
+    attend.prepare()
+
+    def at(s, k):
+        return pl.ds(pl.multiple_of((s * CHUNKS + k) * rows, rows), rows)
 
     def merge(k):
-        y = mm(rows_of(att, k), mw[...], NN).astype(BF)
+        x = jnp.concatenate([att[at(s, k), :] for s in range(size)], axis=0)
+        y = mm(x, mw[...], NN).astype(BF)
         for s in range(size):
             part[s, k] = y[s * rows:(s + 1) * rows]
         first.send(k)
 
-    loop(CHUNKS, merge)
-    loop(CHUNKS, first.combine)
+    def resid_store(k):
+        return Move(resid.at[span(k)], resid_hbm.at[span(k)], out_sem.at[0, k])
 
     def norm(k):
         x = tok[span(k), :].astype(F32) + first.final(k) + mb[...]
         resid[span(k), :] = x
+        resid_store(k).start()
         unit, _ = norm_stats(x)
         full[g.me, k] = (unit * gain[...] + shift[...]).astype(BF)
         spread.send(k)
 
-    loop(CHUNKS, norm)
-    loop(CHUNKS, first.drain)
-    bias[...] = jnp.zeros_like(bias)
-
-    def enter(k):
+    def inner(k):
         spread.forward(k)
         spread.wait(k)
         x = rows_of(full, k)
         top = rows_of(cot, k)
 
-        def inner(j):
+        def tile(j):
             cols = pl.ds(pl.multiple_of(j * step, step), step)
             v = mm(x, up[:, cols], NN) + ub[:, cols]
             gh = mm(top, down[cols, :], NT)
@@ -631,9 +687,29 @@
                 hid[s, k, :, cols] = h[s * rows:(s + 1) * rows]
                 gb[s, k, :, cols] = gv[s * rows:(s + 1) * rows]
 
-        loop(units // step, inner)
-
-    loop(CHUNKS, enter)
+        loop(units // step, tile)
+
+    def pout_store(k):
+        return Move(pout.at[k % 2], pout_hbm.at[:, k], out_sem.at[1, k])
+
+    def leave(k):
+        h, gv = rows_of(hid, k), rows_of(gb, k)
+
+        @pl.when(k >= 2)
+        def _():
+            pout_store(k - 2).wait()
+
+        def tile(j):
+            cols = pl.ds(pl.multiple_of(j * 512, 512), 512)
+            y = mm(h, down[:, cols], NN).astype(BF)
+            z = mm(gv, up[cols, :], NT).astype(BF)
+            for s in range(size):
+                pout[k % 2, s, :, cols] = y[s * rows:(s + 1) * rows]
+                part[s, k, :, cols] = z[s * rows:(s + 1) * rows]
+
+        loop(d // 512, tile)
+        pout_store(k).start()
+        second.send(k)
 
     def flat(ref, cols):
         x = ref[:, :, :, cols]
@@ -655,67 +731,36 @@
 
         return block, extent // tall
 
-    block, blocks = products(g_down, hid, cot, units)
-    if count:
+    def weights(ref, left, right, extent, pair):
+        block, blocks = products(ref, left, right, extent)
+        if not count:
+            loop(blocks, block)
+            return
         for h in range(2):
             loop_range(h * blocks // 2, (h + 1) * blocks // 2, block)
-            sums[h].start()
-    else:
-        loop(blocks, block)
-
-    def leave(k):
-        h, gv = rows_of(hid, k), rows_of(gb, k)
-
-        def outer(j):
-            cols = pl.ds(pl.multiple_of(j * 256, 256), 256)
-            y = mm(h, down[:, cols], NN).astype(BF)
-            z = mm(gv, up[cols, :], NT).astype(BF)
-            for s in range(size):
-                pout[s, k, :, cols] = y[s * rows:(s + 1) * rows]
-                part[s, k, :, cols] = z[s * rows:(s + 1) * rows]
-
-        loop(d // 256, outer)
-        second.send(k)
-
-        @pl.when(k > 0)
-        def _():
-            second.combine(k - 1)
-
-    if count:
-        loop_range(0, 3, leave)
-        sums[0].halve()
-        loop_range(3, CHUNKS, leave)
-    else:
-        loop(CHUNKS, leave)
-    second.combine(CHUNKS - 1)
-    block, blocks = products(g_up, full, gb, d)
-    if count:
-        for h in range(2):
-            loop_range(h * blocks // 2, (h + 1) * blocks // 2, block)
-            sums[2 + h].start()
-        sums[1].halve()
-    else:
-        loop(blocks, block)
-    loop(CHUNKS, spread.drain)
-    small[...] = jnp.zeros_like(small)
+            pair[h].start()
+
+    def gres_store(k):
+        return Move(gres.at[k % 2], gres_hbm.at[span(k)], out_sem.at[2, k])
 
     def pull(k):
         gs = second.final(k)
         unit, inverse = norm_stats(resid[span(k), :])
         top = cot[g.me, k].astype(F32)
         gr = top + norm_pull(gs, unit, inverse, gain[...])
-        gres[span(k), :] = gr
+
+        @pl.when(k >= 2)
+        def _():
+            gres_store(k - 2).wait()
+
+        gres[k % 2] = gr
+        gres_store(k).start()
         gfull[g.me, k] = gr.astype(BF)
         back.send(k)
         small[2:3, :] += col_sum(gr)
         small[3:4, :] += col_sum(gs * unit)
         small[4:5, :] += col_sum(gs)
         small[5:6, :] += col_sum(top)
-
-    loop(CHUNKS, pull)
-    loop(CHUNKS, second.drain)
-    if count:
-        sums[2].halve()
 
     def last(k):
         back.forward(k)
@@ -725,71 +770,125 @@
             row = lax.broadcasted_iota(jnp.int32, (rows, 1), 0) + (s * CHUNKS + k) * rows
             gatt[s, k] = jnp.where(row < length[0], y[s * rows:(s + 1) * rows], 0.0).astype(BF)
 
-    loop(CHUNKS // 2, last)
-    if count:
-        sums[3].halve()
-    loop_range(CHUNKS // 2, CHUNKS, last)
-    block, blocks = products(g_merge, att, gfull, mw.shape[0])
+    def later(*steps):
+        if count:
+            for one in steps:
+                one()
+
+    bias[...] = jnp.zeros_like(bias)
+    small[...] = jnp.zeros_like(small)
+    attend.run(0, 0, size)
+    for load in loads[1:]:
+        load.wait()
+    loop(2, merge)
+    loop(2, first.combine)
+    loop(2, tops.forward)
+    attend.run(1, 0, size - 1)
+    loop_range(2, CHUNKS, tops.forward)
+    loop(2, norm)
+    attend.run(1, size - 1, size)
+    loop_range(2, CHUNKS, merge)
+    loop_range(2, CHUNKS, first.combine)
+    loop(CHUNKS, tops.wait)
+    loop(2, inner)
+    loop(2, first.drain)
+    loop(2, leave)
+    loop_range(2, CHUNKS, norm)
+    loop(2, second.combine)
+    loop_range(2, CHUNKS, first.drain)
+    loop_range(2, CHUNKS, inner)
+    weights(g_down, hid, cot, units, sums[:2])
+    peers = g.greet(free)
+    loop_range(2, CHUNKS, leave)
+    loop_range(2, CHUNKS, second.combine)
+    pl.semaphore_wait(free, peers)
+    loop(2, pull)
+    weights(g_up, full, gb, d, sums[2:])
+    later(lambda: sums[0].halve())
+    loop(CHUNKS, tops.drain)
+    loop(CHUNKS, spread.drain)
+    loop_range(2, CHUNKS, pull)
+    later(lambda: sums[1].halve())
+    loop(2, last)
+    later(lambda: sums[2].halve())
+    loop_range(2, CHUNKS, last)
+    y = mm(att[...], flat(gfull, slice(None)), TN).astype(BF)
     if count:
         deep = g_merge.shape[2]
-        y = mm(flat(att, slice(None)), flat(gfull, slice(None)), TN).astype(BF)
         for f in range(2 * p.line):
             g_merge[f // p.line, f % p.line] = y[f * deep:(f + 1) * deep]
+        for h in range(3):
+            pieces[h][...] = sums[h].settle()
+        sums[3].add()
+        held[...] = sums[3].near[...]
         for h in range(4):
-            pieces[h // 2][h % 2] = sums[h].settle()
-        for h in range(4):
-            sums[h].drain()
+            sums[h].drain(True, h < 3)
     else:
-        loop(blocks, block)
+        g_merge[...] = y
+    loop(CHUNKS, second.drain)
     loop(CHUNKS, back.drain)
-
-
-def middle(size, count, lengths, att, tokens, cot, mw, mb, gain, shift, up, ub, down):
+    loop(CHUNKS, lambda k: resid_store(k).wait())
+    loop_range(2, CHUNKS, lambda k: pout_store(k).wait())
+    loop_range(2, CHUNKS, lambda k: gres_store(k).wait())
+
+
+def core(size, count, lengths, mixed, mb, gain, shift, ub, tokens, cotangent, mw, up, down):
     rows, d = tokens.shape
     r = rows // CHUNKS
+    n = rows * size
     width, units = mw.shape[0], up.shape[1]
+    pairs = width // 128
     shape = jax.ShapeDtypeStruct
-    wide = lambda c: pltpu.VMEM((size, CHUNKS, r, c), BF)
+    dma = pltpu.SemaphoreType.DMA
+    vm = pltpu.VMEM
+    wide = lambda c: vm((size, CHUNKS, r, c), BF)
     line = count // 2
     if count:
-        grads = (
-            shape((2, 2, line, d // (4 * line), units), BF),
-            shape((2, 2, line, units // (4 * line), d), BF),
-            shape((2, line, width // (2 * line), d), BF),
-        )
-        extra = (
-            shape((2, units // (4 * line), d), BF),
-            shape((2, d // (4 * line), units), BF),
-        )
-        scratch = total_scratch(line, (units // (4 * line), d)) * 2
-        scratch += total_scratch(line, (d // (4 * line), units)) * 2
+        blocks = ((2, 2, line, d // (4 * line), units), (2, 2, line, units // (4 * line), d))
+        merge = shape((2, line, width // (2 * line), d), BF)
+        piece = [shape(b[3:], BF) for b in blocks[::-1]]
+        extra = (piece[0], piece[0], piece[1], shape((line,) + blocks[0][3:], BF))
+        scratch = [vm(b, BF) for b in blocks]
+        for b in blocks[::-1]:
+            scratch += total_scratch(line, b[3:]) * 2
     else:
-        grads = (shape((d, units), BF), shape((units, d), BF), shape((width, d), BF))
-        extra, scratch = (), []
+        merge = shape((width, d), BF)
+        extra = (shape((d, units), BF), shape((units, d), BF))
+        scratch = []
+    if units != d:
+        scratch = [wide(d)] + scratch
     outs = (
-        shape((size, CHUNKS, r, width), BF),
-        shape((rows, d), F32),
-        shape((rows, d), F32),
-        shape((size, CHUNKS, r, d), BF),
-        *grads,
-        shape((8, d), F32),
-        shape((8, units), F32),
-        *extra,
+        (shape((n, width), BF), VMEM_SPEC),
+        (shape((pairs, 8, n), F32), VMEM_SPEC),
+        (shape((size, CHUNKS, r, width), BF), VMEM_SPEC),
+        (shape((rows, d), F32), ANY_SPEC),
+        (shape((rows, d), F32), ANY_SPEC),
+        (shape((size, CHUNKS, r, d), BF), ANY_SPEC),
+        (merge, VMEM_SPEC),
+        (shape((8, d), F32), VMEM_SPEC),
+        (shape((8, units), F32), VMEM_SPEC),
+        *((x, VMEM_SPEC) for x in extra),
     )
     return pl.pallas_call(
-        functools.partial(middle_kernel, size, count),
-        out_shape=outs,
-        in_specs=[SMEM_SPEC] + [VMEM_SPEC] * 10,
-        out_specs=(VMEM_SPEC,) * len(outs),
-        scratch_shapes=scatter_scratch(size, r, d)
-        + [wide(d), wide(d), wide(units), wide(units)]
-        + [sems(size)] * 4
+        functools.partial(core_kernel, size, count),
+        out_shape=tuple(x for x, _ in outs),
+        in_specs=[SMEM_SPEC] + [VMEM_SPEC] * 4 + [ANY_SPEC] * 6,
+        out_specs=tuple(x for _, x in outs),
+        scratch_shapes=[
+            vm(mixed.shape, BF), vm((rows, d), BF), wide(d), vm((width, d), BF), vm((d, units), BF), vm((units, d), BF),
+            vm((2, size, rows // 2, rows), F32), vm((2 * pairs, n, 128), BF), vm((rows, d), F32),
+            vm((2, r, d), F32), vm((2, size, r, d), BF),
+        ]
+        + scatter_scratch(size, r, d)
+        + [wide(d), wide(units), wide(units)]
+        + [sems(size)] * 5
+        + [dma((5,)), dma((CHUNKS,)), dma((3, CHUNKS)), pltpu.SemaphoreType.REGULAR]
         + scratch,
         compiler_params=pltpu.CompilerParams(
-            collective_id=1, has_side_effects=True, vmem_limit_bytes=63 << 20
+            collective_id=1, has_side_effects=True, vmem_limit_bytes=64 << 20
         ),
-        name="middle",
-    )(lengths, att, tokens, cot, mw, mb, gain, shift, up, ub, down)
+        name="core",
+    )(lengths, mb, gain, shift, ub, mixed, tokens, cotangent.reshape(CHUNKS, r, d), mw, up, down)
 
 
 def tail_kernel(
@@ -900,12 +999,24 @@
 
 
 def late_kernel(
-    size, count, bk, mixed, att, gatt, lse, full, w, tok, gres, gain, p_down, p_up, g_merge,
-    small_in, bias_in,
-    gtok, o_down, o_up, o_merge, o_triple, small,
-    qm, km, dom, dsc, dq_acc, gm, g_triple, part, in_near, out_far, in_far, sem,
-    m_near, m_half, m_far, m_sem, t_near, t_half, t_far, t_sem, s_sem, t_buf, t_sems, d_buf, d_sems,
+    size, count, bk, gain, db, p_down0, p_down1, p_up0, u_held, g_merge, small_in, bias_in,
+    mixed_hbm, att_hbm, gatt_hbm, lse_hbm, full_hbm, w_hbm, tok_hbm, gres_hbm, resid_hbm, pout_hbm,
+    out, gtok, o_down, o_up, o_merge, o_triple, small,
+    mixed, att, gatt, lse, full, w, tok, gres, resid, pout, load_sem,
+    qm, km, dom, dsc, dq_acc, gm, g_triple, part, in_near, out_far, in_far,
+    in_near2, out_far2, in_far2, sem, sem2, u_far, u_sem,
+    m_near, m_far, m_sem, t_near, t_far, t_sem, s_sem, t_buf, t_sems, d_buf, d_sems,
 ):
+    loads = [
+        Move(src, dst, load_sem.at[i]).start()
+        for i, (src, dst) in enumerate(
+            (
+                (mixed_hbm, mixed), (gatt_hbm, gatt), (att_hbm, att), (lse_hbm, lse),
+                (pout_hbm, pout), (resid_hbm, resid), (full_hbm, full), (w_hbm, w),
+                (tok_hbm, tok), (gres_hbm, gres),
+            )
+        )
+    ]
     g, p = Group(size), Place(count)
     n = mixed.shape[0]
     rows, d = tok.shape[0] // CHUNKS, tok.shape[1]
@@ -922,17 +1033,35 @@
             )
     pl.semaphore_wait(barrier, size + count - 2)
 
-    shares = [Share(p, ref.at[h], s_sem.at[2 * a + h]) for a, ref in enumerate((o_down, o_up)) for h in range(2)]
-    merge_total = Total(p, g_merge, m_near, m_half, m_far, None, m_sem)
-    merge_share = Share(p, o_merge, s_sem.at[4])
-    totals = [
-        Total(p, g_triple.at[x], t_near.at[x], t_half.at[x], t_far.at[x], None, t_sem.at[x])
-        for x in range(pairs)
+    def share(ref, sem):
+        return Share(p, lambda side, line: ref.at[side, line], lambda side: ref.at[side], sem)
+
+    def triple_share(x):
+        lanes = pl.ds(x * 128, 128)
+        return Share(
+            p,
+            lambda side, line: o_triple.at[:, side, line, :, lanes],
+            lambda side: o_triple.at[:, side, :, :, lanes],
+            s_sem.at[5 + x],
+        )
+
+    shares = [
+        share(ref.at[h], s_sem.at[2 * a + h])
+        for a, ref in enumerate((o_down, o_up))
+        for h in range(2)
     ]
-    triples = [Share(p, o_triple.at[x], s_sem.at[5 + x]) for x in range(pairs)]
-    for h in range(4):
-        shares[h].start((p_down, p_up)[h // 2][h % 2])
+    merge_total = Total(p, g_merge, m_near, m_far, m_sem)
+    merge_share = share(o_merge, s_sem.at[4])
+    totals = [Total(p, g_triple.at[x], t_near.at[x], t_far.at[x], t_sem.at[x]) for x in range(pairs)]
+    triples = [triple_share(x) for x in range(pairs)]
+    branch = Scatter(g, pout, in_near2, out_far2, in_far2, sem2)
+    up_total = Total(p, None, u_held, u_far, u_sem)
+    up_total.scatter()
+    for h, piece in enumerate((p_down0, p_down1, p_up0)):
+        shares[h].start(piece[...])
     merge_total.start()
+    for load in loads[:4]:
+        load.wait()
 
     lane = lax.broadcasted_iota(jnp.int32, (1, 128), 1)
     heads = [lane < HD, lane >= HD]
@@ -1017,19 +1146,39 @@
         loop(d // 256, tile)
         totals[x].start()
 
+    span = lambda k: pl.ds(pl.multiple_of(k * rows, rows), rows)
+
+    def branch_start():
+        loads[4].wait()
+        loop(CHUNKS, branch.send)
+
+    def branch_end():
+        loads[5].wait()
+
+        def one(k):
+            out[span(k), :] = (resid[span(k), :] + branch.final(k) + db[...]).astype(BF)
+
+        loop(CHUNKS, one)
+
     schedule = [[] for _ in range(pairs)]
-    schedule[0] = [(2, shares[0].spread), (3, shares[1].spread)]
+    schedule[0] = [
+        (0, branch_start),
+        (1, lambda: loop(CHUNKS, branch.combine)),
+        (2, lambda: shares[3].start(up_total.settle())),
+    ]
     schedule[-1] = schedule[-1] + [
-        (1, shares[2].spread),
-        (2, merge_total.halve),
-        (3, shares[3].spread),
+        (0, shares[0].spread),
+        (1, branch_end),
+        (1, merge_total.halve),
+        (2, shares[1].spread),
+        (3, totals[0].halve),
     ]
     for x in range(pairs):
         attention(x, schedule[x])
+        if x == 0:
+            for load in loads[6:]:
+                load.wait()
         weights(x)
-        if x == 0 and pairs > 1:
-            continue
-    totals[0].halve()
 
     scatter = Scatter(g, part, in_near, out_far, in_far, sem)
 
@@ -1053,17 +1202,18 @@
         scatter.send(k)
 
     loop(CHUNKS, back)
+    shares[2].spread()
     loop(CHUNKS, scatter.combine)
+    shares[3].spread()
+    merge_share.start(merge_total.settle())
     for x in range(1, pairs):
         totals[x].halve()
-    merge_share.start(merge_total.settle())
     triples[0].start(totals[0].settle())
     small[...] = small_in[...]
     units = bias_in.shape[1]
     small[6:7, :units] = bias_in[0:1, :]
     for c in range(3):
         small[7:8, c * width:(c + 1) * width] = col_sum(gm[c].astype(F32))
-    span = lambda k: pl.ds(pl.multiple_of(k * rows, rows), rows)
 
     def pull(k):
         gf = scatter.final(k)
@@ -1086,16 +1236,18 @@
     for x in range(1, pairs):
         triples[x].spread()
     small[...] = all_sum.finish()
-    for share in shares + [merge_share] + triples:
-        share.finish()
+    for one in shares + [merge_share] + triples:
+        one.finish()
     merge_total.drain()
+    up_total.drain(False)
     for t in totals:
         t.drain()
     loop(CHUNKS, scatter.drain)
-
-
-def late(size, count, mixed, att, gatt, lse, full, w, tokens, gres, gain, p_down, p_up, g_merge,
-         small_in, bias_in):
+    loop(CHUNKS, branch.drain)
+
+
+def late(size, count, gain, db, p_down0, p_down1, p_up0, u_held, g_merge, small_in, bias_in,
+         mixed, att, gatt, lse, full, w, tokens, gres, resid, pout):
     rows, d = tokens.shape
     n, width = att.shape
     r = rows // CHUNKS
@@ -1107,33 +1259,81 @@
     vm = pltpu.VMEM
     dma = pltpu.SemaphoreType.DMA
     deep = g_merge.shape[2]
-    units = bias_in.shape[1]
+    scatter = scatter_scratch(size, r, d)
+    loads = (mixed, att, gatt, lse, full, w, tokens, gres, resid, pout)
     return pl.pallas_call(
         functools.partial(late_kernel, size, count, bk),
         out_shape=(
+            shape((rows, d), BF),
             shape((rows, d), F32),
-            shape((2, 2, line) + p_down.shape[1:], BF),
-            shape((2, 2, line) + p_up.shape[1:], BF),
+            shape((2, 2, line) + p_down0.shape, BF),
+            shape((2, 2, line) + p_up0.shape, BF),
             shape(g_merge.shape, BF),
-            shape((pairs, 2, line, 3, piece, 128), BF),
+            shape((3, 2, line, piece, width), BF),
             shape((8, d), F32),
         ),
-        in_specs=[VMEM_SPEC] * 14,
-        out_specs=(VMEM_SPEC,) * 6,
-        scratch_shapes=[vm((2, n, 128), BF)] * 3
+        in_specs=[VMEM_SPEC] * 9 + [ANY_SPEC] * len(loads),
+        out_specs=(VMEM_SPEC,) * 7,
+        scratch_shapes=[vm(x.shape, x.dtype) for x in loads]
+        + [dma((len(loads),))]
+        + [vm((2, n, 128), BF)] * 3
         + [vm((8, n), F32), vm((n, 128), F32), vm((3, n, width), BF)]
         + [vm((pairs, 2, line, 3, piece, 128), BF)]
-        + scatter_scratch(size, r, d)
-        + [sems(size)]
+        + scatter
+        + scatter[1:]
+        + [sems(size)] * 2
+        + total_scratch(line, p_up0.shape)[1:]
         + total_scratch(line, (deep, d))
-        + [vm((pairs, line, 3, piece, 128), BF)] * 2
-        + [vm((pairs, line - 1, 3, piece, 128), BF), dma((pairs, 2, line)), dma((5 + pairs, 2, line))]
+        + [vm((pairs, line, 3, piece, 128), BF), vm((pairs, line - 1, 3, piece, 128), BF)]
+        + [dma((pairs, 2, line)), dma((5 + pairs, 2, line))]
         + [vm((size, 8, d), F32), dma((2, size)), vm((count, 8, d), F32), dma((2, count))],
         compiler_params=pltpu.CompilerParams(
-            collective_id=3, has_side_effects=True, vmem_limit_bytes=63 << 20
+            collective_id=3, has_side_effects=True, vmem_limit_bytes=64 << 20
         ),
         name="late",
-    )(mixed, att, gatt, lse, full, w, tokens, gres, gain, p_down, p_up, g_merge, small_in, bias_in)
+    )(gain, db, p_down0, p_down1, p_up0, u_held, g_merge, small_in, bias_in, *loads)
+
+
+def widen_kernel(down, up, merge, triple, small, out, tok, o_down, o_up, o_merge, o_triple, o_out, o_tok, *o_small):
+    for src, dst in ((down, o_down), (up, o_up), (merge, o_merge), (triple, o_triple)):
+        dst[...] = src[...].astype(F32)
+    o_out[...] = out[...]
+    o_tok[...] = tok[...]
+
+    @pl.when(pl.program_id(0) == 0)
+    def _():
+        for i, dst in enumerate(o_small[:7]):
+            dst[...] = small[i:i + 1, :dst.shape[1]]
+        width = o_small[7].shape[1]
+        for c in range(3):
+            o_small[7][c:c + 1, :] = small[7:8, c * width:(c + 1) * width]
+
+
+def widen(down, up, merge, triple, small, out, tok):
+    steps = 16
+    d, units, width = small.shape[1], up.shape[1], triple.shape[2]
+
+    def spec(x):
+        axis = x.ndim - 2
+        block = x.shape[:axis] + (x.shape[axis] // steps, x.shape[-1])
+        return pl.BlockSpec(block, lambda i: (0,) * axis + (i, 0))
+
+    def whole(shape):
+        return pl.BlockSpec(shape, lambda i: (0, 0))
+
+    arrays = (down, up, merge, triple)
+    lines = [(1, d)] * 6 + [(1, units), (3, width)]
+    outs = [(x.shape, F32, spec(x)) for x in arrays] + [(x.shape, x.dtype, spec(x)) for x in (out, tok)]
+    outs += [(x, F32, whole(x)) for x in lines]
+    return pl.pallas_call(
+        widen_kernel,
+        grid=(steps,),
+        out_shape=tuple(jax.ShapeDtypeStruct(x, t) for x, t, _ in outs),
+        in_specs=[spec(x) for x in arrays] + [whole(small.shape), spec(out), spec(tok)],
+        out_specs=tuple(x for _, _, x in outs),
+        compiler_params=pltpu.CompilerParams(vmem_limit_bytes=60 << 20),
+        name="widen",
+    )(down, up, merge, triple, small, out, tok)
 
 
 def on_device(
@@ -1164,30 +1364,31 @@
     count = count if fused else 0
     line = lambda v: v.reshape(1, -1)
     w = jnp.transpose(triple_weight, (1, 0, 2))
-    full, mixed, top = project(
-        size, lengths, tokens, cotangent, line(first_gain), line(first_shift), w, line(triple_bias)
+    full, mixed = project(
+        size, tokens, line(first_gain), line(first_shift), w, triple_bias
     )
     mixed = mixed.reshape(n, 3 * width)
-    every_top = lax.all_gather(top, "tensor", axis=0, tiled=True).reshape(size, CHUNKS, rows, d)
-    attended, log_total = attend_fwd(mixed, lengths)
-    blocks = lambda x: x.reshape(size, CHUNKS, rows, x.shape[-1])
-    gatt, gres, resid, pout, g_up, g_down, g_merge, small_b, bias_b, *pieces = middle(
-        size, count, lengths, blocks(attended), tokens, every_top, merge_weight, line(merge_bias),
-        line(second_gain), line(second_shift), up_weight, line(up_bias), down_weight,
+    attended, log_total, gatt, gres, resid, pout, g_merge, small_b, bias_b, *rest = core(
+        size, count, lengths, mixed, line(merge_bias), line(second_gain), line(second_shift),
+        line(up_bias), tokens, cotangent, merge_weight, up_weight, down_weight,
     )
-    branch = lax.psum_scatter(pout.reshape(n, d), "tensor", scatter_dimension=0, tiled=True)
     gatt = gatt.reshape(n, width)
     if fused:
-        gtok, down, up, merge, triple, small = late(
-            size, count, mixed, attended, gatt, log_total, full, w, tokens, gres, line(first_gain),
-            pieces[0], pieces[1], g_merge, small_b, bias_b,
+        output, gtok, down, up, merge, triple, small = late(
+            size, count, line(first_gain), line(down_bias), *rest, g_merge, small_b, bias_b,
+            mixed, attended, gatt, log_total, full, w, tokens, gres, resid, pout,
         )
-        down = down.reshape(units, d).astype(F32)
-        up = up.reshape(d, units).astype(F32)
-        merge = merge.reshape(width, d).astype(F32)
-        triple = jnp.transpose(triple, (1, 2, 4, 3, 0, 5)).reshape(d, 3, width).astype(F32)
-        triple_b, up_b = small[7, :3 * width].reshape(3, width), small[6, :units]
+        down, up, merge, triple, output, gtok, *small, up_b, triple_b = widen(
+            down.reshape(units, d), up.reshape(d, units), merge.reshape(width, d),
+            triple.reshape(3, d, width), small, output, gtok,
+        )
+        triple = jnp.transpose(triple, (1, 0, 2))
+        small = [x.reshape(d) for x in small]
+        up_b = up_b.reshape(units)
     else:
+        branch = lax.psum_scatter(pout.reshape(n, d), "tensor", scatter_dimension=0, tiled=True)
+        g_up, g_down = rest
+        blocks = lambda x: x.reshape(size, CHUNKS, rows, x.shape[-1])
         dq, dk, dv = attend_bwd(mixed, attended, log_total, gatt)
         gtok, g_triple, small_c, bias_c = tail(
             size, blocks(dq), blocks(dk), blocks(dv), full, w, tokens, gres, line(first_gain)
@@ -1198,7 +1399,7 @@
         triple = jnp.transpose(triple, (1, 0, 2)).astype(F32)
         triple_b = triple_b.reshape(3, width)
         merge, up, down = merge.astype(F32), up.astype(F32), down.astype(F32)
-    output = (resid + branch.astype(F32) + down_bias).astype(BF)
+        output = (resid + branch.astype(F32) + down_bias).astype(BF)
     return (
         output,
         gtok,

time: 385 us -> 317 us (0.82)
  Pallas kernels: 337 us -> 315 us
  local copies, waits for them, and re-layouts: 19.2 us -> 0 us
  other arithmetic: 13.4 us -> 0 us
  between operations: 14.8 us -> 1.5 us
    pallas_call x1, Pallas kernels: 144 us -> 130 us  [late(): pl.pallas_call(functools.partial(late_kernel, size, count, bk), out_shape...]
    convert_element_type x4 -> x0, other arithmetic: 13.4 us -> none  [the longest x1 6.81 us: on_device(): down = down.reshape(units, d).astype(F32)]
    unnamed x30 -> x0, local copies, waits for them, and re-layouts: 11.9 us -> none
    pallas_call x3, Pallas kernels: 193 us -> 185 us  [the longest x1 141 us: core(): pl.pallas_call(functools.partial(core_kernel, size, count), out_shape=tup...]
    convert_element_type x2 -> x0, local copies, waits for them, and re-layouts: 6.09 us -> none  [on_device(): jnp.transpose(triple, (1, 2, 4, 3, 0, 5)).reshape(d, 3, width).astype(F32)]
  transfers between devices with their start and end apart: 2 -> 0, of which waited for: 0 -> 0; matrix products, arithmetic and copies ran while one was open for 5% -> 0% of each run, Pallas kernels for 46% -> 0%
where the time goes in v2:
time: 317 us; the launch traced here: 316 us
  Pallas kernels  315 us (99%)
    pallas_call x1, Pallas kernels, core(): pl.pallas_call(functools.partial(core_kernel, size, count), out_shape=tup...  141 us
    pallas_call x1, Pallas kernels, late(): pl.pallas_call(functools.partial(late_kernel, size, count, bk), out_shape...  130 us
    pallas_call x1, Pallas kernels, project(): pl.pallas_call(functools.partial(project_kernel, size), out_shape=tuple((...  30.1 us
    pallas_call x1, Pallas kernels, widen(): pl.pallas_call(widen_kernel, grid=(steps,), out_shape=tuple((jax.ShapeDty...  14.4 us

profile of v2, /device:TPU:24, one launch (start us, length us, event | category | flops | bytes accessed | tf_op | source)
XLA Modules:
  0.0 316.4 jit_solution(3182430170449295819)
XLA Ops:
  1.3 30.1 %project.1 = (bf16[4,4,128,1024]{3,2,1,0:T(8,128)(2,1)}, bf16[4,4,128,768]{3,2,1,0:T(8,128)(2,1)}) custom-call(bf16[512,1024]{1,0:T(8,128)(2,1)} %tok_hbm.3, f32[1,1024]{1,0:T(1,128)} %bitcast.33, f32[1,1024]{1,0:T(1,128)} %bitcast.39, bf16[3,1024,256]{2,1,0:T(8,128)(2,1)} %bitcast.25, f32[3,256]{1,0:T(4,128)} %b.1), custom_call_target="tpu_custom_call" | custom-call | tf_op jit(solution)/shard_map/project/pallas_call | solution.py:489
  31.4 140.6 %core.1 = (bf16[2048,256]{1,0:T(8,128)(2,1)}, f32[2,8,2048]{2,1,0:T(8,128)}, bf16[4,4,128,256]{3,2,1,0:T(8,128)(2,1)}, f32[512,1024]{1,0:T(8,128)}, f32[512,1024...) custom-call(s32[1]{0:T(128)S(6)} %copy.29.length, ...), custom_call_target="tpu_custom_call" | custom-call | tf_op jit(solution)/shard_map/core/pallas_call | solution.py:872
  172.0 129.8 %late.1 = (bf16[512,1024]{1,0:T(8,128)(2,1)}, f32[512,1024]{1,0:T(8,128)}, bf16[2,2,4,64,1024]{4,3,2,1,0:T(8,128)(2,1)}, bf16[2,2,4,64,1024]{4,3,2,1,0:T(8,128)(...) custom-call(f32[1,1024]{1,0:T(1,128)} %bitcast.34, ...), custom_call_target="tpu_custom_call" | custom-call | tf_op jit(solution)/shard_map/late/pallas_call | solution.py:1264
  301.8 14.4 %widen.1 = (f32[1024,1024]{1,0:T(8,128)}, f32[1024,1024]{1,0:T(8,128)}, f32[256,1024]{1,0:T(8,128)}, f32[3,1024,256]{2,1,0:T(8,128)}, bf16[512,1024]{1,0:T(8,128...) custom-call(bf16[1024,1024]{1,0:T(8,128)(2,1)} %bitcast.27, ...), custom_call_target="tpu_custom_call" | custom-call | tf_op jit(solution)/shard_map/widen/pallas_call | solution.py:1328

commit v3 on v2

--- a/solution.py
+++ b/solution.py
@@ -277,12 +277,14 @@
         self.row = self.me // 2
         self.side = self.me % 2
         self.partner = self.row * 2 + 1 - self.side
-
-    def step(self, off):
-        return (self.row + off) % self.line
+        self.next = self.row + 1 - self.row % 2 * 2
+        self.inner = self.next % 3 == 0
+
+    def at(self, row):
+        return row * 2 + self.side
 
     def peer(self, off):
-        return self.step(off) * 2 + self.side
+        return self.at((self.row + off) % self.line)
 
     def greet(self, barrier):
         peers = [self.partner] + [self.peer(off) for off in range(1, self.line)]
@@ -303,12 +305,24 @@
             self.src.at[1 - p.side], self.near, sem.at[0, 0], sem.at[1, 0], "dp", p.partner
         )
 
-    def piece(self, off):
+    def outward(self):
         p, sem = self.p, self.sem
-        back = p.line - off
         return remote(
-            self.near.at[p.step(off)], self.far.at[back - 1], sem.at[0, off], sem.at[1, back],
-            "dp", p.peer(off),
+            self.near.at[pl.ds(1 - p.row // 3, 3)], self.far.at[pl.ds(0, 3)], sem.at[0, 1],
+            sem.at[1, 1], "dp", p.at(p.next),
+        )
+
+    def inward(self):
+        p, sem = self.p, self.sem
+        return remote(
+            self.near.at[p.next], self.far.at[0], sem.at[0, 1], sem.at[1, 1], "dp", p.at(p.next)
+        )
+
+    def summed(self, i):
+        p, sem = self.p, self.sem
+        target = (3 - p.row, 3 - p.next)[i]
+        return remote(
+            self.near.at[target], self.far.at[3], sem.at[0, 2 + i], sem.at[1, 2], "dp", p.at(target)
         )
 
     def start(self):
@@ -321,72 +335,130 @@
             self.near[j] = total.astype(BF)
 
     def scatter(self):
-        for off in range(1, self.p.line):
-            self.piece(off).start()
+        @pl.when(self.p.inner)
+        def _():
+            self.inward().start()
+
+        @pl.when(jnp.logical_not(self.p.inner))
+        def _():
+            self.outward().start()
 
     def halve(self):
         self.add()
         self.scatter()
 
+    def relay(self):
+        p = self.p
+
+        @pl.when(p.inner)
+        def _():
+            self.outward().wait_recv()
+            skip = 2 - p.row
+            for i, target in enumerate((3 - p.row, 3 - p.next)):
+                total = self.near[target].astype(F32) + self.far[target - skip].astype(F32)
+                self.near[target] = total.astype(BF)
+                self.summed(i).start()
+            total = self.near[p.row].astype(F32) + self.far[p.row - skip].astype(F32)
+            self.near[p.row] = total.astype(BF)
+
+        @pl.when(jnp.logical_not(p.inner))
+        def _():
+            self.inward().wait_recv()
+            total = self.near[p.row].astype(F32) + self.far[0].astype(F32)
+            self.near[p.row] = total.astype(BF)
+
     def settle(self):
-        p, sem = self.p, self.sem
-        total = self.near[p.row].astype(F32)
-        for off in range(1, p.line):
-            remote(
-                self.near.at[p.row], self.far.at[off - 1], sem.at[0, off], sem.at[1, off],
-                "dp", p.peer(off),
-            ).wait_recv()
-            total = total + self.far[off - 1].astype(F32)
-        return total.astype(BF)
+        self.summed(0).wait_recv()
+        return (self.near[self.p.row].astype(F32) + self.far[3].astype(F32)).astype(BF)
 
     def drain(self, pair=True, pieces=True):
         if pair:
             self.pair().wait_send()
-        for off in range(1, self.p.line) if pieces else ():
-            self.piece(off).wait_send()
+        if not pieces:
+            return
+
+        @pl.when(self.p.inner)
+        def _():
+            self.inward().wait_send()
+            self.summed(0).wait_send()
+            self.summed(1).wait_send()
+
+        @pl.when(jnp.logical_not(self.p.inner))
+        def _():
+            self.outward().wait_send()
 
 
 class Share:
     def __init__(self, place, piece, half, sem):
         self.p, self.piece_at, self.half_at, self.sem = place, piece, half, sem
 
-    def piece(self, off):
+    def piece(self, i, owner, target):
         p, sem = self.p, self.sem
-        here = self.piece_at(p.side, p.row)
-        return remote(here, here, sem.at[0, off], sem.at[1, p.line - off], "dp", p.peer(off))
+        here = self.piece_at(p.side, owner)
+        return remote(here, here, sem.at[0, i], sem.at[1, owner], "dp", p.at(target))
+
+    def first(self):
+        p = self.p
+        second = jnp.where(p.inner, 3 - p.row, 3 - p.next)
+        return self.piece(0, p.row, p.next), self.piece(1, p.row, second)
+
+    def passed(self):
+        p = self.p
+        return self.piece(2, 3 - p.row, p.next), self.piece(3, 3 - p.next, p.next)
 
     def half(self):
         p, sem = self.p, self.sem
         here = self.half_at(p.side)
-        return remote(here, here, sem.at[0, 0], sem.at[1, 0], "dp", p.partner)
+        return remote(here, here, sem.at[0, 4], sem.at[1, 4], "dp", p.partner)
 
     def start(self, piece):
         self.piece_at(self.p.side, self.p.row)[...] = piece
-        for off in range(1, self.p.line):
-            self.piece(off).start()
+        for one in self.first():
+            one.start()
+
+    def relay(self):
+        p = self.p
+
+        @pl.when(p.inner)
+        def _():
+            for i, owner in ((2, 3 - p.row), (3, 3 - p.next)):
+                self.piece(i, owner, p.next).wait_recv()
+                self.piece(i, owner, p.next).start()
+
+    def gathered(self):
+        p = self.p
+        self.piece(0, p.next, p.next).wait_recv()
+
+        @pl.when(jnp.logical_not(p.inner))
+        def _():
+            self.piece(0, 3 - p.row, p.next).wait_recv()
+            self.piece(0, 3 - p.next, p.next).wait_recv()
 
     def spread(self):
-        p, sem = self.p, self.sem
-        for off in range(1, p.line):
-            here = self.piece_at(p.side, p.step(off))
-            remote(here, here, sem.at[0, off], sem.at[1, off], "dp", p.peer(off)).wait_recv()
+        self.gathered()
         self.half().start()
 
-    def finish(self):
+    def sent(self):
+        p = self.p
+        for one in self.first():
+            one.wait_send()
+
+        @pl.when(p.inner)
+        def _():
+            for one in self.passed():
+                one.wait_send()
+
+    def finish(self, pieces=True):
         p, sem = self.p, self.sem
         there = self.half_at(1 - p.side)
-        remote(there, there, sem.at[0, 0], sem.at[1, 0], "dp", p.partner).wait_recv()
-        for off in range(1, p.line):
-            self.piece(off).wait_send()
+        remote(there, there, sem.at[0, 4], sem.at[1, 4], "dp", p.partner).wait_recv()
+        if pieces:
+            self.sent()
         self.half().wait_send()
 
 
 def total_scratch(line, block):
-    return [
-        pltpu.VMEM((line,) + block, BF),
-        pltpu.VMEM((line - 1,) + block, BF),
-        pltpu.SemaphoreType.DMA((2, line)),
-    ]
+    return [pltpu.VMEM((line,) + block, BF)] * 2 + [pltpu.SemaphoreType.DMA((2, line))]
 
 
 ANY_SPEC = pl.BlockSpec(memory_space=pl.ANY)
@@ -428,76 +500,6 @@
 def enter_kernel(group):
     barrier = pltpu.get_barrier_semaphore()
     pl.semaphore_wait(barrier, group.greet(barrier))
-
-
-def project_kernel(size, tok, gain, shift, w_hbm, b, full_hbm, mixed_hbm, full, mixed, w, sem, w_sem, out_sem):
-    g = Group(size)
-    rows = tok.shape[0] // CHUNKS
-    width = w.shape[2]
-    load = Move(w_hbm, w, w_sem).start()
-    enter_kernel(g)
-    gather = Gather(g, full, sem)
-
-    def norm(k):
-        unit, _ = norm_stats(tok[pl.ds(pl.multiple_of(k * rows, rows), rows), :].astype(F32))
-        full[g.me, k] = (unit * gain[...] + shift[...]).astype(BF)
-        gather.send(k)
-
-    loop(CHUNKS, norm)
-    load.wait()
-
-    def stores(k):
-        return (
-            Move(full.at[:, k], full_hbm.at[:, k], out_sem.at[0, k]),
-            Move(mixed.at[:, k], mixed_hbm.at[:, k], out_sem.at[1, k]),
-        )
-
-    def multiply(k):
-        gather.wait(k)
-        x = rows_of(full, k)
-        for c in range(3):
-            cols = slice(c * width, (c + 1) * width)
-            y = (mm(x, w[c], NN) + b[c:c + 1, :]).astype(BF)
-            for s in range(size):
-                mixed[s, k, :, cols] = y[s * rows:(s + 1) * rows]
-        for store in stores(k):
-            store.start()
-
-    def body(k):
-        gather.forward(k)
-
-        @pl.when(k > 0)
-        def _():
-            multiply(k - 1)
-
-    loop(CHUNKS, body)
-    multiply(CHUNKS - 1)
-
-    def drain(k):
-        gather.drain(k)
-        for store in stores(k):
-            store.wait()
-
-    loop(CHUNKS, drain)
-
-
-def project(size, tokens, gain, shift, w, b):
-    rows, d = tokens.shape
-    r = rows // CHUNKS
-    shapes = ((size, CHUNKS, r, d), (size, CHUNKS, r, 3 * w.shape[2]))
-    dma = pltpu.SemaphoreType.DMA
-    return pl.pallas_call(
-        functools.partial(project_kernel, size),
-        out_shape=tuple(jax.ShapeDtypeStruct(x, BF) for x in shapes),
-        in_specs=[VMEM_SPEC] * 3 + [ANY_SPEC, VMEM_SPEC],
-        out_specs=(ANY_SPEC,) * 2,
-        scratch_shapes=[pltpu.VMEM(x, BF) for x in shapes]
-        + [pltpu.VMEM(w.shape, BF), sems(size), dma, dma((2, CHUNKS))],
-        compiler_params=pltpu.CompilerParams(
-            collective_id=0, has_side_effects=True, vmem_limit_bytes=63 << 20
-        ),
-        name="project",
-    )(tokens, gain, shift, w, b)
 
 
 def fold(x, op):
@@ -524,11 +526,13 @@
                 v = self.mixed[:, 2 * self.width + x * 128:2 * self.width + (x + 1) * 128]
                 self.values[2 * x + h] = jnp.where(self.heads[h], v, jnp.zeros_like(v))
 
-    def run(self, u, low, high):
+    def run(self, u, event=None):
         def body(i):
             self.unit(u, i // self.pairs, i % self.pairs)
-
-        loop_range(low * self.pairs, high * self.pairs, body)
+            if event is not None:
+                pl.when(i == (self.size - 1) * self.pairs - 1)(event)
+
+        loop(self.size * self.pairs, body)
 
     def unit(self, u, s, x):
         bq, bk = self.rows, self.block
@@ -587,18 +591,19 @@
 
 
 def core_kernel(
-    size, count, length, mb, gain, shift, ub, mixed_hbm, tok_hbm, cot_hbm, mw_hbm, up_hbm, down_hbm,
-    att, lse, gatt, gres_hbm, resid_hbm, pout_hbm, g_merge, small, bias, *rest,
+    size, count, length, gain1, shift1, tb, mb, gain, shift, ub,
+    w_hbm, tok_hbm, cot_hbm, mw_hbm, up_hbm, down_hbm,
+    full_hbm, mixed_hbm, att, lse, gatt, gres_hbm, resid_hbm, pout_hbm, g_merge, small, bias, *rest,
 ):
     if count:
-        (pieces, held, rest) = (rest[:3], rest[3], rest[4:])
+        (pieces, held, raw, rest) = (rest[:2], rest[2], rest[3], rest[4:])
     else:
         (g_up, g_down, rest) = (rest[0], rest[1], rest[2:])
     (
-        mixed, tok, cot, mw, up, down, scores, values, resid, gres, pout, part, in_near, out_far, in_far,
-        full, hid, gb, sem1, sem2, sem3, sem4, sem5, load_sem, cot_sem, out_sem, free,
-    ) = rest[:27]
-    rest = rest[27:]
+        w, mixed, tok, cot, mw, up, down, scores, values, resid, gres, pout, part, in_near, out_far, in_far,
+        full, hid, gb, sem0, sem1, sem2, sem3, sem4, sem5, load_sem, cot_sem, out_sem, free,
+    ) = rest[:29]
+    rest = rest[29:]
     g = Group(size)
     rows, d = tok.shape[0] // CHUNKS, tok.shape[1]
     width, units = mw.shape[0], up.shape[1]
@@ -608,11 +613,12 @@
     loads = [
         Move(src, dst, load_sem.at[i]).start()
         for i, (src, dst) in enumerate(
-            ((mixed_hbm, mixed), (tok_hbm, tok), (mw_hbm, mw), (up_hbm, up), (down_hbm, down))
+            ((tok_hbm, tok), (w_hbm, w), (mw_hbm, mw), (up_hbm, up), (down_hbm, down))
         )
     ]
     own = lambda k: Move(cot_hbm.at[k], cot.at[g.me, k], cot_sem.at[k])
     loop(CHUNKS, lambda k: own(k).start())
+    begin = Gather(g, full, sem0)
     barrier = pltpu.get_barrier_semaphore()
     pl.semaphore_wait(barrier, g.greet(barrier) + (p.greet(barrier) if count else 0))
     tops = Gather(g, cot, sem5)
@@ -627,11 +633,21 @@
     sums = []
     if count:
         g_up, g_down, rest = rest[0], rest[1], rest[2:]
-        for ref in (g_down, g_up):
-            for h in range(2):
-                near, far, sem = rest[:3]
-                rest = rest[3:]
-                sums.append(Total(p, ref.at[h], near, far, sem))
+        for ref in (g_down.at[0], g_down.at[1], g_up.at[0]):
+            near, far, sem = rest[:3]
+            rest = rest[3:]
+            sums.append(Total(p, ref, near, far, sem))
+
+    def at(s, k):
+        return pl.ds(pl.multiple_of((s * CHUNKS + k) * rows, rows), rows)
+
+    def enter(k):
+        unit, _ = norm_stats(tok[span(k), :].astype(F32))
+        full[g.me, k] = (unit * gain1[...] + shift1[...]).astype(BF)
+        begin.send(k)
+
+    loads[0].wait()
+    loop(CHUNKS, enter)
 
     def mask(k):
         own(k).wait()
@@ -640,12 +656,33 @@
         tops.send(k)
 
     loop(CHUNKS, mask)
+    loads[1].wait()
+
+    def full_store(k):
+        return Move(full.at[:, k], full_hbm.at[:, k], out_sem.at[3, k])
+
+    def project(k):
+        begin.wait(k)
+        full_store(k).start()
+        x = rows_of(full, k)
+        for j in range(3):
+            cols = slice(j * width, (j + 1) * width)
+            y = (mm(x, w[j], NN) + tb[j:j + 1, :]).astype(BF)
+            for s in range(size):
+                mixed[at(s, k), cols] = y[s * rows:(s + 1) * rows]
+
+    def begin_step(k):
+        begin.forward(k)
+
+        @pl.when(k > 0)
+        def _():
+            project(k - 1)
+
+    loop(CHUNKS, begin_step)
+    project(CHUNKS - 1)
+    mixed_store = Move(mixed, mixed_hbm, load_sem.at[5]).start()
     attend = Attend(size, 2, length, mixed, att, lse, scores, values)
-    loads[0].wait()
     attend.prepare()
-
-    def at(s, k):
-        return pl.ds(pl.multiple_of((s * CHUNKS + k) * rows, rows), rows)
 
     def merge(k):
         x = jnp.concatenate([att[at(s, k), :] for s in range(size)], axis=0)
@@ -731,14 +768,18 @@
 
         return block, extent // tall
 
-    def weights(ref, left, right, extent, pair):
+    def weights(ref, left, right, extent, event=None):
         block, blocks = products(ref, left, right, extent)
-        if not count:
-            loop(blocks, block)
-            return
-        for h in range(2):
-            loop_range(h * blocks // 2, (h + 1) * blocks // 2, block)
-            pair[h].start()
+        after(0, blocks, block, {blocks // 2 - 1: event})
+
+    def after(low, high, body, events):
+        def step(k):
+            body(k)
+            for at_k, event in events.items():
+                if count and event is not None:
+                    pl.when(k == at_k)(event)
+
+        loop_range(low, high, step)
 
     def gres_store(k):
         return Move(gres.at[k % 2], gres_hbm.at[span(k)], out_sem.at[2, k])
@@ -777,16 +818,20 @@
 
     bias[...] = jnp.zeros_like(bias)
     small[...] = jnp.zeros_like(small)
-    attend.run(0, 0, size)
-    for load in loads[1:]:
+    attend.run(0)
+    for load in loads[2:]:
         load.wait()
+    loop(CHUNKS, begin.drain)
+    loop(CHUNKS, lambda k: full_store(k).wait())
     loop(2, merge)
     loop(2, first.combine)
     loop(2, tops.forward)
-    attend.run(1, 0, size - 1)
-    loop_range(2, CHUNKS, tops.forward)
-    loop(2, norm)
-    attend.run(1, size - 1, size)
+
+    def between():
+        loop_range(2, CHUNKS, tops.forward)
+        loop(2, norm)
+
+    attend.run(1, between)
     loop_range(2, CHUNKS, merge)
     loop_range(2, CHUNKS, first.combine)
     loop(CHUNKS, tops.wait)
@@ -797,42 +842,47 @@
     loop(2, second.combine)
     loop_range(2, CHUNKS, first.drain)
     loop_range(2, CHUNKS, inner)
-    weights(g_down, hid, cot, units, sums[:2])
-    peers = g.greet(free)
-    loop_range(2, CHUNKS, leave)
+    weights(g_down, hid, cot, units, sums[0].start if count else None)
+    pl.semaphore_wait(free, g.greet(free))
+    loop(2, pull)
+    after(2, CHUNKS, leave, {2: sums[1].start if count else None})
     loop_range(2, CHUNKS, second.combine)
-    pl.semaphore_wait(free, peers)
-    loop(2, pull)
-    weights(g_up, full, gb, d, sums[2:])
     later(lambda: sums[0].halve())
+    weights(g_up, full, gb, d)
+    later(lambda: sums[2].start())
     loop(CHUNKS, tops.drain)
     loop(CHUNKS, spread.drain)
-    loop_range(2, CHUNKS, pull)
-    later(lambda: sums[1].halve())
-    loop(2, last)
-    later(lambda: sums[2].halve())
-    loop_range(2, CHUNKS, last)
+
+    def turn():
+        sums[0].relay()
+        sums[1].halve()
+
+    after(2, CHUNKS, pull, {2: turn})
+    after(0, CHUNKS, last, {0: lambda: sums[1].relay()})
     y = mm(att[...], flat(gfull, slice(None)), TN).astype(BF)
     if count:
         deep = g_merge.shape[2]
         for f in range(2 * p.line):
             g_merge[f // p.line, f % p.line] = y[f * deep:(f + 1) * deep]
+        raw[...] = g_up[1]
+        sums[2].add()
+        held[...] = sums[2].near[...]
+        pieces[0][...] = sums[0].settle()
+        pieces[1][...] = sums[1].settle()
         for h in range(3):
-            pieces[h][...] = sums[h].settle()
-        sums[3].add()
-        held[...] = sums[3].near[...]
-        for h in range(4):
-            sums[h].drain(True, h < 3)
+            sums[h].drain(True, h < 2)
     else:
         g_merge[...] = y
     loop(CHUNKS, second.drain)
     loop(CHUNKS, back.drain)
     loop(CHUNKS, lambda k: resid_store(k).wait())
+    mixed_store.wait()
     loop_range(2, CHUNKS, lambda k: pout_store(k).wait())
     loop_range(2, CHUNKS, lambda k: gres_store(k).wait())
 
 
-def core(size, count, lengths, mixed, mb, gain, shift, ub, tokens, cotangent, mw, up, down):
+def core(size, count, lengths, gain1, shift1, tb, mb, gain, shift, ub, w, tokens, cotangent, mw,
+         up, down):
     rows, d = tokens.shape
     r = rows // CHUNKS
     n = rows * size
@@ -847,10 +897,9 @@
         blocks = ((2, 2, line, d // (4 * line), units), (2, 2, line, units // (4 * line), d))
         merge = shape((2, line, width // (2 * line), d), BF)
         piece = [shape(b[3:], BF) for b in blocks[::-1]]
-        extra = (piece[0], piece[0], piece[1], shape((line,) + blocks[0][3:], BF))
+        extra = (piece[0], piece[0], shape((line,) + blocks[0][3:], BF), shape(blocks[0][1:], BF))
         scratch = [vm(b, BF) for b in blocks]
-        for b in blocks[::-1]:
-            scratch += total_scratch(line, b[3:]) * 2
+        scratch += total_scratch(line, blocks[1][3:]) * 2 + total_scratch(line, blocks[0][3:])
     else:
         merge = shape((width, d), BF)
         extra = (shape((d, units), BF), shape((units, d), BF))
@@ -858,6 +907,8 @@
     if units != d:
         scratch = [wide(d)] + scratch
     outs = (
+        (shape((size, CHUNKS, r, d), BF), ANY_SPEC),
+        (shape((n, 3 * width), BF), ANY_SPEC),
         (shape((n, width), BF), VMEM_SPEC),
         (shape((pairs, 8, n), F32), VMEM_SPEC),
         (shape((size, CHUNKS, r, width), BF), VMEM_SPEC),
@@ -872,23 +923,24 @@
     return pl.pallas_call(
         functools.partial(core_kernel, size, count),
         out_shape=tuple(x for x, _ in outs),
-        in_specs=[SMEM_SPEC] + [VMEM_SPEC] * 4 + [ANY_SPEC] * 6,
+        in_specs=[SMEM_SPEC] + [VMEM_SPEC] * 7 + [ANY_SPEC] * 6,
         out_specs=tuple(x for _, x in outs),
         scratch_shapes=[
-            vm(mixed.shape, BF), vm((rows, d), BF), wide(d), vm((width, d), BF), vm((d, units), BF), vm((units, d), BF),
+            vm(w.shape, BF), vm((n, 3 * width), BF), vm((rows, d), BF), wide(d), vm((width, d), BF), vm((d, units), BF), vm((units, d), BF),
             vm((2, size, rows // 2, rows), F32), vm((2 * pairs, n, 128), BF), vm((rows, d), F32),
             vm((2, r, d), F32), vm((2, size, r, d), BF),
         ]
         + scatter_scratch(size, r, d)
         + [wide(d), wide(units), wide(units)]
-        + [sems(size)] * 5
-        + [dma((5,)), dma((CHUNKS,)), dma((3, CHUNKS)), pltpu.SemaphoreType.REGULAR]
+        + [sems(size)] * 6
+        + [dma((6,)), dma((CHUNKS,)), dma((4, CHUNKS)), pltpu.SemaphoreType.REGULAR]
         + scratch,
         compiler_params=pltpu.CompilerParams(
             collective_id=1, has_side_effects=True, vmem_limit_bytes=64 << 20
         ),
         name="core",
-    )(lengths, mb, gain, shift, ub, mixed, tokens, cotangent.reshape(CHUNKS, r, d), mw, up, down)
+    )(lengths, gain1, shift1, tb, mb, gain, shift, ub, w, tokens, cotangent.reshape(CHUNKS, r, d), mw,
+      up, down)
 
 
 def tail_kernel(
@@ -999,13 +1051,13 @@
 
 
 def late_kernel(
-    size, count, bk, gain, db, p_down0, p_down1, p_up0, u_held, g_merge, small_in, bias_in,
+    size, count, bk, gain, db, p_down0, p_down1, u_held, u_raw, g_merge, small_in, bias_in,
     mixed_hbm, att_hbm, gatt_hbm, lse_hbm, full_hbm, w_hbm, tok_hbm, gres_hbm, resid_hbm, pout_hbm,
-    out, gtok, o_down, o_up, o_merge, o_triple, small,
+    out, gtok_hbm, o_down, o_up, o_merge, o_triple, small,
     mixed, att, gatt, lse, full, w, tok, gres, resid, pout, load_sem,
     qm, km, dom, dsc, dq_acc, gm, g_triple, part, in_near, out_far, in_far,
-    in_near2, out_far2, in_far2, sem, sem2, u_far, u_sem,
-    m_near, m_far, m_sem, t_near, t_far, t_sem, s_sem, t_buf, t_sems, d_buf, d_sems,
+    in_near2, out_far2, in_far2, sem, sem2, u_far, u_sem, v_near, v_far, v_sem,
+    m_near, m_far, m_sem, t_near, t_far, t_sem, s_sem, t_buf, t_sems, d_buf, d_sems, g_sem,
 ):
     loads = [
         Move(src, dst, load_sem.at[i]).start()
@@ -1036,14 +1088,19 @@
     def share(ref, sem):
         return Share(p, lambda side, line: ref.at[side, line], lambda side: ref.at[side], sem)
 
-    def triple_share(x):
-        lanes = pl.ds(x * 128, 128)
+    deep = g_triple.shape[5]
+
+    def triple_share(x, h):
+        lanes, part_rows = pl.ds(x * 128, 128), pl.ds(h * deep, deep)
         return Share(
             p,
-            lambda side, line: o_triple.at[:, side, line, :, lanes],
-            lambda side: o_triple.at[:, side, :, :, lanes],
-            s_sem.at[5 + x],
+            lambda side, line: o_triple.at[:, side, line, part_rows, lanes],
+            lambda side: o_triple.at[:, side, :, part_rows, lanes],
+            s_sem.at[5 + 2 * x + h],
         )
+
+    def triple_total(x, h):
+        return Total(p, g_triple.at[x, h], t_near.at[x, h], t_far.at[x, h], t_sem.at[x, h])
 
     shares = [
         share(ref.at[h], s_sem.at[2 * a + h])
@@ -1052,14 +1109,14 @@
     ]
     merge_total = Total(p, g_merge, m_near, m_far, m_sem)
     merge_share = share(o_merge, s_sem.at[4])
-    totals = [Total(p, g_triple.at[x], t_near.at[x], t_far.at[x], t_sem.at[x]) for x in range(pairs)]
-    triples = [triple_share(x) for x in range(pairs)]
+    totals = [triple_total(x, h) for x in range(pairs) for h in range(2)]
+    triples = [triple_share(x, h) for x in range(pairs) for h in range(2)]
     branch = Scatter(g, pout, in_near2, out_far2, in_far2, sem2)
     up_total = Total(p, None, u_held, u_far, u_sem)
     up_total.scatter()
-    for h, piece in enumerate((p_down0, p_down1, p_up0)):
-        shares[h].start(piece[...])
-    merge_total.start()
+    raw_total = Total(p, u_raw, v_near, v_far, v_sem)
+    raw_total.start()
+    shares[0].start(p_down0[...])
     for load in loads[:4]:
         load.wait()
 
@@ -1070,7 +1127,7 @@
 
     def attention(x, events):
         def lanes(c):
-            return slice(c * width + x * 128, c * width + (x + 1) * 128)
+            return pl.ds(pl.multiple_of(c * width + x * 128, 128), 128)
 
         def prepare(i):
             sl = pl.ds(pl.multiple_of(i * bk, bk), bk)
@@ -1108,43 +1165,48 @@
             dq_acc[qs, :] += dq
             return dk, dv
 
+        def serve(j, i):
+            for at_x, at_j, at_i, event in events:
+                pl.when((x == at_x) & (j == at_j) & (i == at_i))(event)
+
         def block(j):
-            for at, event in events:
-                @pl.when(j == at)
-                def _():
-                    event()
-
+            serve(j, j)
             z = jnp.zeros((bk, 128), F32)
             dk, dv = tile(j, j, z, z, True)
-            dk, dv = lax.fori_loop(
-                j + 1, n // bk, lambda i, c: tile(j, i, c[0], c[1], False), (dk, dv)
-            )
+
+            def more(i, c):
+                serve(j, i)
+                return tile(j, i, c[0], c[1], False)
+
+            dk, dv = lax.fori_loop(j + 1, n // bk, more, (dk, dv))
             ks = pl.ds(pl.multiple_of(j * bk, bk), bk)
-            gm[1, ks, x * 128:(x + 1) * 128] = (dk * HD ** (-0.5)).astype(BF)
-            gm[2, ks, x * 128:(x + 1) * 128] = dv.astype(BF)
+            gm[1, ks, lanes(0)] = (dk * HD ** (-0.5)).astype(BF)
+            gm[2, ks, lanes(0)] = dv.astype(BF)
 
         loop(n // bk, block)
-        gm[0, :, x * 128:(x + 1) * 128] = (dq_acc[...] * HD ** (-0.5)).astype(BF)
+        gm[0, :, lanes(0)] = (dq_acc[...] * HD ** (-0.5)).astype(BF)
 
     def flat(ref, cols):
         y = ref[:, :, :, cols]
         return y.reshape(n, y.shape[3])
 
     def weights(x):
-        y = jnp.concatenate([gm[c, :, x * 128:(x + 1) * 128] for c in range(3)], axis=1)
-        deep = g_triple.shape[4]
+        mine = pl.ds(pl.multiple_of(x * 128, 128), 128)
+        y = jnp.concatenate([gm[c, :, mine] for c in range(3)], axis=1)
 
         def tile(i):
             z = mm(flat(full, pl.ds(pl.multiple_of(i * 256, 256), 256)), y, TN).astype(BF)
-            for e in range(256 // deep):
-                f = i * (256 // deep) + e
-                for c in range(3):
-                    g_triple[x, f // p.line, f % p.line, c] = z[
-                        e * deep:(e + 1) * deep, c * 128:(c + 1) * 128
-                    ]
+            for e in range(128 // deep):
+                f = i * (128 // deep) + e
+                for h in range(2):
+                    at = (2 * e + h) * deep
+                    for c in range(3):
+                        g_triple[x, h, f // p.line, f % p.line, c] = z[
+                            at:at + deep, c * 128:(c + 1) * 128
+                        ]
 
         loop(d // 256, tile)
-        totals[x].start()
+        triple_total(x, 0).start()
 
     span = lambda k: pl.ds(pl.multiple_of(k * rows, rows), rows)
 
@@ -1160,25 +1222,60 @@
 
         loop(CHUNKS, one)
 
+    span = lambda k: pl.ds(pl.multiple_of(k * rows, rows), rows)
+
+    def branch_start():
+        loads[4].wait()
+        loop(CHUNKS, branch.send)
+
+    def branch_end():
+        loads[5].wait()
+
+        def one(k):
+            out[span(k), :] = (resid[span(k), :] + branch.final(k) + db[...]).astype(BF)
+
+        loop(CHUNKS, one)
+
     schedule = [[] for _ in range(pairs)]
-    schedule[0] = [
-        (0, branch_start),
-        (1, lambda: loop(CHUNKS, branch.combine)),
-        (2, lambda: shares[3].start(up_total.settle())),
+    end = pairs - 1
+    events = [
+        (0, 0, 0, branch_start),
+        (0, 0, 2, merge_total.start),
+        (0, 1, 1, lambda: loop(CHUNKS, branch.combine)),
+        (0, 1, 2, up_total.relay),
+        (0, 1, 2, raw_total.halve),
+        (0, 1, 3, shares[0].relay),
+        (0, 1, 3, lambda: shares[1].start(p_down1[...])),
+        (0, 2, 3, lambda: shares[2].start(up_total.settle())),
+        (0, 3, 3, shares[0].spread),
+        (0, 3, 3, raw_total.relay),
+        (0, 3, 3, shares[1].relay),
+        (end, 0, 1, totals[1].start),
+        (end, 0, 1, shares[2].relay),
+        (end, 0, 1, lambda: shares[3].start(raw_total.settle())),
+        (end, 0, 2, shares[1].spread),
+        (end, 0, 3, merge_total.halve),
+        (end, 1, 1, shares[3].relay),
+        (end, 1, 1, branch_end),
+        (end, 1, 2, shares[2].spread),
+        (end, 1, 3, totals[0].halve),
+        (end, 2, 2, merge_total.relay),
+        (end, 2, 3, totals[1].halve),
+        (end, 3, 3, totals[0].relay),
+        (end, 3, 3, lambda: merge_share.start(merge_total.settle())),
     ]
-    schedule[-1] = schedule[-1] + [
-        (0, shares[0].spread),
-        (1, branch_end),
-        (1, merge_total.halve),
-        (2, shares[1].spread),
-        (3, totals[0].halve),
-    ]
-    for x in range(pairs):
-        attention(x, schedule[x])
-        if x == 0:
+
+    def pair(x):
+        attention(x, events)
+
+        @pl.when(x == 0)
+        def _():
             for load in loads[6:]:
                 load.wait()
+
         weights(x)
+
+    loop(pairs, pair)
 
     scatter = Scatter(g, part, in_near, out_far, in_far, sem)
 
@@ -1201,52 +1298,87 @@
         loop(d // 256, tile)
         scatter.send(k)
 
-    loop(CHUNKS, back)
-    shares[2].spread()
-    loop(CHUNKS, scatter.combine)
-    shares[3].spread()
-    merge_share.start(merge_total.settle())
-    for x in range(1, pairs):
-        totals[x].halve()
-    triples[0].start(totals[0].settle())
+    near_end, far_end = totals[-2:]
+
+    def back_step(k):
+        back(k)
+        pl.when(k == 0)(totals[1].relay)
+        pl.when(k == 1)(far_end.start)
+        pl.when(k == 1)(lambda: triples[0].start(totals[0].settle()))
+        pl.when(k == 2)(lambda: triples[1].start(totals[1].settle()))
+        pl.when(k == 2)(merge_share.relay)
+        pl.when(k == 3)(shares[3].spread)
+
+        @pl.when(k > 0)
+        def _():
+            scatter.combine(k - 1)
+
+    loop(CHUNKS, back_step)
+    near_end.halve()
+    scatter.combine(CHUNKS - 1)
     small[...] = small_in[...]
     units = bias_in.shape[1]
     small[6:7, :units] = bias_in[0:1, :]
     for c in range(3):
         small[7:8, c * width:(c + 1) * width] = col_sum(gm[c].astype(F32))
 
+    def gtok_store(k):
+        return Move(gres.at[span(k)], gtok_hbm.at[span(k)], g_sem.at[k])
+
     def pull(k):
         gf = scatter.final(k)
         unit, inverse = norm_stats(tok[span(k), :].astype(F32))
-        gtok[span(k), :] = gres[span(k), :] + norm_pull(gf, unit, inverse, gain[...])
+        gres[span(k), :] += norm_pull(gf, unit, inverse, gain[...])
+        gtok_store(k).start()
         small[0:1, :] += col_sum(gf * unit)
         small[1:2, :] += col_sum(gf)
 
-    loop(CHUNKS, pull)
+    triples[0].relay()
+    far_end.halve()
+    near_end.relay()
+    triples[1].relay()
+
+    def pull_step(k):
+        pull(k)
+
+        @pl.when(k == 0)
+        def _():
+            merge_share.spread()
+            triples[-2].start(near_end.settle())
+            far_end.relay()
+
+        @pl.when(k == 1)
+        def _():
+            triples[0].spread()
+            triples[1].spread()
+            triples[-1].start(far_end.settle())
+            triples[-2].relay()
+
+        pl.when(k == 2)(triples[-2].spread)
+
+    loop(CHUNKS, pull_step)
     group_sum = Everyone("tensor", size, t_buf, t_sems)
     group_sum.start(small[...])
-    merge_share.spread()
-    for x in range(1, pairs):
-        triples[x].start(totals[x].settle())
+    triples[-1].relay()
     total = group_sum.finish()
     keep = lax.broadcasted_iota(jnp.int32, (8, 1), 0) < 6
     all_sum = Everyone("dp", count, d_buf, d_sems)
     all_sum.start(jnp.where(keep, total, small[...]))
-    triples[0].spread()
-    for x in range(1, pairs):
-        triples[x].spread()
+    triples[-1].spread()
     small[...] = all_sum.finish()
     for one in shares + [merge_share] + triples:
         one.finish()
     merge_total.drain()
     up_total.drain(False)
+    raw_total.drain()
     for t in totals:
         t.drain()
     loop(CHUNKS, scatter.drain)
     loop(CHUNKS, branch.drain)
-
-
-def late(size, count, gain, db, p_down0, p_down1, p_up0, u_held, g_merge, small_in, bias_in,
+    loop(CHUNKS, lambda k: gtok_store(k).wait())
+
+
+def late(size, count, gain, db, p_down0, p_down1, u_held, u_raw, g_merge, small_in, bias_in,
          mixed, att, gatt, lse, full, w, tokens, gres, resid, pout):
     rows, d = tokens.shape
     n, width = att.shape
@@ -1266,32 +1398,32 @@
         out_shape=(
             shape((rows, d), BF),
             shape((rows, d), F32),
-            shape((2, 2, line) + p_down0.shape, BF),
-            shape((2, 2, line) + p_up0.shape, BF),
+            shape((2, 2, line) + p_down1.shape, BF),
+            shape((2, 2, line) + u_raw.shape[2:], BF),
             shape(g_merge.shape, BF),
             shape((3, 2, line, piece, width), BF),
             shape((8, d), F32),
         ),
         in_specs=[VMEM_SPEC] * 9 + [ANY_SPEC] * len(loads),
-        out_specs=(VMEM_SPEC,) * 7,
+        out_specs=(VMEM_SPEC, ANY_SPEC) + (VMEM_SPEC,) * 5,
         scratch_shapes=[vm(x.shape, x.dtype) for x in loads]
         + [dma((len(loads),))]
         + [vm((2, n, 128), BF)] * 3
         + [vm((8, n), F32), vm((n, 128), F32), vm((3, n, width), BF)]
-        + [vm((pairs, 2, line, 3, piece, 128), BF)]
+        + [vm((pairs, 2, 2, line, 3, piece // 2, 128), BF)]
         + scatter
         + scatter[1:]
         + [sems(size)] * 2
-        + total_scratch(line, p_up0.shape)[1:]
+        + total_scratch(line, u_raw.shape[2:])[1:] + total_scratch(line, u_raw.shape[2:])
         + total_scratch(line, (deep, d))
-        + [vm((pairs, line, 3, piece, 128), BF), vm((pairs, line - 1, 3, piece, 128), BF)]
-        + [dma((pairs, 2, line)), dma((5 + pairs, 2, line))]
-        + [vm((size, 8, d), F32), dma((2, size)), vm((count, 8, d), F32), dma((2, count))],
+        + [vm((pairs, 2, line, 3, piece // 2, 128), BF)] * 2
+        + [dma((pairs, 2, 2, line)), dma((5 + 2 * pairs, 2, line + 1))]
+        + [vm((size, 8, d), F32), dma((2, size)), vm((count, 8, d), F32), dma((2, count)), dma((CHUNKS,))],
         compiler_params=pltpu.CompilerParams(
             collective_id=3, has_side_effects=True, vmem_limit_bytes=64 << 20
         ),
         name="late",
-    )(gain, db, p_down0, p_down1, p_up0, u_held, g_merge, small_in, bias_in, *loads)
+    )(gain, db, p_down0, p_down1, u_held, u_raw, g_merge, small_in, bias_in, *loads)
 
 
 def widen_kernel(down, up, merge, triple, small, out, tok, o_down, o_up, o_merge, o_triple, o_out, o_tok, *o_small):
@@ -1310,7 +1442,7 @@
 
 
 def widen(down, up, merge, triple, small, out, tok):
-    steps = 16
+    steps = 2
     d, units, width = small.shape[1], up.shape[1], triple.shape[2]
 
     def spec(x):
@@ -1360,17 +1492,16 @@
     width = triple_weight.shape[2]
     units = up_weight.shape[1]
     n = row_count * size
-    fused = units % (64 * count) == 0 and width % (8 * count) == 0 and 3 * width <= d and units <= d
+    fused = (
+        count == 8 and units % 512 == 0 and width % 256 == 0 and 3 * width <= d and units <= d
+    )
     count = count if fused else 0
     line = lambda v: v.reshape(1, -1)
     w = jnp.transpose(triple_weight, (1, 0, 2))
-    full, mixed = project(
-        size, tokens, line(first_gain), line(first_shift), w, triple_bias
-    )
-    mixed = mixed.reshape(n, 3 * width)
-    attended, log_total, gatt, gres, resid, pout, g_merge, small_b, bias_b, *rest = core(
-        size, count, lengths, mixed, line(merge_bias), line(second_gain), line(second_shift),
-        line(up_bias), tokens, cotangent, merge_weight, up_weight, down_weight,
+    full, mixed, attended, log_total, gatt, gres, resid, pout, g_merge, small_b, bias_b, *rest = core(
+        size, count, lengths, line(first_gain), line(first_shift), triple_bias, line(merge_bias),
+        line(second_gain), line(second_shift), line(up_bias), w, tokens, cotangent, merge_weight,
+        up_weight, down_weight,
     )
     gatt = gatt.reshape(n, width)
     if fused:

time: 317 us -> 294 us (0.927)
  Pallas kernels: 315 us -> 289 us
    pallas_call x1 -> x0, Pallas kernels: 30.1 us -> none  [project(): pl.pallas_call(functools.partial(project_kernel, size), out_shape=tuple((...]
    pallas_call x1, Pallas kernels: 141 us -> 155 us  [core(): pl.pallas_call(functools.partial(core_kernel, size, count), out_shape=tup...]
    pallas_call x1, Pallas kernels: 14.4 us -> 8.41 us  [widen(): pl.pallas_call(widen_kernel, grid=(steps,), out_shape=tuple((jax.ShapeDty...]
    pallas_call x1, Pallas kernels: 130 us -> 126 us  [late(): pl.pallas_call(functools.partial(late_kernel, size, count, bk), out_shape...]
where the time goes in v3:
time: 294 us; the launch traced here: 291 us
  Pallas kernels  289 us (98%)
    pallas_call x1, Pallas kernels, core(): pl.pallas_call(functools.partial(core_kernel, size, count), out_shape=tup...  155 us
    pallas_call x1, Pallas kernels, late(): pl.pallas_call(functools.partial(late_kernel, size, count, bk), out_shape...  126 us
    pallas_call x1, Pallas kernels, widen(): pl.pallas_call(widen_kernel, grid=(steps,), out_shape=tuple((jax.ShapeDty...  8.41 us

profile of v3, /device:TPU:24, one launch (start us, length us, event | category | flops | bytes accessed | tf_op | source)
XLA Modules:
  0.0 290.8 jit_solution(968409663105303754)
XLA Ops:
  1.3 155.1 %core.1 = (bf16[4,4,128,1024]{3,2,1,0:T(8,128)(2,1)}, bf16[2048,768]{1,0:T(8,128)(2,1)}, bf16[2048,256]{1,0:T(8,128)(2,1)}, f32[2,8,2048]{2,1,0:T(8,128)}, bf16[...) custom-call(s32[1]{0:T(128)S(6)} %copy.29.length, ...), custom_call_target="tpu_custom_call" | custom-call | tf_op jit(solution)/shard_map/core/pallas_call | solution.py:923
  156.4 125.8 %late.1 = (bf16[512,1024]{1,0:T(8,128)(2,1)}, f32[512,1024]{1,0:T(8,128)}, bf16[2,2,4,64,1024]{4,3,2,1,0:T(8,128)(2,1)}, bf16[2,2,4,64,1024]{4,3,2,1,0:T(8,128)(...) custom-call(f32[1,1024]{1,0:T(1,128)} %bitcast.31, ...), custom_call_target="tpu_custom_call" | custom-call | tf_op jit(solution)/shard_map/late/pallas_call | solution.py:1396
  282.2 8.4 %widen.1 = (f32[1024,1024]{1,0:T(8,128)}, f32[1024,1024]{1,0:T(8,128)}, f32[256,1024]{1,0:T(8,128)}, f32[3,1024,256]{2,1,0:T(8,128)}, bf16[512,1024]{1,0:T(8,128...) custom-call(bf16[1024,1024]{1,0:T(8,128)(2,1)} %bitcast.24, ...), custom_call_target="tpu_custom_call" | custom-call | tf_op jit(solution)/shard_map/widen/pallas_call | solution.py:1460

commit v4 on v3

--- a/solution.py
+++ b/solution.py
@@ -1053,11 +1053,12 @@
 def late_kernel(
     size, count, bk, gain, db, p_down0, p_down1, u_held, u_raw, g_merge, small_in, bias_in,
     mixed_hbm, att_hbm, gatt_hbm, lse_hbm, full_hbm, w_hbm, tok_hbm, gres_hbm, resid_hbm, pout_hbm,
-    out, gtok_hbm, o_down, o_up, o_merge, o_triple, small,
+    out_hbm, gtok_hbm, down_hbm, up_hbm, merge_hbm, o_triple, small,
     mixed, att, gatt, lse, full, w, tok, gres, resid, pout, load_sem,
     qm, km, dom, dsc, dq_acc, gm, g_triple, part, in_near, out_far, in_far,
     in_near2, out_far2, in_far2, sem, sem2, u_far, u_sem, v_near, v_far, v_sem,
     m_near, m_far, m_sem, t_near, t_far, t_sem, s_sem, t_buf, t_sems, d_buf, d_sems, g_sem,
+    t_buf2, t_sems2, d_buf2, d_sems2, o_down, o_up, o_merge, o_sem, out_sem,
 ):
     loads = [
         Move(src, dst, load_sem.at[i]).start()
@@ -1113,10 +1114,15 @@
     triples = [triple_share(x, h) for x in range(pairs) for h in range(2)]
     branch = Scatter(g, pout, in_near2, out_far2, in_far2, sem2)
     up_total = Total(p, None, u_held, u_far, u_sem)
-    up_total.scatter()
     raw_total = Total(p, u_raw, v_near, v_far, v_sem)
     raw_total.start()
     shares[0].start(p_down0[...])
+    group_early = Everyone("tensor", size, t_buf, t_sems)
+    all_early = Everyone("dp", count, d_buf, d_sems)
+    group_early.start(small_in[...])
+
+    def early():
+        small[...] = group_early.finish()
     for load in loads[:4]:
         load.wait()
 
@@ -1214,11 +1220,15 @@
         loads[4].wait()
         loop(CHUNKS, branch.send)
 
+    def out_store(k):
+        return Move(pout.at[g.me, k], out_hbm.at[span(k)], out_sem.at[k])
+
     def branch_end():
         loads[5].wait()
 
         def one(k):
-            out[span(k), :] = (resid[span(k), :] + branch.final(k) + db[...]).astype(BF)
+            pout[g.me, k] = (resid[span(k), :] + branch.final(k) + db[...]).astype(BF)
+            out_store(k).start()
 
         loop(CHUNKS, one)
 
@@ -1228,11 +1238,15 @@
         loads[4].wait()
         loop(CHUNKS, branch.send)
 
+    def out_store(k):
+        return Move(pout.at[g.me, k], out_hbm.at[span(k)], out_sem.at[k])
+
     def branch_end():
         loads[5].wait()
 
         def one(k):
-            out[span(k), :] = (resid[span(k), :] + branch.final(k) + db[...]).astype(BF)
+            pout[g.me, k] = (resid[span(k), :] + branch.final(k) + db[...]).astype(BF)
+            out_store(k).start()
 
         loop(CHUNKS, one)
 
@@ -1240,40 +1254,40 @@
     end = pairs - 1
     events = [
         (0, 0, 0, branch_start),
-        (0, 0, 2, merge_total.start),
+        (0, 0, 2, up_total.scatter),
+        (0, 1, 1, shares[0].relay),
         (0, 1, 1, lambda: loop(CHUNKS, branch.combine)),
-        (0, 1, 2, up_total.relay),
-        (0, 1, 2, raw_total.halve),
-        (0, 1, 3, shares[0].relay),
-        (0, 1, 3, lambda: shares[1].start(p_down1[...])),
-        (0, 2, 3, lambda: shares[2].start(up_total.settle())),
-        (0, 3, 3, shares[0].spread),
-        (0, 3, 3, raw_total.relay),
+        (0, 1, 1, early),
+        (0, 1, 2, lambda: shares[1].start(p_down1[...])),
+        (0, 1, 3, shares[0].spread),
+        (0, 1, 3, raw_total.halve),
+        (0, 2, 2, up_total.relay),
         (0, 3, 3, shares[1].relay),
-        (end, 0, 1, totals[1].start),
-        (end, 0, 1, shares[2].relay),
-        (end, 0, 1, lambda: shares[3].start(raw_total.settle())),
-        (end, 0, 2, shares[1].spread),
-        (end, 0, 3, merge_total.halve),
-        (end, 1, 1, shares[3].relay),
+        (0, 3, 3, merge_total.start),
+        (end, 0, 0, raw_total.relay),
+        (end, 0, 1, lambda: shares[2].start(up_total.settle())),
+        (end, 0, 1, shares[1].spread),
+        (end, 0, 2, totals[1].start),
+        (end, 0, 3, lambda: shares[3].start(raw_total.settle())),
+        (end, 0, 3, shares[2].relay),
         (end, 1, 1, branch_end),
-        (end, 1, 2, shares[2].spread),
-        (end, 1, 3, totals[0].halve),
-        (end, 2, 2, merge_total.relay),
+        (end, 1, 1, totals[0].halve),
+        (end, 1, 2, merge_total.halve),
+        (end, 1, 3, shares[2].spread),
+        (end, 2, 2, shares[3].relay),
         (end, 2, 3, totals[1].halve),
-        (end, 3, 3, totals[0].relay),
-        (end, 3, 3, lambda: merge_share.start(merge_total.settle())),
+        (end, 2, 3, totals[0].relay),
+        (end, 3, 3, merge_total.relay),
+        (end, 3, 3, shares[3].spread),
     ]
 
     def pair(x):
         attention(x, events)
 
-        @pl.when(x == 0)
+        @pl.when(x < end)
         def _():
-            for load in loads[6:]:
-                load.wait()
-
-        weights(x)
+            pl.when(x == 0)(lambda: [load.wait() for load in loads[6:]] and None)
+            weights(x)
 
     loop(pairs, pair)
 
@@ -1299,28 +1313,32 @@
         scatter.send(k)
 
     near_end, far_end = totals[-2:]
+    loop(2, back)
+    scatter.combine(0)
+    triples[0].start(totals[0].settle())
+    scatter.combine(1)
+    totals[1].relay()
+    weights(end)
+    merge_share.start(merge_total.settle())
 
     def back_step(k):
         back(k)
-        pl.when(k == 0)(totals[1].relay)
-        pl.when(k == 1)(far_end.start)
-        pl.when(k == 1)(lambda: triples[0].start(totals[0].settle()))
-        pl.when(k == 2)(lambda: triples[1].start(totals[1].settle()))
-        pl.when(k == 2)(merge_share.relay)
-        pl.when(k == 3)(shares[3].spread)
-
-        @pl.when(k > 0)
+
+        @pl.when(k == 2)
         def _():
-            scatter.combine(k - 1)
-
-    loop(CHUNKS, back_step)
-    near_end.halve()
-    scatter.combine(CHUNKS - 1)
-    small[...] = small_in[...]
+            far_end.start()
+            triples[1].start(totals[1].settle())
+
+    loop_range(2, CHUNKS, back_step)
+    scatter.combine(2)
+    merge_share.relay()
+    scatter.combine(3)
     units = bias_in.shape[1]
     small[6:7, :units] = bias_in[0:1, :]
     for c in range(3):
         small[7:8, c * width:(c + 1) * width] = col_sum(gm[c].astype(F32))
+    all_early.start(small[...])
+    small[0:2, :] = jnp.zeros((2, d), F32)
 
     def gtok_store(k):
         return Move(gres.at[span(k)], gtok_hbm.at[span(k)], g_sem.at[k])
@@ -1333,41 +1351,60 @@
         small[0:1, :] += col_sum(gf * unit)
         small[1:2, :] += col_sum(gf)
 
+    near_end.halve()
     triples[0].relay()
+    merge_share.spread()
     far_end.halve()
     near_end.relay()
     triples[1].relay()
+    triples[0].spread()
 
     def pull_step(k):
         pull(k)
 
-        @pl.when(k == 0)
+        @pl.when(k == 1)
         def _():
-            merge_share.spread()
             triples[-2].start(near_end.settle())
             far_end.relay()
-
-        @pl.when(k == 1)
+            triples[1].spread()
+            triples[-2].relay()
+            triples[-1].start(far_end.settle())
+
+        @pl.when(k == 2)
         def _():
-            triples[0].spread()
-            triples[1].spread()
-            triples[-1].start(far_end.settle())
-            triples[-2].relay()
-
-        pl.when(k == 2)(triples[-2].spread)
+            triples[-2].spread()
+            triples[-1].relay()
 
     loop(CHUNKS, pull_step)
-    group_sum = Everyone("tensor", size, t_buf, t_sems)
-    group_sum.start(small[...])
-    triples[-1].relay()
-    total = group_sum.finish()
-    keep = lax.broadcasted_iota(jnp.int32, (8, 1), 0) < 6
-    all_sum = Everyone("dp", count, d_buf, d_sems)
-    all_sum.start(jnp.where(keep, total, small[...]))
+    quarter = d // 4
+    group_sum = Everyone("tensor", size, t_buf2, t_sems2)
+    all_sum = Everyone("dp", count, d_buf2, d_sems2)
+    group_sum.start(
+        jnp.concatenate(
+            [small[r:r + 1, c * quarter:(c + 1) * quarter] for r in range(2) for c in range(4)],
+            axis=0,
+        )
+    )
     triples[-1].spread()
-    small[...] = all_sum.finish()
-    for one in shares + [merge_share] + triples:
+    all_sum.start(group_sum.finish())
+    stores = [
+        Move(ref, hbm, o_sem.at[i])
+        for i, (ref, hbm) in enumerate(((o_down, down_hbm), (o_up, up_hbm), (o_merge, merge_hbm)))
+    ]
+    for one, store in ((shares[:2], stores[0]), (shares[2:], stores[1]), ([merge_share], stores[2])):
+        for x in one:
+            x.finish()
+        store.start()
+    small[...] = all_early.finish()
+    total = all_sum.finish()
+    for r in range(2):
+        for c in range(4):
+            i = 4 * r + c
+            small[r:r + 1, c * quarter:(c + 1) * quarter] = total[i:i + 1, :]
+    for one in triples:
         one.finish()
+    for store in stores:
+        store.wait()
     merge_total.drain()
     up_total.drain(False)
     raw_total.drain()
@@ -1376,6 +1413,7 @@
     loop(CHUNKS, scatter.drain)
     loop(CHUNKS, branch.drain)
     loop(CHUNKS, lambda k: gtok_store(k).wait())
+    loop(CHUNKS, lambda k: out_store(k).wait())
 
 
 def late(size, count, gain, db, p_down0, p_down1, u_held, u_raw, g_merge, small_in, bias_in,
@@ -1405,7 +1443,7 @@
             shape((8, d), F32),
         ),
         in_specs=[VMEM_SPEC] * 9 + [ANY_SPEC] * len(loads),
-        out_specs=(VMEM_SPEC, ANY_SPEC) + (VMEM_SPEC,) * 5,
+        out_specs=(ANY_SPEC,) * 5 + (VMEM_SPEC,) * 2,
         scratch_shapes=[vm(x.shape, x.dtype) for x in loads]
         + [dma((len(loads),))]
         + [vm((2, n, 128), BF)] * 3
@@ -1418,7 +1456,10 @@
         + total_scratch(line, (deep, d))
         + [vm((pairs, 2, line, 3, piece // 2, 128), BF)] * 2
         + [dma((pairs, 2, 2, line)), dma((5 + 2 * pairs, 2, line + 1))]
-        + [vm((size, 8, d), F32), dma((2, size)), vm((count, 8, d), F32), dma((2, count)), dma((CHUNKS,))],
+        + [vm((size, 8, d), F32), dma((2, size)), vm((count, 8, d), F32), dma((2, count)), dma((CHUNKS,))]
+        + [vm((size, 8, d // 4), F32), dma((2, size)), vm((count, 8, d // 4), F32), dma((2, count))]
+        + [vm((2, 2, line) + p_down1.shape, BF), vm((2, 2, line) + u_raw.shape[2:], BF)]
+        + [vm(g_merge.shape, BF), dma((3,)), dma((CHUNKS,))],
         compiler_params=pltpu.CompilerParams(
             collective_id=3, has_side_effects=True, vmem_limit_bytes=64 << 20
         ),

time: 294 us -> 291 us (0.990)
  Pallas kernels: 289 us -> 286 us
    pallas_call x1, Pallas kernels: 126 us -> 122 us  [late(): pl.pallas_call(functools.partial(late_kernel, size, count, bk), out_shape...]
where the time goes in v4:
time: 291 us; the launch traced here: 287 us
  Pallas kernels  286 us (98%)
    pallas_call x1, Pallas kernels, core(): pl.pallas_call(functools.partial(core_kernel, size, count), out_shape=tup...  155 us
    pallas_call x1, Pallas kernels, late(): pl.pallas_call(functools.partial(late_kernel, size, count, bk), out_shape...  122 us
    pallas_call x1, Pallas kernels, widen(): pl.pallas_call(widen_kernel, grid=(steps,), out_shape=tuple((jax.ShapeDty...  8.41 us

profile of v4, /device:TPU:24, one launch (start us, length us, event | category | flops | bytes accessed | tf_op | source)
XLA Modules:
  0.0 287.1 jit_solution(1818384212306218018)
XLA Ops:
  1.3 155.1 %core.1 = (bf16[4,4,128,1024]{3,2,1,0:T(8,128)(2,1)}, bf16[2048,768]{1,0:T(8,128)(2,1)}, bf16[2048,256]{1,0:T(8,128)(2,1)}, f32[2,8,2048]{2,1,0:T(8,128)}, bf16[...) custom-call(s32[1]{0:T(128)S(6)} %copy.29.length, ...), custom_call_target="tpu_custom_call" | custom-call | tf_op jit(solution)/shard_map/core/pallas_call | solution.py:923
  156.4 122.2 %late.1 = (bf16[512,1024]{1,0:T(8,128)(2,1)}, f32[512,1024]{1,0:T(8,128)}, bf16[2,2,4,64,1024]{4,3,2,1,0:T(8,128)(2,1)}, bf16[2,2,4,64,1024]{4,3,2,1,0:T(8,128)(...) custom-call(f32[1,1024]{1,0:T(1,128)} %bitcast.31, ...), custom_call_target="tpu_custom_call" | custom-call | tf_op jit(solution)/shard_map/late/pallas_call | solution.py:1434
  278.6 8.4 %widen.1 = (f32[1024,1024]{1,0:T(8,128)}, f32[1024,1024]{1,0:T(8,128)}, f32[256,1024]{1,0:T(8,128)}, f32[3,1024,256]{2,1,0:T(8,128)}, bf16[512,1024]{1,0:T(8,128...) custom-call(bf16[1024,1024]{1,0:T(8,128)(2,1)} %bitcast.24, ...), custom_call_target="tpu_custom_call" | custom-call | tf_op jit(solution)/shard_map/widen/pallas_call | solution.py:1501

commit v5 on v4

--- a/solution.py
+++ b/solution.py
@@ -1331,8 +1331,8 @@
 
     loop_range(2, CHUNKS, back_step)
     scatter.combine(2)
+    scatter.combine(3)
     merge_share.relay()
-    scatter.combine(3)
     units = bias_in.shape[1]
     small[6:7, :units] = bias_in[0:1, :]
     for c in range(3):
@@ -1341,12 +1341,13 @@
     small[0:2, :] = jnp.zeros((2, d), F32)
 
     def gtok_store(k):
-        return Move(gres.at[span(k)], gtok_hbm.at[span(k)], g_sem.at[k])
+        return Move(tok.at[span(k)], gtok_hbm.at[span(k)], g_sem.at[k])
 
     def pull(k):
         gf = scatter.final(k)
         unit, inverse = norm_stats(tok[span(k), :].astype(F32))
-        gres[span(k), :] += norm_pull(gf, unit, inverse, gain[...])
+        total = gres[span(k), :] + norm_pull(gf, unit, inverse, gain[...])
+        tok[span(k), :] = total.astype(BF)
         gtok_store(k).start()
         small[0:1, :] += col_sum(gf * unit)
         small[1:2, :] += col_sum(gf)
@@ -1435,7 +1436,7 @@
         functools.partial(late_kernel, size, count, bk),
         out_shape=(
             shape((rows, d), BF),
-            shape((rows, d), F32),
+            shape((rows, d), BF),
             shape((2, 2, line) + p_down1.shape, BF),
             shape((2, 2, line) + u_raw.shape[2:], BF),
             shape(g_merge.shape, BF),
@@ -1471,7 +1472,7 @@
     for src, dst in ((down, o_down), (up, o_up), (merge, o_merge), (triple, o_triple)):
         dst[...] = src[...].astype(F32)
     o_out[...] = out[...]
-    o_tok[...] = tok[...]
+    o_tok[...] = tok[...].astype(F32)
 
     @pl.when(pl.program_id(0) == 0)
     def _():
@@ -1496,7 +1497,7 @@
 
     arrays = (down, up, merge, triple)
     lines = [(1, d)] * 6 + [(1, units), (3, width)]
-    outs = [(x.shape, F32, spec(x)) for x in arrays] + [(x.shape, x.dtype, spec(x)) for x in (out, tok)]
+    outs = [(x.shape, F32, spec(x)) for x in arrays] + [(out.shape, out.dtype, spec(out)), (tok.shape, F32, spec(tok))]
     outs += [(x, F32, whole(x)) for x in lines]
     return pl.pallas_call(
         widen_kernel,

time: 291 us -> 291 us (level)
  no operation moved by 1% of the time
where the time goes in v5:
time: 291 us; the launch traced here: 287 us
  Pallas kernels  286 us (98%)
    pallas_call x1, Pallas kernels, core(): pl.pallas_call(functools.partial(core_kernel, size, count), out_shape=tup...  155 us
    pallas_call x1, Pallas kernels, late(): pl.pallas_call(functools.partial(late_kernel, size, count, bk), out_shape...  122 us
    pallas_call x1, Pallas kernels, widen(): pl.pallas_call(widen_kernel, grid=(steps,), out_shape=tuple((jax.ShapeDty...  8.22 us

profile of v5, /device:TPU:24, one launch (start us, length us, event | category | flops | bytes accessed | tf_op | source)
XLA Modules:
  0.0 287.0 jit_solution(17073549830338035616)
XLA Ops:
  1.3 155.1 %core.1 = (bf16[4,4,128,1024]{3,2,1,0:T(8,128)(2,1)}, bf16[2048,768]{1,0:T(8,128)(2,1)}, bf16[2048,256]{1,0:T(8,128)(2,1)}, f32[2,8,2048]{2,1,0:T(8,128)}, bf16[...) custom-call(s32[1]{0:T(128)S(6)} %copy.29.length, ...), custom_call_target="tpu_custom_call" | custom-call | tf_op jit(solution)/shard_map/core/pallas_call | solution.py:923
  156.4 122.1 %late.1 = (bf16[512,1024]{1,0:T(8,128)(2,1)}, bf16[512,1024]{1,0:T(8,128)(2,1)}, bf16[2,2,4,64,1024]{4,3,2,1,0:T(8,128)(2,1)}, bf16[2,2,4,64,1024]{4,3,2,1,0:T(8...) custom-call(f32[1,1024]{1,0:T(1,128)} %bitcast.31, ...), custom_call_target="tpu_custom_call" | custom-call | tf_op jit(solution)/shard_map/late/pallas_call | solution.py:1435
  278.6 8.2 %widen.1 = (f32[1024,1024]{1,0:T(8,128)}, f32[1024,1024]{1,0:T(8,128)}, f32[256,1024]{1,0:T(8,128)}, f32[3,1024,256]{2,1,0:T(8,128)}, bf16[512,1024]{1,0:T(8,128...) custom-call(bf16[1024,1024]{1,0:T(8,128)(2,1)} %bitcast.24, ...), custom_call_target="tpu_custom_call" | custom-call | tf_op jit(solution)/shard_map/widen/pallas_call | solution.py:1502
